TPU v7x, 32 devices: a whole 2x2x4 slice. The times are simulated.
32 devices in a mesh: tower: 2 (over core), dp: 16 (over z, y, x).
Axes of the slice: x: 2, y: 2, z: 4, core: 2. Of those that a mesh axis runs over, the one named last changes fastest.
Arguments:
- tokens: bfloat16 [2, 8192, 768], P('tower', 'dp'), may hold values from -6 to 6
- doc_ids: int32 [2, 8192], P('tower', 'dp'), may hold values from 0 to 11, as said below
- pad_mask: int32 [2, 8192], P('tower', 'dp'), may hold values 0 or 1
- targets: int32 [12], replicated, may hold values from 0 to 11, each once
- w_qkv: bfloat16 [768, 2304], replicated, may hold values from -0.21875 to 0.21875
- w_out: bfloat16 [768, 768], replicated, may hold values from -0.875 to 0.875
- ln1_gain: float32 [768], replicated, may hold values from 0.5 to 1.5
- ln1_bias: float32 [768], replicated, may hold values from -0.6 to 0.6
- w_gate: bfloat16 [768, 3072], replicated, may hold values from -0.21875 to 0.21875
- w_up: bfloat16 [768, 3072], replicated, may hold values from -0.21875 to 0.21875
- w_down: bfloat16 [3072, 768], replicated, may hold values from -0.109375 to 0.109375
- ln2_gain: float32 [768], replicated, may hold values from 0.5 to 1.5
- ln2_bias: float32 [768], replicated, may hold values from -0.6 to 0.6
Outputs:
- scores: float32 [12, 12], replicated
- loss: float32 [], replicated
- token_grad: float32 [2, 8192, 768], P('tower', 'dp')
- w_qkv_grad: float32 [768, 2304], P('dp')
- w_out_grad: float32 [768, 768], P('dp')
- ln1_gain_grad: float32 [768], P('dp')
- ln1_bias_grad: float32 [768], P('dp')
- w_gate_grad: float32 [768, 3072], P('dp')
- w_up_grad: float32 [768, 3072], P('dp')
- w_down_grad: float32 [3072, 768], P('dp')
- ln2_gain_grad: float32 [768], P('dp')
- ln2_bias_grad: float32 [768], P('dp')
Inputs may be any that keep to these rules, and one draw needn't show every extreme that they name: `doc_ids`: within each tower the ids never fall; the k-th aligned group of 2048 slots holds exactly the documents k * 3 to k * 3 + 2, one of them exactly 1024 slots long. `targets`: each document of the second tower is the target of exactly one query.
All inputs are finite; a program needn't handle non-finite values. No bound on the sum of `pad_mask` on one device may be relied on, other than what follows from the above.
Results may differ from a plain program's by a relative error of at most 0.015.
Values may be sent and summed in bfloat16 or wider, within the bound.
A program may use at most 192 MiB of HBM per device.

v0:
```python
import jax
import jax.numpy as jnp
from jax import lax
from jax.sharding import PartitionSpec as P

HEADS = 12
HEAD_DIM = 64
SPAN = 4
DOCS_GRP = 3


precise = lax.Precision.HIGHEST
norm_eps = 1e-05


def swapped(value, axis, bit):
    return lax.ppermute(value, axis, [(i, i ^ 1 << bit) for i in range(lax.axis_size(axis))])


def for_sending(value):
    return jax.tree.map(lambda a: a.astype(jnp.bfloat16) if a.dtype == jnp.float32 else a, value)


def angles_for(positions, half):
    freqs = 1000.0 ** (-jnp.arange(half, dtype=jnp.float32) / half)
    theta = positions.astype(jnp.float32)[:, None] * freqs[None, :]
    return (jnp.cos(theta)[:, None, :], jnp.sin(theta)[:, None, :])


def rotate(values, cosine, sine):
    half = values.shape[-1] // 2
    upper = values[..., :half]
    lower = values[..., half:]
    return jnp.concatenate([upper * cosine - lower * sine, lower * cosine + upper * sine], -1)


def unrotate(values, cosine, sine):
    half = values.shape[-1] // 2
    upper = values[..., :half]
    lower = values[..., half:]
    return jnp.concatenate([upper * cosine + lower * sine, lower * cosine - upper * sine], -1)


def norm_rows(values, gain, bias):
    centred = values - jnp.mean(values, -1, keepdims=True)
    spread = jnp.mean(centred * centred, -1, keepdims=True)
    scale = lax.rsqrt(spread + norm_eps)
    normed = centred * scale
    return (normed * gain + bias, normed, scale)


def norm_back(grad, normed, scale, gain):
    shaped = grad * gain
    inner = (
        shaped
        - jnp.mean(shaped, -1, keepdims=True)
        - normed * jnp.mean(shaped * normed, -1, keepdims=True)
    )
    return (inner * scale, jnp.sum(grad * normed, 0), jnp.sum(grad, 0))


def contract_last(left, right):
    return lax.dot_general(
        left, right, (((1,), (1,)), ((), ())), preferred_element_type=jnp.float32
    )


def contract_first(left, right):
    return lax.dot_general(
        left, right, (((0,), (0,)), ((), ())), preferred_element_type=jnp.float32
    )


def local(
    tokens,
    doc_ids,
    pad_mask,
    targets,
    w_qkv,
    w_out,
    ln1_gain,
    ln1_bias,
    w_gate,
    w_up,
    w_down,
    ln2_gain,
    ln2_bias,
):
    width = w_out.shape[0]
    rows = tokens[0]
    count = rows.shape[0]
    tower = lax.axis_index("tower")
    place = lax.axis_index("dp")
    member_of = doc_ids[0] % DOCS_GRP
    live_row = pad_mask[0] == 1
    positions = place % SPAN * count + jnp.arange(count, dtype=jnp.int32)
    cosine, sine = angles_for(positions, HEAD_DIM // 2)
    mixed = jnp.dot(rows, w_qkv, preferred_element_type=jnp.float32)
    query = rotate(mixed[:, :width].reshape(count, HEADS, HEAD_DIM), cosine, sine).astype(
        jnp.bfloat16
    )
    keys = rotate(mixed[:, width : 2 * width].reshape(count, HEADS, HEAD_DIM), cosine, sine).astype(
        jnp.bfloat16
    )
    values = mixed[:, 2 * width :].astype(jnp.bfloat16)
    key_tags = jnp.where(live_row, member_of, -1).astype(jnp.bfloat16)
    group_keys = keys.reshape(count, width)
    group_values = values
    group_tags = key_tags
    levels = SPAN.bit_length() - 1
    for level in range(levels):
        other = swapped((group_keys, group_values, group_tags), "dp", level)
        group_keys = jnp.concatenate([group_keys, other[0]], 0)
        group_values = jnp.concatenate([group_values, other[1]], 0)
        group_tags = jnp.concatenate([group_tags, other[2]], 0)
    group_len = group_keys.shape[0]
    key_tag = group_tags.astype(jnp.float32)
    keys_heads = group_keys.reshape(group_len, HEADS, HEAD_DIM).transpose(1, 0, 2)
    values_heads = group_values.reshape(group_len, HEADS, HEAD_DIM).transpose(1, 0, 2)
    block = min(512, count)
    nblocks = count // block
    query_heads = query.transpose(1, 0, 2).reshape(HEADS, nblocks, block, HEAD_DIM)
    query_tag = member_of.astype(jnp.float32).reshape(nblocks, block)

    def head_scores(query_block, tag_block, head_keys):
        scores = contract_last(query_block, head_keys) * 0.125
        return jnp.where(tag_block[:, None] == key_tag[None, :], scores, -1e30)

    def attend_head(parts):
        head_query, head_keys, head_values = parts

        def attend_block(inputs):
            query_block, tag_block = inputs
            masked = head_scores(query_block, tag_block, head_keys)
            top = jnp.max(masked, -1, keepdims=True)
            expo = jnp.exp(masked - top)
            total = jnp.sum(expo, -1, keepdims=True)
            probs = (expo / total).astype(jnp.bfloat16)
            result = jnp.dot(probs, head_values, preferred_element_type=jnp.float32)
            return (result, (top + jnp.log(total))[:, 0])

        return lax.map(attend_block, (head_query, query_tag))

    outputs, log_totals = lax.map(attend_head, (query_heads, keys_heads, values_heads))
    attended = outputs.transpose(1, 2, 0, 3).reshape(count, width).astype(jnp.bfloat16)
    branch = jnp.dot(attended, w_out, preferred_element_type=jnp.float32)
    first, normed_one, scale_one = norm_rows(rows.astype(jnp.float32) + branch, ln1_gain, ln1_bias)
    inner = first.astype(jnp.bfloat16)
    gate = jnp.dot(inner, w_gate, preferred_element_type=jnp.float32)
    upper = jnp.dot(inner, w_up, preferred_element_type=jnp.float32)
    sigmoid = jax.nn.sigmoid(gate)
    activated = jax.nn.silu(gate)
    hidden = (activated * upper).astype(jnp.bfloat16)
    second, normed_two, scale_two = norm_rows(
        first + jnp.dot(hidden, w_down, preferred_element_type=jnp.float32), ln2_gain, ln2_bias
    )
    member = ((member_of[:, None] == jnp.arange(DOCS_GRP)[None, :]) & live_row[:, None]).astype(
        jnp.float32
    )
    sums = jnp.dot(member.T, second, precision=precise)
    group = place // SPAN
    part_sums = lax.all_gather(sums, "dp", axis=0, tiled=True)
    own_pooled = jnp.sum(part_sums.reshape(-1, SPAN, DOCS_GRP, width), 1).reshape(-1, width)
    own_embed = own_pooled * lax.rsqrt(jnp.sum(own_pooled * own_pooled, -1, keepdims=True) + 1e-06)
    embed = lax.all_gather(
        own_embed[None].astype(jnp.bfloat16), "tower", axis=0, tiled=True
    ).astype(jnp.float32)
    scores = jnp.dot(embed[0], embed[1].T, precision=precise) * 50.0
    docs = scores.shape[0]
    top = jnp.max(scores, -1, keepdims=True)
    log_sums = top[:, 0] + jnp.log(jnp.sum(jnp.exp(scores - top), -1))
    onehot = (jnp.arange(docs)[None, :] == targets[:, None]).astype(jnp.float32)
    chosen = jnp.sum(onehot * scores, -1)
    loss = jnp.mean(log_sums - chosen)
    grad_scores = (jnp.exp(scores - log_sums[:, None]) - onehot) / docs
    grad_query_embed = jnp.dot(grad_scores, embed[1], precision=precise) * 50.0
    grad_doc_embed = jnp.dot(grad_scores.T, embed[0], precision=precise) * 50.0
    own_grad = jnp.where(tower == 0, grad_query_embed, grad_doc_embed)
    start = group * DOCS_GRP
    grad_mine = lax.dynamic_slice_in_dim(own_grad, start, DOCS_GRP, 0)
    pooled_mine = lax.dynamic_slice_in_dim(own_pooled, start, DOCS_GRP, 0)
    inverse = lax.rsqrt(jnp.sum(pooled_mine * pooled_mine, -1, keepdims=True) + 1e-06)
    grad_pool = inverse * grad_mine - inverse**3 * pooled_mine * jnp.sum(
        pooled_mine * grad_mine, -1, keepdims=True
    )
    grad_second = jnp.dot(member, grad_pool, precision=precise)
    grad_h2, gain_two_grad, bias_two_grad = norm_back(grad_second, normed_two, scale_two, ln2_gain)
    grad_mlp = grad_h2.astype(jnp.bfloat16)
    w_down_grad = contract_first(hidden, grad_mlp)
    grad_hidden = contract_last(grad_mlp, w_down)
    grad_gate = (grad_hidden * upper * sigmoid * (1.0 + gate * (1.0 - sigmoid))).astype(
        jnp.bfloat16
    )
    grad_up = (grad_hidden * activated).astype(jnp.bfloat16)
    w_gate_grad = contract_first(inner, grad_gate)
    w_up_grad = contract_first(inner, grad_up)
    grad_first = grad_h2 + contract_last(grad_gate, w_gate) + contract_last(grad_up, w_up)
    grad_h1, gain_one_grad, bias_one_grad = norm_back(grad_first, normed_one, scale_one, ln1_gain)
    grad_branch = grad_h1.astype(jnp.bfloat16)
    w_out_grad = contract_first(attended, grad_branch)
    grad_attended = contract_last(grad_branch, w_out).astype(jnp.bfloat16)
    grad_heads = (
        grad_attended.reshape(count, HEADS, HEAD_DIM)
        .transpose(1, 0, 2)
        .reshape(HEADS, nblocks, block, HEAD_DIM)
    )

    def back_head(parts):
        head_query, head_keys, head_values, head_grad, head_totals = parts

        def back_block(carry, inputs):
            key_acc, value_acc = carry
            query_block, tag_block, grad_block, total_block = inputs
            masked = head_scores(query_block, tag_block, head_keys)
            probs = jnp.exp(masked - total_block[:, None])
            grad_probs = contract_last(grad_block, head_values)
            inner_sum = jnp.sum(probs * grad_probs, -1, keepdims=True)
            grad_logits = (probs * (grad_probs - inner_sum)).astype(jnp.bfloat16)
            grad_query_block = (
                jnp.dot(grad_logits, head_keys, preferred_element_type=jnp.float32) * 0.125
            )
            key_acc = key_acc + contract_first(grad_logits, query_block) * 0.125
            value_acc = value_acc + contract_first(probs.astype(jnp.bfloat16), grad_block)
            return ((key_acc, value_acc), grad_query_block)

        empty = jnp.zeros((group_len, HEAD_DIM), jnp.float32)
        (key_grad, value_grad), query_grad = lax.scan(
            back_block, (empty, empty), (head_query, query_tag, head_grad, head_totals)
        )
        return (key_grad, value_grad, query_grad)

    key_grads, value_grads, query_grads = lax.map(
        back_head, (query_heads, keys_heads, values_heads, grad_heads, log_totals)
    )
    key_full = key_grads.transpose(1, 0, 2).reshape(group_len, width)
    value_full = value_grads.transpose(1, 0, 2).reshape(group_len, width)
    for level in reversed(range(levels)):
        half = key_full.shape[0] // 2
        returned = swapped(
            (for_sending(key_full[half:]), for_sending(value_full[half:])), "dp", level
        )
        key_full = key_full[:half] + returned[0]
        value_full = value_full[:half] + returned[1]
    grad_query_rows = unrotate(
        query_grads.transpose(1, 2, 0, 3).reshape(count, HEADS, HEAD_DIM), cosine, sine
    )
    grad_key_rows = unrotate(key_full.reshape(count, HEADS, HEAD_DIM), cosine, sine)
    grad_mixed = jnp.concatenate(
        [grad_query_rows.reshape(count, width), grad_key_rows.reshape(count, width), value_full], 1
    ).astype(jnp.bfloat16)
    w_qkv_grad = contract_first(rows, grad_mixed)
    token_grad = grad_h1 + contract_last(grad_mixed, w_qkv)
    gain_grads = jnp.stack([gain_one_grad, bias_one_grad, gain_two_grad, bias_two_grad], 1)
    terms = (w_qkv_grad, w_out_grad, w_gate_grad, w_up_grad, w_down_grad, gain_grads)
    pieces = (
        lax.psum_scatter(terms[0], "dp", scatter_dimension=0, tiled=True),
        lax.psum_scatter(terms[1], "dp", scatter_dimension=0, tiled=True),
        lax.psum_scatter(terms[2], "dp", scatter_dimension=0, tiled=True),
        lax.psum_scatter(terms[3], "dp", scatter_dimension=0, tiled=True),
        lax.psum_scatter(terms[4], "dp", scatter_dimension=0, tiled=True),
        lax.psum_scatter(terms[5], "dp", scatter_dimension=0, tiled=True),
    )
    totals = (
        lax.psum(pieces[0].astype(jnp.bfloat16), "tower").astype(jnp.float32),
        lax.psum(pieces[1].astype(jnp.bfloat16), "tower").astype(jnp.float32),
        lax.psum(pieces[2].astype(jnp.bfloat16), "tower").astype(jnp.float32),
        lax.psum(pieces[3].astype(jnp.bfloat16), "tower").astype(jnp.float32),
        lax.psum(pieces[4].astype(jnp.bfloat16), "tower").astype(jnp.float32),
        lax.psum(pieces[5].astype(jnp.bfloat16), "tower").astype(jnp.float32),
    )
    gains_out = totals[5]
    return (
        scores,
        loss,
        token_grad[None],
        totals[0],
        totals[1],
        gains_out[:, 0],
        gains_out[:, 1],
        totals[2],
        totals[3],
        totals[4],
        gains_out[:, 2],
        gains_out[:, 3],
    )


def solution(mesh):
    placed = (
        P("tower", "dp", None),
        P("tower", "dp"),
        P("tower", "dp"),
        P(),
        P(),
        P(),
        P(),
        P(),
        P(),
        P(),
        P(),
        P(),
        P(),
    )
    return jax.shard_map(
        local,
        mesh=mesh,
        in_specs=placed,
        out_specs=(
            P(),
            P(),
            P("tower", "dp", None),
            P("dp", None),
            P("dp", None),
            P("dp"),
            P("dp"),
            P("dp", None),
            P("dp", None),
            P("dp", None),
            P("dp"),
            P("dp"),
        ),
        check_vma=False,
    )
```

profile of v0, /device:TPU:25, one launch (start us, length us, event | category | flops | bytes accessed | tf_op | source)
XLA Modules:
  0.0 1404.7 jit_solution(15379904082017169689)
XLA Ops:
  26.0 8.2 collective-permute-done.4
  38.1 13.0 collective-permute-done.2
  65.1 39.0 %collective-permute-done.1 = bf16[1024]{0:T(1024)(128)(2,1)} collective-permute-done((bf16[1024]{0:T(1024)(128)(2,1)S(1)}, bf16[1024]{0:T(1024)(128)(2,1)}, u32[]{:S(2)}, u32[]{:S(2)}) %collective-permute-start.1) | collective-permute-done | bytes 2080 | tf_op jit(solution)/shard_map/ppermute | solution.py:17
  113.2 6.6 copy.55
  123.7 6.6 copy.54
  130.3 71.9 %while.28 = (s32[]{:T(128)}, bf16[12,1,512,64]{2,3,1,0:T(8,128)(2,1)}, f32[12,1,512]{2,1,0:T(1,128)}, f32[1,512]{1,0:T(1,128)S(1)}, f32[2048]{0:T(1024)S(1)}, /*...) while((s32[]{:T(128)}, ...), condition=%wide.region_3.4_spmd.clone, body=%wide.region_0.3_spmd.sunk.clone | while | flops 277872128 | bytes 13926497 | solution.py:144
  220.7 27.2 %all-gather = f32[16,3,768]{2,1,0:T(4,128)S(1)} all-gather(f32[1,3,768]{2,1,0:T(4,128)S(1)} %fusion.44), channel_id=1, replica_groups=mesh['tower'=2,'dp'=16] {'dp'}, dimensions={0}, use_global_device_ids=true | all-gather | bytes 156672 | tf_op jit(solution)/shard_map/all_gather | solution.py:162
  252.7 11.9 all_gather.7
  274.0 9.4 multiply_convert_fusion.1
  297.8 149.7 %while.29 = (s32[]{:T(128)}, f32[12,2048,64]{1,2,0:T(8,128)}, f32[12,2048,64]{1,2,0:T(8,128)}, f32[12,1,512,64]{2,3,1,0:T(8,128)}, f32[1,512]{1,0:T(1,128)}, /*i...) while((s32[]{:T(128)}, f32[12,2048,64]{1,2,0:T(8,128)}, ...), condition=%wide.region_22.23_spmd.clone, body=%wide.region_20.22_spmd.sunk.clone | while | flops 681737728 | bytes 34636948 | solution.py:232
  455.6 31.5 %collective-permute-done.6 = bf16[1024,768]{0,1:T(8,128)(2,1)S(1)} collective-permute-done((bf16[1024,768]{0,1:T(8,128)(2,1)S(1)}, bf16[1024,768]{0,1:T(8,128)(2,1)S(1)}, u32[]{:S(2)}, u32[]{:S(2)}) %collective-permute-start.6) | collective-permute-done | bytes 1572896 | tf_op jit(solution)/shard_map/ppermute | solution.py:17
  490.4 30.4 %collective-permute-done.8 = bf16[1024,768]{0,1:T(8,128)(2,1)S(1)} collective-permute-done((bf16[1024,768]{0,1:T(8,128)(2,1)S(1)}, bf16[1024,768]{0,1:T(8,128)(2,1)S(1)}, u32[]{:S(2)}, u32[]{:S(2)}) %collective-permute-start.8) | collective-permute-done | bytes 1572896 | tf_op jit(solution)/shard_map/ppermute | solution.py:17
  524.7 16.0 %collective-permute-done.9 = bf16[512,768]{0,1:T(8,128)(2,1)S(1)} collective-permute-done((bf16[512,768]{0,1:T(8,128)(2,1)S(1)}, bf16[512,768]{0,1:T(8,128)(2,1)S(1)}, u32[]{:S(2)}, u32[]{:S(2)}) %collective-permute-start.9) | collective-permute-done | bytes 786464 | tf_op jit(solution)/shard_map/ppermute | solution.py:17
  546.9 8.0 copy.64
  555.1 8.7 fusion.57
  563.9 8.4 fusion.101
  572.4 8.5 fusion.100
  586.9 119.3 %reduce-scatter.19.cloned.1.call-done = f32[48,2304]{1,0:T(8,128)} async-done(((f32[768,2304]{1,0:T(8,128)}), f32[48,2304]{1,0:T(8,128)}) %reduce-scatter.19.cloned.1.call-update) | async-done | bytes 442384
  708.3 174.7 %reduce-scatter.17.cloned.1.call-done = f32[192,768]{1,0:T(8,128)} async-done(((f32[3072,768]{1,0:T(8,128)}), f32[192,768]{1,0:T(8,128)}) %reduce-scatter.17.cloned.1.call-update) | async-done | bytes 589840 | tf_op jit(solution)/shard_map/reduce_scatter | solution.py:260
  884.8 173.8 %reduce-scatter.15.cloned.1.call-done = f32[48,3072]{1,0:T(8,128)} async-done(((f32[768,3072]{1,0:T(8,128)}), f32[48,3072]{1,0:T(8,128)}) %reduce-scatter.15.cloned.1.call-update) | async-done | bytes 589840 | tf_op jit(solution)/shard_map/reduce_scatter | solution.py:259
  1060.4 174.4 %reduce-scatter.13.cloned.1.call-done = f32[48,3072]{1,0:T(8,128)} async-done(((f32[768,3072]{1,0:T(8,128)}), f32[48,3072]{1,0:T(8,128)}) %reduce-scatter.13.cloned.1.call-update) | async-done | bytes 589840 | tf_op jit(solution)/shard_map/reduce_scatter | solution.py:258
  1238.0 122.2 %reduce-scatter.21.cloned.1.call-done = f32[48,4]{1,0:T(8,128)} async-done(((f32[768,4]{1,0:T(8,128)}), f32[48,4]{1,0:T(8,128)}) %reduce-scatter.21.cloned.1.call-update) | async-done | bytes 784
  1366.0 5.3 add_bitcast_fusion
  1371.3 16.2 %all-reduce.3.cloned.1.call-done = (bf16[48,2304]{0,1:T(8,128)(2,1)}, bf16[48,768]{1,0:T(8,128)(2,1)}, bf16[48,3072]{1,0:T(8,128)(2,1)}, bf16[48,3072]{1,0:T(8,128)(2,1)}, bf16[192,768]{1,0:T(8,128)(2,1)}) async-done(((bf16[48,2304]{0,1:T(8,128)(2,1)}, bf16[48,768]{1,0:T(8,128)(2,1)}, bf16[48,3072]{1,0:T(8,128)(2,1)}, bf16[48,3072]{1,0:T(8,128)(2,1)}, bf16[192,768]{1,0:T(8,128)(2,1)}), ...) | async-done | bytes 1179664 | tf_op jit(solution)/shard_map/psum | solution.py:264
  (422 shorter events, 367.6 us)
Async XLA Ops:
  7.2 578.2 %reduce-scatter.11.cloned.1.call-start = ((), (), s32[]{:S(2)}) async-start(), calls=%async_computation.6 | async-start | bytes 2506752 | tf_op jit(solution)/shard_map/reduce_scatter | solution.py:257
  15.5 18.7 %collective-permute-start.4 = (bf16[512,768]{1,0:T(8,128)(2,1)}, bf16[512,768]{1,0:T(8,128)(2,1)}, u32[]{:S(2)}, u32[]{:S(2)}) collective-permute-start(bf16[512,768]{1,0:T(8,128)(2,1)} %slice.177), channel_id=1, source_target_pairs={{0,1},{1,0},{2,3},{3,2},{4,5},{5,4},{6,7},{7,6},{8,9},{9,8},{10,11... | collective-permute-start | bytes 2359304 | tf_op jit(solution)/shard_map/ppermute | solution.py:17
  25.7 26.8 %copy-start.4 = (bf16[512,12,64]{0,2,1:T(8,128)(2,1)}, bf16[512,12,64]{0,2,1:T(8,128)(2,1)S(1)}, u32[]{:S(2)}) copy-start(bf16[512,12,64]{0,2,1:T(8,128)(2,1)S(1)} %maximum_convert_fusion) | copy-start | bytes 2359300
  25.7 28.0 %copy-start.44 = (s32[1,512]{1,0:T(1,128)S(1)}, s32[1,512]{1,0:T(1,128)}, u32[]{:S(2)}) copy-start(s32[1,512]{1,0:T(1,128)} %param.19) | copy-start | bytes 6148
  25.7 28.1 %copy-start.43 = (s32[1,512]{1,0:T(1,128)S(1)}, s32[1,512]{1,0:T(1,128)}, u32[]{:S(2)}) copy-start(s32[1,512]{1,0:T(1,128)} %param.18) | copy-start | bytes 6148
  25.7 25.3 %collective-permute-start.2 = (bf16[512,768]{0,1:T(8,128)(2,1)S(1)}, bf16[512,768]{0,1:T(8,128)(2,1)S(1)}, u32[]{:S(2)}, u32[]{:S(2)}) collective-permute-start(bf16[512,768]{0,1:T(8,128)(2,1)S(1)} %bitcast.217), channel_id=1, source_target_pairs={{0,1},{1,0},{2,3},{3,2},{4,5},{5,4},{6,7},{7,6},{8,9},{9,8},{10,11... | collective-permute-start | bytes 2359304 | tf_op jit(solution)/shard_map/ppermute | solution.py:17
  36.9 68.0 %collective-permute-start.5 = (bf16[1024,768]{1,0:T(8,128)(2,1)}, bf16[1024,768]{1,0:T(8,128)(2,1)}, u32[]{:S(2)}, u32[]{:S(2)}) collective-permute-start(bf16[1024,768]{1,0:T(8,128)(2,1)} %pad_maximum_fusion.3), channel_id=1, source_target_pairs={{0,2},{1,3},{2,0},{3,1},{4,6},{5,7},{6,4},{7,5},{8,10},{9,11},{10,... | collective-permute-start | bytes 4718600 | tf_op jit(solution)/shard_map/ppermute | solution.py:17
  52.5 67.3 %collective-permute-start.3 = (bf16[1024,768]{0,1:T(8,128)(2,1)}, bf16[1024,768]{0,1:T(8,128)(2,1)}, u32[]{:S(2)}, u32[]{:S(2)}) collective-permute-start(bf16[1024,768]{0,1:T(8,128)(2,1)} %pad_maximum_fusion.2), channel_id=1, source_target_pairs={{0,2},{1,3},{2,0},{3,1},{4,6},{5,7},{6,4},{7,5},{8,10},{9,11},{10,... | collective-permute-start | bytes 4718600 | tf_op jit(solution)/shard_map/ppermute | solution.py:17
  54.4 6.8 collective-permute-start
  61.2 42.9 %collective-permute-start.1 = (bf16[1024]{0:T(1024)(128)(2,1)S(1)}, bf16[1024]{0:T(1024)(128)(2,1)}, u32[]{:S(2)}, u32[]{:S(2)}) collective-permute-start(bf16[1024]{0:T(1024)(128)(2,1)S(1)} %pad_maximum_fusion.9), channel_id=1, source_target_pairs={{0,2},{1,3},{2,0},{3,1},{4,6},{5,7},{6,4},{7,5},{8,10},{9,11},{10,... | collective-permute-start | bytes 6152 | tf_op jit(solution)/shard_map/ppermute | solution.py:17
  218.6 29.4 %copy-start.32 = (f32[512]{0:T(512)}, f32[512]{0:T(512)S(1)}, u32[]{:S(2)}) copy-start(f32[512]{0:T(512)S(1)} %broadcast_multiply_fusion.4) | copy-start | bytes 6148
  218.9 29.1 %copy-start.36 = (f32[512]{0:T(512)}, f32[512]{0:T(512)S(1)}, u32[]{:S(2)}) copy-start(f32[512]{0:T(512)S(1)} %add_rsqrt_fusion.1) | copy-start | bytes 6148
  297.7 408.5 %reduce-scatter.19.cloned.1.call-start = ((), (), s32[]{:S(2)}) async-start(), calls=%async_computation.10 | async-start | bytes 7520256
  449.8 37.4 %collective-permute-start.6 = (bf16[1024,768]{0,1:T(8,128)(2,1)S(1)}, bf16[1024,768]{0,1:T(8,128)(2,1)S(1)}, u32[]{:S(2)}, u32[]{:S(2)}) collective-permute-start(bf16[1024,768]{0,1:T(8,128)(2,1)S(1)} %bitcast.235), channel_id=1, source_target_pairs={{0,2},{1,3},{2,0},{3,1},{4,6},{5,7},{6,4},{7,5},{8,10},{9,11},{10,... | collective-permute-start | bytes 4718600 | tf_op jit(solution)/shard_map/ppermute | solution.py:17
  454.7 66.1 %collective-permute-start.8 = (bf16[1024,768]{0,1:T(8,128)(2,1)S(1)}, bf16[1024,768]{0,1:T(8,128)(2,1)S(1)}, u32[]{:S(2)}, u32[]{:S(2)}) collective-permute-start(bf16[1024,768]{0,1:T(8,128)(2,1)S(1)} %bitcast.234), channel_id=1, source_target_pairs={{0,2},{1,3},{2,0},{3,1},{4,6},{5,7},{6,4},{7,5},{8,10},{9,11},{10,... | collective-permute-start | bytes 4718600 | tf_op jit(solution)/shard_map/ppermute | solution.py:17
  455.2 34.8 %slice-start.2 = ((s8[6291456]{0:T(1024)(128)(4,1)}), s8[4194304]{0:T(1024)(128)(4,1)S(1)}, s32[]{:S(2)}) async-start(s8[6291456]{0:T(1024)(128)(4,1)} %bitcast.225), calls=%async_computation.15 | async-start | bytes 8388608
  455.6 34.4 %slice-start.3 = ((s8[6291456]{0:T(1024)(128)(4,1)}), s8[2097152]{0:T(1024)(128)(4,1)S(1)}, s32[]{:S(2)}) async-start(s8[6291456]{0:T(1024)(128)(4,1)} %bitcast.225), calls=%async_computation.16 | async-start | bytes 4194304
  488.0 35.7 %collective-permute-start.7 = (bf16[512,768]{0,1:T(8,128)(2,1)S(1)}, bf16[512,768]{0,1:T(8,128)(2,1)S(1)}, u32[]{:S(2)}, u32[]{:S(2)}) collective-permute-start(bf16[512,768]{0,1:T(8,128)(2,1)S(1)} %slice.176), channel_id=1, source_target_pairs={{0,1},{1,0},{2,3},{3,2},{4,5},{5,4},{6,7},{7,6},{8,9},{9,8},{10,11... | collective-permute-start | bytes 2359304 | tf_op jit(solution)/shard_map/ppermute | solution.py:17
  521.8 19.0 %collective-permute-start.9 = (bf16[512,768]{0,1:T(8,128)(2,1)S(1)}, bf16[512,768]{0,1:T(8,128)(2,1)S(1)}, u32[]{:S(2)}, u32[]{:S(2)}) collective-permute-start(bf16[512,768]{0,1:T(8,128)(2,1)S(1)} %slice.175), channel_id=1, source_target_pairs={{0,1},{1,0},{2,3},{3,2},{4,5},{5,4},{6,7},{7,6},{8,9},{9,8},{10,11... | collective-permute-start | bytes 2359304 | tf_op jit(solution)/shard_map/ppermute | solution.py:17
  554.9 328.1 %reduce-scatter.17.cloned.1.call-start = ((), (), s32[]{:S(2)}) async-start(), calls=%async_computation.9 | async-start | bytes 10027008 | tf_op jit(solution)/shard_map/reduce_scatter | solution.py:260
  563.8 494.8 %reduce-scatter.15.cloned.1.call-start = ((), (), s32[]{:S(2)}) async-start(), calls=%async_computation.8 | async-start | bytes 10027008 | tf_op jit(solution)/shard_map/reduce_scatter | solution.py:259
  572.3 662.5 %reduce-scatter.13.cloned.1.call-start = ((), (), s32[]{:S(2)}) async-start(), calls=%async_computation.7 | async-start | bytes 10027008 | tf_op jit(solution)/shard_map/reduce_scatter | solution.py:258
  580.9 779.2 %reduce-scatter.21.cloned.1.call-start = ((), (), s32[]{:S(2)}) async-start(), calls=%async_computation.11 | async-start | bytes 417792
  585.3 802.2 %all-reduce.3.cloned.1.call-start = ((), (), s32[]{:S(2)}) async-start(), calls=%async_computation.12 | async-start | bytes 3096576 | tf_op jit(solution)/shard_map/psum | solution.py:264
  (65 other events, 354.2 us)
Sparse Core Ops, SparseCore 0:
  297.8 129.1 reduce-scatter.10
  555.0 151.1 reduce-scatter.18
  712.9 170.0 reduce-scatter.16
  888.5 170.0 reduce-scatter.14
  1065.1 169.6 reduce-scatter.12
  1239.9 120.2 reduce-scatter.20
  1364.2 23.1 all-reduce.2
where the time goes:
time: 1410 us; the launch traced here: 1400 us
  waiting for transfers between devices  919 us (65%)
  matrix products  273 us (19%)
  local copies, waits for them, and re-layouts  82.1 us (6%)
  other arithmetic  55.8 us (4%)
  blocking collectives  43.6 us (3%)
  between operations  17.1 us (1%)
    unnamed x9, waiting for transfers between devices  242 us
    reduce_scatter x1, waiting for transfers between devices, local(): lax.psum_scatter(terms[4], 'dp', scatter_dimension=0, tiled=True)  175 us
    reduce_scatter x1, waiting for transfers between devices, local(): lax.psum_scatter(terms[2], 'dp', scatter_dimension=0, tiled=True)  174 us
    reduce_scatter x1, waiting for transfers between devices, local(): lax.psum_scatter(terms[3], 'dp', scatter_dimension=0, tiled=True)  174 us
    ppermute x10, waiting for transfers between devices, swapped(): lax.ppermute(value, axis, [(i, i ^ 1 << bit) for i in range(lax.axis_size...  138 us
    dot_general x41, matrix products, contract_last(): lax.dot_general(left, right, (((1,), (1,)), ((), ())), preferred_element_...  100 us
    dot_general x29, matrix products, contract_first(): lax.dot_general(left, right, (((0,), (0,)), ((), ())), preferred_element_...  85.4 us
    dot_general x12, matrix products, attend_block(): result = jnp.dot(probs, head_values, preferred_element_type=jnp.float32)  32.8 us
  transfers between devices with their start and end apart: 17, of which 12 were waited for; matrix products, arithmetic and copies ran while one was open for 18% of the time, Pallas kernels for 0%

commit v1 on v0

v1 whole, which is shorter than its diff:
```python
import functools

import jax
import jax.numpy as jnp
import numpy as np
from jax import lax
from jax.experimental import pallas as pl
from jax.experimental.pallas import tpu as pltpu
from jax.sharding import PartitionSpec as P

HEADS = 12
HEAD_DIM = 64
SPAN = 4
DOCS_GRP = 3
NH = HEADS // SPAN
HW = NH * HEAD_DIM
CHUNK = 512
VLIM = 62 * 2**20
MESH = pl.DeviceIdType.MESH
f32 = jnp.float32
bf = jnp.bfloat16
precise = lax.Precision.HIGHEST
norm_eps = 1e-05
ANY = pl.BlockSpec(memory_space=pl.ANY)
VM = pl.BlockSpec(memory_space=pltpu.VMEM)


def nn(a, b):
    return lax.dot_general(a, b, (((1,), (0,)), ((), ())), preferred_element_type=f32)


def nt(a, b):
    return lax.dot_general(a, b, (((1,), (1,)), ((), ())), preferred_element_type=f32)


def tn(a, b):
    return lax.dot_general(a, b, (((0,), (0,)), ((), ())), preferred_element_type=f32)


def split3(v):
    one = v.astype(bf).astype(f32)
    rest = v - one
    two = rest.astype(bf).astype(f32)
    return [one, two, rest - two]


def here():
    t = lax.axis_index("tower")
    p = lax.axis_index("dp")
    x = lax.rem(p, 2)
    y = lax.rem(lax.div(p, 2), 2)
    return t, p, x, y, lax.div(p, SPAN)


def plane_peers():
    t, p, x, y, g = here()
    px = p + 1 - 2 * x
    py = p + 2 - 4 * y
    pd = px + 2 - 4 * y
    return (t, px), (t, py), (t, pd)


def greet(peers):
    barrier = pltpu.get_barrier_semaphore()
    for peer in peers:
        pl.semaphore_signal(barrier, inc=1, device_id=peer, device_id_type=MESH)
    pl.semaphore_wait(barrier, len(peers))


def remote(src, dst, send, recv, peer):
    return pltpu.make_async_remote_copy(
        src_ref=src, dst_ref=dst, send_sem=send, recv_sem=recv, device_id=peer, device_id_type=MESH
    )


def dma_sems(n):
    return pltpu.SemaphoreType.DMA((n,))


def comm_params(cid):
    return pltpu.CompilerParams(collective_id=cid, has_side_effects=True, vmem_limit_bytes=VLIM)


def gather_kernel(tok_ref, code_ref, out_ref, codes_ref, send, recv, csend, crecv, lsem):
    t, p, x, y, g = here()
    count = tok_ref.shape[0]
    half = count // 2
    me = lax.rem(p, SPAN)
    ex, ey, ed = plane_peers()
    mx = lax.rem(ex[1], SPAN)
    my = lax.rem(ey[1], SPAN)

    def rows(m, h):
        return pl.ds(pl.multiple_of(m * count + h * half, half), half)

    def lanes(m):
        return pl.ds(pl.multiple_of(m * count, count), count)

    greet((ex, ey, ed))
    first = []
    for i, (peer, h) in enumerate(((ex, 0), (ey, 1), (ex, 1), (ey, 0))):
        c = remote(
            tok_ref.at[pl.ds(h * half, half)], out_ref.at[rows(me, h)], send.at[i], recv.at[i], peer
        )
        c.start()
        first.append(c)
    small = []
    for i, peer in enumerate((ex, ey, ed)):
        c = remote(code_ref, codes_ref.at[:, lanes(me)], csend.at[i], crecv.at[i], peer)
        c.start()
        small.append(c)
    own = pltpu.make_async_copy(tok_ref, out_ref.at[lanes(me)], lsem.at[0])
    own.start()
    own_code = pltpu.make_async_copy(code_ref, codes_ref.at[:, lanes(me)], lsem.at[1])
    own_code.start()
    first[0].wait_recv()
    f0 = remote(out_ref.at[rows(mx, 0)], out_ref.at[rows(mx, 0)], send.at[4], recv.at[4], ey)
    f0.start()
    first[1].wait_recv()
    f1 = remote(out_ref.at[rows(my, 1)], out_ref.at[rows(my, 1)], send.at[5], recv.at[5], ex)
    f1.start()
    first[2].wait_recv()
    first[3].wait_recv()
    f0.wait_recv()
    f1.wait_recv()
    for c in first + [f0, f1]:
        c.wait_send()
    for c in small:
        c.wait()
    own.wait()
    own_code.wait()


def gather(tok, code):
    count, width = tok.shape
    return pl.pallas_call(
        gather_kernel,
        out_shape=(
            jax.ShapeDtypeStruct((SPAN * count, width), bf),
            jax.ShapeDtypeStruct((1, SPAN * count), f32),
        ),
        in_specs=[VM, VM],
        out_specs=(ANY, ANY),
        scratch_shapes=[dma_sems(6), dma_sems(6), dma_sems(3), dma_sems(3), dma_sems(2)],
        compiler_params=comm_params(0),
        name="gather",
    )(tok, code)


def heads_to_tokens_kernel(parts, in_ref, out_ref, send, recv, lsem):
    t, p, x, y, g = here()
    count = out_ref.shape[1]
    me = lax.rem(p, SPAN)
    peers = plane_peers()
    width = parts and out_ref.shape[0] // parts
    greet(peers)
    copies = []
    for i, peer in enumerate((peers[2], peers[0], peers[1])):
        m = lax.rem(peer[1], SPAN)
        for k in range(parts):
            c = remote(
                in_ref.at[pl.ds(k * HW, HW), pl.ds(pl.multiple_of(m * count, count), count)],
                out_ref.at[pl.ds(pl.multiple_of(k * width + me * HW, HW), HW)],
                send.at[i * parts + k],
                recv.at[i * parts + k],
                peer,
            )
            c.start()
            copies.append(c)
    for k in range(parts):
        c = pltpu.make_async_copy(
            in_ref.at[pl.ds(k * HW, HW), pl.ds(pl.multiple_of(me * count, count), count)],
            out_ref.at[pl.ds(pl.multiple_of(k * width + me * HW, HW), HW)],
            lsem.at[k],
        )
        c.start()
        copies.append(c)
    for c in copies:
        c.wait()


def heads_to_tokens(a, cid, name):
    parts = a.shape[0] // HW
    count = a.shape[1] // SPAN
    return pl.pallas_call(
        functools.partial(heads_to_tokens_kernel, parts),
        out_shape=jax.ShapeDtypeStruct((parts * HEADS * HEAD_DIM, count), a.dtype),
        in_specs=[VM],
        out_specs=ANY,
        scratch_shapes=[dma_sems(3 * parts), dma_sems(3 * parts), dma_sems(parts)],
        compiler_params=comm_params(cid),
        name=name,
    )(a)


def tokens_to_heads_kernel(in_ref, out_ref, send, recv, lsem):
    t, p, x, y, g = here()
    count = in_ref.shape[1]
    me = lax.rem(p, SPAN)
    peers = plane_peers()
    greet(peers)
    mine = pl.ds(pl.multiple_of(me * count, count), count)
    copies = []
    for i, peer in enumerate((peers[2], peers[0], peers[1])):
        m = lax.rem(peer[1], SPAN)
        c = remote(
            in_ref.at[pl.ds(pl.multiple_of(m * HW, HW), HW)],
            out_ref.at[:, mine],
            send.at[i],
            recv.at[i],
            peer,
        )
        c.start()
        copies.append(c)
    c = pltpu.make_async_copy(
        in_ref.at[pl.ds(pl.multiple_of(me * HW, HW), HW)], out_ref.at[:, mine], lsem.at[0]
    )
    c.start()
    for c in copies + [c]:
        c.wait()


def tokens_to_heads(a, cid, name):
    return pl.pallas_call(
        tokens_to_heads_kernel,
        out_shape=jax.ShapeDtypeStruct((HW, SPAN * a.shape[1]), a.dtype),
        in_specs=[VM],
        out_specs=ANY,
        scratch_shapes=[dma_sems(3), dma_sems(3), dma_sems(1)],
        compiler_params=comm_params(cid),
        name=name,
    )(a)


def loss_kernel(groups, sums_ref, goal_ref, gp_ref, scores_ref, loss_ref, plane, allp, ge, send, recv):
    t, p, x, y, g = here()
    docs = groups * DOCS_GRP
    me = lax.rem(p, SPAN)
    peers = plane_peers()
    sibling = (1 - t, p)
    line = [(t, lax.rem(p + SPAN * k, SPAN * groups)) for k in range(1, groups)]
    greet(tuple(peers) + tuple(line) + (sibling,))
    copies = []
    for i, peer in enumerate(peers):
        c = remote(sums_ref, plane.at[i], send.at[i], recv.at[i], peer)
        c.start()
        copies.append(c)
    for c in copies:
        c.wait()
    own = sums_ref[...] + plane[0]
    own = own + (plane[1] + plane[2])
    allp[t, g] = own
    rows = allp.at[t, g]
    copies = []
    for i, peer in enumerate(line):
        c = remote(rows, rows, send.at[3 + i], recv.at[3 + i], peer)
        c.start()
        copies.append(c)
    for c in copies:
        c.wait()
    c = remote(allp.at[t], allp.at[t], send.at[2 + groups], recv.at[2 + groups], sibling)
    c.start()
    c.wait()
    width = sums_ref.shape[1]
    size = groups * 8
    pools = [allp[k].reshape(size, width) for k in range(2)]
    invs = [lax.rsqrt(jnp.sum(v * v, -1, keepdims=True) + 1e-06) for v in pools]
    embeds = [v * r for v, r in zip(pools, invs)]
    dot = functools.partial(lax.dot_general, precision=precise, preferred_element_type=f32)
    scores = dot(embeds[0], embeds[1], (((1,), (1,)), ((), ()))) * 50.0
    col = lax.broadcasted_iota(jnp.int32, (size, size), 1)
    row = lax.broadcasted_iota(jnp.int32, (size, size), 0)
    live = lax.rem(col, 8) < DOCS_GRP
    alive = lax.rem(row, 8) < DOCS_GRP
    masked = jnp.where(live, scores, -1e30)
    top = jnp.max(masked, -1, keepdims=True)
    total = jnp.sum(jnp.exp(masked - top), -1, keepdims=True)
    log_sums = top + jnp.log(total)
    hot = jnp.where(col.astype(f32) == goal_ref[:, 0:1], 1.0, 0.0)
    chosen = jnp.sum(hot * scores, -1, keepdims=True)
    each = jnp.where(alive[:, 0:1], log_sums - chosen, 0.0)
    loss_ref[...] = jnp.broadcast_to(jnp.sum(each, 0, keepdims=True) / docs, loss_ref.shape)
    scores_ref[...] = scores
    gs = jnp.where(alive & live, (jnp.exp(masked - log_sums) - hot) / docs, 0.0)
    gq = dot(gs, embeds[1], (((1,), (0,)), ((), ())))
    gd = dot(gs, embeds[0], (((0,), (0,)), ((), ())))
    ge[...] = jnp.where(t == 0, gq, gd) * 50.0
    mine = ge[pl.ds(pl.multiple_of(g * 8, 8), 8), :]
    pooled = allp[t, g]
    inv = lax.rsqrt(jnp.sum(pooled * pooled, -1, keepdims=True) + 1e-06)
    gp_ref[...] = inv * mine - inv * inv * inv * pooled * jnp.sum(pooled * mine, -1, keepdims=True)


def contrast(sums, goal, groups):
    size = groups * 8
    width = sums.shape[1]
    return pl.pallas_call(
        functools.partial(loss_kernel, groups),
        out_shape=(
            jax.ShapeDtypeStruct((8, width), f32),
            jax.ShapeDtypeStruct((size, size), f32),
            jax.ShapeDtypeStruct((8, 128), f32),
        ),
        in_specs=[VM, VM],
        out_specs=(VM, VM, VM),
        scratch_shapes=[
            pltpu.VMEM((3, 8, width), f32),
            pltpu.VMEM((2, groups, 8, width), f32),
            pltpu.VMEM((size, width), f32),
            dma_sems(3 + groups),
            dma_sems(3 + groups),
        ],
        compiler_params=comm_params(1),
        name="contrast",
    )(sums, goal)


def doc_limits(code):
    pad = code >= 4.0
    mem = jnp.where(pad, code - 4.0, code)
    n0 = jnp.sum(jnp.where(mem < 0.5, 1.0, 0.0)).astype(jnp.int32)
    n1 = jnp.sum(jnp.where(mem < 1.5, 1.0, 0.0)).astype(jnp.int32)
    l = [jnp.sum(jnp.where(code == float(d), 1.0, 0.0)).astype(jnp.int32) for d in range(3)]
    return n0, n1, l

def block_range(lims, a, size, total):
    n0, n1, l = lims
    b = a + size - 1
    first = (a >= n0).astype(jnp.int32) + (a >= n1).astype(jnp.int32)
    last = (b >= n0).astype(jnp.int32) + (b >= n1).astype(jnp.int32)
    lo = jnp.where(first == 0, 0, jnp.where(first == 1, n0, n1))
    hi = jnp.where(last == 0, n0, jnp.where(last == 1, n1, total))
    dead = jnp.zeros((), jnp.bool_)
    for d in range(3):
        dead = dead | ((first <= d) & (d <= last) & (l[d] == 0))
    return jnp.where(dead, 0, lo), jnp.where(dead, total, hi)

def fwd_kernel(KB, QB, tok_ref, wt_ref, cos_ref, sin_ref, code_ref, out_ref, lse_ref, o32_ref, qa_ref, ka_ref, va_ref,
               kt_ref, acc_ref):
    T = tok_ref.shape[0]
    CH = 512
    hw = HW
    code = code_ref[...]
    lims = doc_limits(code)
    def proj(c, _):
        sl = pl.ds(pl.multiple_of(c*CH, CH), CH)
        mx = nt(wt_ref[...], tok_ref[sl, :])
        cos = cos_ref[:, sl]; sin = sin_ref[:, sl]
        cd = code_ref[:, sl]
        mem = jnp.where(cd >= 4.0, cd-4.0, cd)
        hot = jnp.concatenate([jnp.where(mem == float(d), 1.0, 0.0) for d in range(3)] + [jnp.zeros((13, CH), f32)], 0)
        neg = jnp.concatenate([jnp.where(cd == float(d), 0.0, -1e30) for d in range(3)] + [jnp.zeros((13, CH), f32)], 0)
        zer = jnp.zeros((48, CH), f32)
        one = jnp.concatenate([jnp.ones((1, CH), f32), jnp.zeros((63, CH), f32)], 0)
        def rope(u):
            a = u[:32]; b = u[32:]
            return jnp.concatenate([a*cos - b*sin, b*cos + a*sin], 0)
        for h in range(NH):
            q = rope(mx[h*HEAD_DIM:(h+1)*HEAD_DIM]).astype(bf).astype(f32)*0.125
            k = rope(mx[hw+h*HEAD_DIM:hw+(h+1)*HEAD_DIM])
            v = mx[2*hw+h*HEAD_DIM:2*hw+(h+1)*HEAD_DIM]
            qa_ref[h, :, sl] = jnp.concatenate([q, hot, zer], 0).astype(bf)
            ka_ref[h, sl, :] = jnp.concatenate([k, neg, zer], 0).T.astype(bf)
            va_ref[h, :, sl] = jnp.concatenate([v, one], 0).astype(bf)
            kt_ref[h, :, sl] = k.astype(bf)
        return 0
    lax.fori_loop(0, T//CH, proj, 0)
    def qblock(i, _):
        a = i*QB
        qs = pl.ds(pl.multiple_of(a, QB), QB)
        lo, hi = block_range(lims, a, QB, T)
        jlo = lo//KB; jhi = (hi+KB-1)//KB
        for h in range(NH):
            acc_ref[h] = jnp.zeros_like(acc_ref[h])
        def kv(j, ms):
            ks = pl.ds(pl.multiple_of(j*KB, KB), KB)
            new = []
            ss = [nn(ka_ref[h, ks, :], qa_ref[h, :, qs]) for h in range(NH)]
            for h in range(NH):
                s = ss[h]
                mn = jnp.maximum(ms[h], jnp.max(s, 0, keepdims=True))
                p = jnp.exp(s - mn).astype(bf)
                al = jnp.exp(ms[h]-mn)
                acc_ref[h] = acc_ref[h]*al + nn(va_ref[h, :80, ks], p)
                new.append(mn)
            return tuple(new)
        ms = lax.fori_loop(jlo, jhi, kv, tuple(jnp.full((1, QB), -3e38, f32) for _ in range(NH)))
        for h in range(NH):
            tot = acc_ref[h, 64:65, :]
            o = acc_ref[h, :64, :]/tot
            o32_ref[h*HEAD_DIM:(h+1)*HEAD_DIM, qs] = o
            lse_ref[h:h+1, qs] = jnp.where(ms[h] < -1e29, 0.0, ms[h] + jnp.log(tot))
            out_ref[h*HEAD_DIM:(h+1)*HEAD_DIM, qs] = o.astype(bf)
        return 0
    lax.fori_loop(0, T//QB, qblock, 0)

def attn_fwd(tok, wt, cos, sin, code, KB=512, QB=256):
    T = tok.shape[0]
    return pl.pallas_call(functools.partial(fwd_kernel, KB, QB),
        out_shape=(jax.ShapeDtypeStruct((NH*HEAD_DIM, T), bf), jax.ShapeDtypeStruct((NH, T), f32), jax.ShapeDtypeStruct((NH*HEAD_DIM, T), f32),
                   jax.ShapeDtypeStruct((NH,128,T), bf), jax.ShapeDtypeStruct((NH,T,128), bf), jax.ShapeDtypeStruct((NH,128,T), bf), jax.ShapeDtypeStruct((NH,HEAD_DIM,T), bf)),
        in_specs=[pl.BlockSpec(memory_space=pltpu.VMEM)]*5, out_specs=tuple([pl.BlockSpec(memory_space=pltpu.VMEM)]*7),
        scratch_shapes=[pltpu.VMEM((NH,80,QB), f32)],
        compiler_params=pltpu.CompilerParams(vmem_limit_bytes=VLIM), name="attn_fwd",
        cost_estimate=pl.CostEstimate(flops=int(2*T*768*576+4*T*T*128*3), bytes_accessed=12<<20, transcendentals=T*T*3))(tok, wt, cos, sin, code)

def bwd_kernel(KB, QB, do_ref, o32_ref, lse_ref, qa_ref, ka_ref, va_ref, kt_ref, cos_ref, sin_ref, code_ref, g_ref,
               vn_ref, dn_ref, da_ref, qb_ref, acc_ref, dq_ref):
    T = do_ref.shape[1]
    hw = HW
    CH = 512
    lims = doc_limits(code_ref[...])
    def prep(c, _):
        sl = pl.ds(pl.multiple_of(c*CH, CH), CH)
        for h in range(NH):
            do = do_ref[h*HEAD_DIM:(h+1)*HEAD_DIM, sl].astype(f32)
            delta = jnp.sum(do*o32_ref[h*HEAD_DIM:(h+1)*HEAD_DIM, sl], 0, keepdims=True)
            def split(x):
                x1 = x.astype(bf).astype(f32); r = x-x1
                x2 = r.astype(bf).astype(f32); x3 = r-x2
                return [x1, x2, x3]
            z13 = jnp.zeros((13, CH), f32); z48 = jnp.zeros((48, CH), f32)
            da_ref[h, :, sl] = jnp.concatenate([do]+split(-delta)+[z13, z48], 0).astype(bf)
            one = jnp.concatenate([jnp.ones((3, CH), f32), jnp.zeros((61, CH), f32)], 0)
            v = va_ref[h, :64, sl].astype(f32)
            vn_ref[h, sl, :] = jnp.concatenate([v, one], 0).T.astype(bf)
            z64 = jnp.zeros((64, CH), f32)
            q = qa_ref[h, :64, sl].astype(f32)
            dn_ref[h, sl, :] = jnp.concatenate([do, z64], 0).T.astype(bf)
            qb_ref[h, sl, :] = jnp.concatenate([z64, q], 0).T.astype(bf)
            acc_ref[h, sl, :] = jnp.zeros((CH, 128), f32)
        return 0
    lax.fori_loop(0, T//CH, prep, 0)
    def qblock(i, _):
        a = i*QB
        qs = pl.ds(pl.multiple_of(a, QB), QB)
        lo, hi = block_range(lims, a, QB, T)
        jlo = lo//KB; jhi = (hi+KB-1)//KB
        dq_ref[...] = jnp.zeros_like(dq_ref)
        def kv(j, _):
            ks = pl.ds(pl.multiple_of(j*KB, KB), KB)
            for h in range(NH):
                s = nn(ka_ref[h, ks, :], qa_ref[h, :, qs])
                dp = nn(vn_ref[h, ks, :], da_ref[h, :, qs])
                p = jnp.exp(s - lse_ref[h:h+1, qs])
                ds = (p*dp).astype(bf)
                acc_ref[h, ks, :] += nn(p.astype(bf), dn_ref[h, qs, :]) + nn(ds, qb_ref[h, qs, :])
                dq_ref[h] += nn(kt_ref[h, :, ks], ds)
            return 0
        lax.fori_loop(jlo, jhi, kv, 0)
        cos = cos_ref[:, qs]; sin = sin_ref[:, qs]
        for h in range(NH):
            u = dq_ref[h]*0.125
            x1 = u[:32]; x2 = u[32:]
            g_ref[h*HEAD_DIM:(h+1)*HEAD_DIM, qs] = jnp.concatenate([x1*cos+x2*sin, x2*cos-x1*sin], 0).astype(bf)
        return 0
    lax.fori_loop(0, T//QB, qblock, 0)
    def fin(c, _):
        sl = pl.ds(pl.multiple_of(c*CH, CH), CH)
        cos = cos_ref[:, sl]; sin = sin_ref[:, sl]
        for h in range(NH):
            t = acc_ref[h, sl, :].T
            x1 = t[64:96]; x2 = t[96:128]
            g_ref[hw+h*HEAD_DIM:hw+(h+1)*HEAD_DIM, sl] = jnp.concatenate([x1*cos+x2*sin, x2*cos-x1*sin], 0).astype(bf)
            g_ref[2*hw+h*HEAD_DIM:2*hw+(h+1)*HEAD_DIM, sl] = t[:64].astype(bf)
        return 0
    lax.fori_loop(0, T//CH, fin, 0)

def attn_bwd(do, o32, lse, qa, ka, va, kt, cos, sin, code, KB=512, QB=256):
    T = do.shape[1]
    return pl.pallas_call(functools.partial(bwd_kernel, KB, QB),
        out_shape=jax.ShapeDtypeStruct((3*NH*HEAD_DIM, T), bf),
        in_specs=[pl.BlockSpec(memory_space=pltpu.VMEM)]*10, out_specs=pl.BlockSpec(memory_space=pltpu.VMEM),
        scratch_shapes=[pltpu.VMEM((NH,T,128), bf), pltpu.VMEM((NH,T,128), bf), pltpu.VMEM((NH,128,T), bf), pltpu.VMEM((NH,T,128), bf),
                        pltpu.VMEM((NH,T,128), f32), pltpu.VMEM((NH,HEAD_DIM,QB), f32)],
        compiler_params=pltpu.CompilerParams(vmem_limit_bytes=VLIM), name="attn_bwd",
        cost_estimate=pl.CostEstimate(flops=int(10*T*T*128*3), bytes_accessed=12<<20, transcendentals=T*T*3))(do, o32, lse, qa, ka, va, kt, cos, sin, code)


def weights_kernel(
    shards, ia, ib, ga, gb, ha, hb, ma, mb, aa, ab, ba, bb, out_ref, it_ref
):
    width = ia.shape[1]
    half = width // 2
    one = width // shards
    steps = ga.shape[1] // half
    down = ha.shape[1] // shards
    count = ia.shape[0]
    it_ref[:, :count] = ia[...].T
    it_ref[:, count:] = ib[...].T

    def upward(j, _):
        cols = pl.ds(pl.multiple_of(j * half, half), half)
        r = nn(it_ref[:, :count], ga[:, cols]) + nn(it_ref[:, count:], gb[:, cols])
        out_ref[:, pl.ds(pl.multiple_of(j * one, one), one), :] = r.astype(bf).reshape(
            shards, one, half
        )
        return 0

    lax.fori_loop(0, steps, upward, 0)
    top = steps * one
    per = half // down

    def downward(j, _):
        cols = pl.ds(pl.multiple_of(j * half, half), half)
        r = tn(ha[:, cols], ma[...]) + tn(hb[:, cols], mb[...])
        out_ref[pl.ds(j * per, per), top : top + down, :] = r.astype(bf).reshape(per, down, half)
        return 0

    lax.fori_loop(0, ha.shape[1] // half, downward, 0)
    r = nn(aa[...], ba[...]) + nn(ab[...], bb[...])
    out_ref[:, top + down :, :] = r.astype(bf).reshape(shards, one, half)


def weight_grads(shards, *arrays):
    width = arrays[0].shape[1]
    count = arrays[0].shape[0]
    half = width // 2
    one = width // shards
    rows = one * (arrays[2].shape[1] // half) + arrays[4].shape[1] // shards + one
    return pl.pallas_call(
        functools.partial(weights_kernel, shards),
        out_shape=jax.ShapeDtypeStruct((shards, rows, half), bf),
        in_specs=[VM] * 12,
        out_specs=VM,
        scratch_shapes=[pltpu.VMEM((width, 2 * count), bf)],
        compiler_params=pltpu.CompilerParams(vmem_limit_bytes=VLIM),
        name="weight_grads",
    )(*arrays)


def add_rows(dst, a, b, rows):
    def step(i, _):
        sl = pl.ds(pl.multiple_of(i * 16, 16), 16)
        dst[sl, :] = (a[sl, :].astype(f32) + b[sl, :].astype(f32)).astype(bf)
        return 0

    lax.fori_loop(0, rows // 16, step, 0)


class Line:
    def __init__(self, z, zt, groups, part, up, down, sems, t, p):
        self.z, self.zt, self.groups = z, zt, groups
        self.part, self.up, self.down = part, up, down
        us, ur, ds, dr = sems
        above = (t, lax.rem(p + SPAN, SPAN * groups))
        below = (t, lax.rem(p + SPAN * (groups - 1), SPAN * groups))
        self.up_first = remote(part, up, us, ur, above)
        self.up_next = remote(up, up, us, ur, above)
        self.down_first = remote(part, down, ds, dr, below)
        self.down_next = remote(down, down, ds, dr, below)

    def start(self):
        if self.zt > 0:
            pl.when(self.z == 0)(lambda: self.up_first.start())
        if self.zt < self.groups - 1:
            pl.when(self.z == self.groups - 1)(lambda: self.down_first.start())

    def relay(self, hop, rows):
        def up():
            self.up_next.wait_recv()
            add_rows(self.up, self.up, self.part, rows)
            self.up_next.start()

        def down():
            self.down_next.wait_recv()
            add_rows(self.down, self.down, self.part, rows)
            self.down_next.start()

        if 0 < hop < self.zt:
            pl.when(self.z == hop)(up)
        if self.zt < self.groups - 1 - hop:
            pl.when(self.z == self.groups - 1 - hop)(down)

    def finish(self, dst, rows):
        def done():
            if self.zt > 0:
                self.up_next.wait_recv()
            if self.zt < self.groups - 1:
                self.down_next.wait_recv()
            if 0 < self.zt < self.groups - 1:
                add_rows(self.up, self.up, self.down, rows)
            add_rows(dst, self.up if self.zt > 0 else self.down, self.part, rows)

        pl.when(self.z == self.zt)(done)

    def drain(self):
        if self.zt > 0:
            pl.when(self.z < self.zt)(lambda: self.up_first.wait_send())
        if self.zt < self.groups - 1:
            pl.when(self.z > self.zt)(lambda: self.down_first.wait_send())


def outward(groups):
    order = []
    lo, hi = 0, groups - 1
    while lo <= hi:
        order.append(hi)
        if lo < hi:
            order.append(lo)
        lo, hi = lo + 1, hi - 1
    return order


def scatter_kernel(groups, w_ref, gain_ref, out_ref, sum_ref, r1a, r1b, r2a, r2b, ua, ub, da, db,
                   s1, q1, s2, q2, us, ur, ds, dr, plane, line, gs, gr, fs, fr):
    t, p, x, y, z = here()
    ex, ey, ed = plane_peers()
    sibling = (1 - t, p)
    others = [(t, lax.rem(p + SPAN * k, SPAN * groups)) for k in range(1, groups)]
    greet((ex, ey, ed, sibling) + tuple(others))
    rows = w_ref.shape[1]
    ra = r1a.shape[1]
    rb = rows - ra
    order = outward(groups)
    colours = (
        (ex, ey, r1a, r2a, ua, da, pl.ds(0, ra), ra,
         lambda zt, k: zt * 4 + k * 2 + (1 - x), lambda zt, k: zt * 4 + k * 2 + x, y),
        (ey, ex, r1b, r2b, ub, db, pl.ds(ra, rb), rb,
         lambda zt, k: zt * 4 + (1 - y) * 2 + k, lambda zt, k: zt * 4 + y * 2 + k, x),
    )

    def first(c, zt, k):
        one, two, r1, r2, u, d, sl, n, away, own, mine = colours[c]
        i = (c * groups + zt) * 2 + k
        return remote(w_ref.at[away(zt, k), sl], r1.at[zt * 2 + k], s1.at[i], q1.at[i], one)

    def second(c, zt):
        one, two, r1, r2, u, d, sl, n, away, own, mine = colours[c]
        i = c * groups + zt
        return remote(r1.at[zt * 2 + 1 - mine], r2.at[zt], s2.at[i], q2.at[i], two)

    def chain(c, zt):
        one, two, r1, r2, u, d, sl, n, away, own, mine = colours[c]
        i = c * groups + zt
        return Line(z, zt, groups, r2.at[zt], u.at[zt], d.at[zt],
                    (us.at[i], ur.at[i], ds.at[i], dr.at[i]), t, p)

    def issue(zt):
        for k in range(2):
            for c in range(2):
                first(c, zt, k).start()

    def half_way(zt):
        for k in range(2):
            for c in range(2):
                one, two, r1, r2, u, d, sl, n, away, own, mine = colours[c]
                first(c, zt, k).wait_recv()
                dst = r1.at[zt * 2 + k]
                add_rows(dst, dst, w_ref.at[own(zt, k), sl], n)
        for c in range(2):
            second(c, zt).start()

    def in_plane(zt):
        for c in range(2):
            one, two, r1, r2, u, d, sl, n, away, own, mine = colours[c]
            second(c, zt).wait_recv()
            dst = r2.at[zt]
            add_rows(dst, dst, r1.at[zt * 2 + mine], n)
            chain(c, zt).start()

    def relay(zt, hop):
        for c in range(2):
            chain(c, zt).relay(hop, colours[c][7])

    issue(order[0])
    if groups > 1:
        issue(order[1])
    gain_copies = []
    for i, peer in enumerate((ex, ey, ed)):
        c = remote(gain_ref, plane.at[i], gs.at[i], gr.at[i], peer)
        c.start()
        gain_copies.append(c)
    todo = []
    for i, zt in enumerate(order):
        half_way(zt)
        if i + 2 < groups:
            issue(order[i + 2])
        if i >= 1:
            in_plane(order[i - 1])
            todo.append((order[i - 1], 0))
        if i == 0:
            for c in gain_copies:
                c.wait()
            sum_ref[...] = gain_ref[...] + plane[0]
            sum_ref[...] = sum_ref[...] + (plane[1] + plane[2])
            line[0] = sum_ref[...]
            gain_copies = []
            for k, peer in enumerate(others):
                c = remote(line.at[0], line.at[1 + k], gs.at[3 + k], gr.at[3 + k], peer)
                c.start()
                gain_copies.append(c)
        if i == 1:
            for c in gain_copies:
                c.wait()
            total = line[0]
            for k in range(1, groups):
                total = total + line[k]
            line[groups] = total
            c = remote(line.at[groups], line.at[groups + 1], gs.at[2 + groups], gr.at[2 + groups], sibling)
            c.start()
            gain_copies = [c]
        if i >= 2:
            for hop in range(1, groups - 1):
                if hop == 1:
                    relay(order[i - 2], hop)
    in_plane(order[groups - 1])
    for hop in range(1, groups - 1):
        for i, zt in enumerate(order):
            if hop > 1 or i >= groups - 2:
                relay(zt, hop)
    for zt in order:
        for c in range(2):
            sl, n = colours[c][6], colours[c][7]
            chain(c, zt).finish(out_ref.at[t, sl], n)
    last = remote(out_ref.at[t], out_ref.at[t], fs.at[0], fr.at[0], sibling)
    last.start()
    for c in gain_copies:
        c.wait()
    sum_ref[...] = line[groups] + line[groups + 1]
    for zt in order:
        for c in range(2):
            for k in range(2):
                first(c, zt, k).wait_send()
            second(c, zt).wait_send()
            chain(c, zt).drain()
    last.wait()


def scatter(w, gains, groups):
    rows, half = w.shape[1:]
    ra = (rows // 32 + 1) * 16 if rows % 32 else rows // 2
    rb = rows - ra
    buf = lambda n, r: pltpu.VMEM((n, r, half), bf)
    return pl.pallas_call(
        functools.partial(scatter_kernel, groups),
        out_shape=(
            jax.ShapeDtypeStruct((2, rows, half), bf),
            jax.ShapeDtypeStruct(gains.shape, f32),
        ),
        in_specs=[VM, VM],
        out_specs=(VM, VM),
        scratch_shapes=[
            buf(2 * groups, ra), buf(2 * groups, rb), buf(groups, ra), buf(groups, rb),
            buf(groups, ra), buf(groups, rb), buf(groups, ra), buf(groups, rb),
            dma_sems(4 * groups), dma_sems(4 * groups), dma_sems(2 * groups), dma_sems(2 * groups),
            dma_sems(2 * groups), dma_sems(2 * groups), dma_sems(2 * groups), dma_sems(2 * groups),
            pltpu.VMEM((3,) + gains.shape, f32), pltpu.VMEM((groups + 2,) + gains.shape, f32),
            dma_sems(3 + groups), dma_sems(3 + groups), dma_sems(1), dma_sems(1),
        ],
        compiler_params=comm_params(2),
        name="scatter",
    )(w, gains)


def tail_kernel(groups, g_ref, tok_ref, gm_ref, out_ref, w2, sib, ub, db, fin, send, recv, ts, tr,
                us, ur, ds, dr, ps, pr, lsem):
    t, p, x, y, z = here()
    count = gm_ref.shape[1]
    me = lax.rem(p, SPAN)
    peers = plane_peers()
    sibling = (1 - t, p)
    others = [(t, lax.rem(p + SPAN * k, SPAN * groups)) for k in range(1, groups)]
    across = [(1 - t, q[1]) for q in peers]
    greet(tuple(peers) + tuple(across) + (sibling,) + tuple(others))
    width = gm_ref.shape[0] // 3
    copies = []
    for i, peer in enumerate((peers[2], peers[0], peers[1])):
        m = lax.rem(peer[1], SPAN)
        for k in range(3):
            c = remote(
                g_ref.at[pl.ds(k * HW, HW), pl.ds(pl.multiple_of(m * count, count), count)],
                gm_ref.at[pl.ds(pl.multiple_of(k * width + me * HW, HW), HW)],
                send.at[i * 3 + k], recv.at[i * 3 + k], peer,
            )
            c.start()
            copies.append(c)
    for k in range(3):
        c = pltpu.make_async_copy(
            g_ref.at[pl.ds(k * HW, HW), pl.ds(pl.multiple_of(me * count, count), count)],
            gm_ref.at[pl.ds(pl.multiple_of(k * width + me * HW, HW), HW)],
            lsem.at[k],
        )
        c.start()
        copies.append(c)
    shards = SPAN * groups
    one = width // shards
    half = width // 2
    for h in range(2):
        r = nn(g_ref[...], tok_ref[:, h * half : (h + 1) * half]).T
        w2[h * (shards // 2) : (h + 1) * (shards // 2)] = r.astype(bf).reshape(shards // 2, one, 3 * HW)
    swaps = []
    for zt in outward(groups):
        c = remote(w2.at[pl.ds(zt * 4 + (1 - t) * 2, 2)], sib.at[zt], ts.at[zt], tr.at[zt], sibling)
        c.start()
        swaps.append(c)

    def chain(zt, k):
        i = zt * 2 + k
        return Line(z, zt, groups, sib.at[zt, k], ub.at[zt, k], db.at[zt, k],
                    (us.at[i], ur.at[i], ds.at[i], dr.at[i]), t, p)

    for c, zt in zip(swaps, outward(groups)):
        c.wait_recv()
        for k in range(2):
            dst = sib.at[zt, k]
            add_rows(dst, dst, w2.at[zt * 4 + t * 2 + k], one)
            chain(zt, k).start()
    for hop in range(1, groups - 1):
        for zt in outward(groups):
            for k in range(2):
                chain(zt, k).relay(hop, one)
    for zt in outward(groups):
        for k in range(2):
            chain(zt, k).finish(fin.at[k], one)
    here_id = t * SPAN + me

    def hand(k, tt):
        m = t * 2 + k
        peer = (tt, z * SPAN + m)
        i = k * 2 + tt
        away = remote(fin.at[k], out_ref.at[me], ps.at[i], pr.at[me], peer)
        stay = pltpu.make_async_copy(fin.at[k], out_ref.at[me], lsem.at[3])
        return away, stay, (tt * SPAN + m) == here_id

    for k in range(2):
        for tt in range(2):
            away, stay, same = hand(k, tt)
            pl.when(jnp.logical_not(same))(lambda away=away: away.start())
            pl.when(same)(lambda stay=stay: stay.start())
    for s in range(SPAN):
        mine = jnp.logical_and(s == me, y == t)
        got = remote(fin.at[0], out_ref.at[s], ps.at[0], pr.at[s], sibling)
        pl.when(jnp.logical_not(mine))(lambda got=got: got.wait_recv())
    for k in range(2):
        for tt in range(2):
            away, stay, same = hand(k, tt)
            pl.when(jnp.logical_not(same))(lambda away=away: away.wait_send())
            pl.when(same)(lambda stay=stay: stay.wait())
    for c in swaps:
        c.wait_send()
    for zt in range(groups):
        for k in range(2):
            chain(zt, k).drain()
    for c in copies:
        c.wait()


def tail(g, tok, groups):
    width = tok.shape[1]
    count = tok.shape[0] // SPAN
    one = width // (SPAN * groups)
    buf = lambda *n: pltpu.VMEM(n + (one, 3 * HW), bf)
    return pl.pallas_call(
        functools.partial(tail_kernel, groups),
        out_shape=(
            jax.ShapeDtypeStruct((3 * width, count), bf),
            jax.ShapeDtypeStruct((SPAN, one, 3 * HW), bf),
        ),
        in_specs=[VM, VM],
        out_specs=(ANY, VM),
        scratch_shapes=[
            buf(SPAN * groups), buf(groups, 2), buf(groups, 2), buf(groups, 2), buf(2),
            dma_sems(9), dma_sems(9), dma_sems(groups), dma_sems(groups),
            dma_sems(2 * groups), dma_sems(2 * groups), dma_sems(2 * groups), dma_sems(2 * groups),
            dma_sems(4), dma_sems(SPAN), dma_sems(4),
        ],
        compiler_params=comm_params(3),
        name="tail",
    )(g, tok)


def swapped(value):
    return lax.ppermute(value, "tower", [(0, 1), (1, 0)])


def norm_rows(values, gain, bias):
    centred = values - jnp.mean(values, -1, keepdims=True)
    spread = jnp.mean(centred * centred, -1, keepdims=True)
    scale = lax.rsqrt(spread + norm_eps)
    normed = centred * scale
    return normed * gain + bias, normed, scale


def norm_back(grad, normed, scale, gain):
    shaped = grad * gain
    inner = (
        shaped
        - jnp.mean(shaped, -1, keepdims=True)
        - normed * jnp.mean(shaped * normed, -1, keepdims=True)
    )
    return inner * scale, jnp.sum(grad * normed, 0), jnp.sum(grad, 0)


def angle_tables(total):
    half = HEAD_DIM // 2
    freqs = np.float32(1000.0) ** (-np.arange(half, dtype=np.float32) / np.float32(half))
    theta = freqs[:, None].astype(np.float32) * np.arange(total, dtype=np.float32)[None, :]
    return np.cos(theta).astype(np.float32), np.sin(theta).astype(np.float32)


def spread_sum(value):
    part = lax.psum_scatter(value, "dp", scatter_dimension=0, tiled=True)
    return lax.psum(part.astype(bf), "tower").astype(f32)


def local(
    tokens, doc_ids, pad_mask, targets, w_qkv, w_out, ln1_gain, ln1_bias,
    w_gate, w_up, w_down, ln2_gain, ln2_bias,
):
    width = w_out.shape[0]
    rows = tokens[0]
    count = rows.shape[0]
    places = lax.axis_size("dp")
    groups = places // SPAN
    tower = lax.axis_index("tower")
    place = lax.axis_index("dp")
    me = place % SPAN
    member_of = doc_ids[0] % DOCS_GRP
    live = pad_mask[0] == 1
    code = jnp.where(live, member_of, member_of + 4).astype(f32)[None, :]
    docs = groups * DOCS_GRP
    slot = jnp.arange(groups * 8)
    goal = jnp.where(
        slot % 8 < DOCS_GRP, targets[jnp.minimum(slot // 8 * DOCS_GRP + slot % 8, docs - 1)], 0
    )
    goal = jnp.where(slot % 8 < DOCS_GRP, goal // DOCS_GRP * 8 + goal % DOCS_GRP, -1)
    goal = jnp.broadcast_to(goal.astype(f32)[:, None], (groups * 8, 128))
    w_mine = lax.dynamic_index_in_dim(w_qkv.reshape(width, 3, SPAN, HW), me, 2, keepdims=False)
    w_mine = w_mine.reshape(width, 3 * HW).T
    cos, sin = angle_tables(SPAN * count)
    tok_all, codes = gather(rows, code)
    heads_out, lse, exact, qa, ka, va, kt = attn_fwd(tok_all, w_mine, cos, sin, codes)
    attended = heads_to_tokens(heads_out, 4, "to_tokens")
    branch = tn(attended, w_out)
    first, normed_one, scale_one = norm_rows(rows.astype(f32) + branch, ln1_gain, ln1_bias)
    inner = first.astype(bf)
    gate = nn(inner, w_gate)
    upper = nn(inner, w_up)
    sigmoid = jax.nn.sigmoid(gate)
    activated = gate * sigmoid
    hidden = (activated * upper).astype(bf)
    second, normed_two, scale_two = norm_rows(first + nn(hidden, w_down), ln2_gain, ln2_bias)
    member = ((member_of[:, None] == jnp.arange(8)[None, :]) & live[:, None]).astype(f32)
    sums = jnp.dot(member.T, second, precision=precise)
    grad_pool, scores_all, loss = contrast(sums, goal, groups)
    scores = scores_all.reshape(groups, 8, groups, 8)[:, :DOCS_GRP, :, :DOCS_GRP].reshape(docs, docs)
    grad_second = jnp.dot(member, grad_pool, precision=precise)
    grad_h2, gain_two, bias_two = norm_back(grad_second, normed_two, scale_two, ln2_gain)
    grad_mlp = grad_h2.astype(bf)
    grad_hidden = nt(grad_mlp, w_down)
    grad_gate = (grad_hidden * upper * sigmoid * (1.0 + gate * (1.0 - sigmoid))).astype(bf)
    grad_up = (grad_hidden * activated).astype(bf)
    grad_first = grad_h2 + nt(grad_gate, w_gate) + nt(grad_up, w_up)
    grad_h1, gain_one, bias_one = norm_back(grad_first, normed_one, scale_one, ln1_gain)
    grad_branch = grad_h1.astype(bf)
    grad_attended = nt(w_out, grad_branch).astype(bf)
    gains = jnp.stack([gain_one, bias_one, gain_two, bias_two], 0)
    here_first = tower == 0
    by_hand = width % (16 * places) == 0
    if by_hand:
        half = width // 2
        own = lambda v: lax.dynamic_slice_in_dim(v, tower * half, half, 1)
        its = lambda v: lax.dynamic_slice_in_dim(v, (1 - tower) * half, half, 1)
        kept = jnp.where(here_first, grad_gate, grad_up)
        sent = jnp.where(here_first, grad_up, grad_gate)
        w_parts = weight_grads(
            places,
            inner, swapped(inner), kept, swapped(sent), hidden, swapped(hidden),
            own(grad_mlp), swapped(its(grad_mlp)), attended, swapped(attended),
            own(grad_branch), swapped(its(grad_branch)),
        )
    d_heads = tokens_to_heads(grad_attended, 5, "to_heads")
    mixed = attn_bwd(d_heads, exact, lse, qa, ka, va, kt, cos, sin, codes)
    if by_hand:
        one = width // places
        down = w_down.shape[0] // places
        pair, gain_sums = scatter(w_parts, jnp.concatenate([gains, jnp.zeros_like(gains)], 0), groups)
        top = pair.shape[1] - down - one
        unfold = lambda v: v.reshape(top // one, one, half).transpose(1, 0, 2).reshape(one, -1)
        sides = lambda v: jnp.concatenate([v[0], v[1]], 1).astype(f32)
        gate_out = unfold(pair[0, :top]).astype(f32)
        up_out = unfold(pair[1, :top]).astype(f32)
        down_out = sides(pair[:, top : top + down])
        out_out = sides(pair[:, top + down :])
        gains_out = lax.dynamic_slice_in_dim(gain_sums[:4], place * one, one, 1)
        grad_mixed, qkv_parts = tail(mixed, tok_all, groups)
        qkv_out = (
            qkv_parts.reshape(SPAN, one, 3, HW).transpose(1, 2, 0, 3).reshape(one, 3 * width).astype(f32)
        )
    else:
        grad_mixed = heads_to_tokens(mixed, 6, "to_tokens_back")
        qkv_out = spread_sum(tn(rows, grad_mixed.T))
        out_out = spread_sum(nn(attended, grad_branch))
        gate_out = spread_sum(tn(inner, grad_gate))
        up_out = spread_sum(tn(inner, grad_up))
        down_out = spread_sum(tn(hidden, grad_mlp))
        gains_out = spread_sum(gains.T).T
    token_grad = grad_h1 + lax.dot_general(
        grad_mixed, w_qkv, (((0,), (1,)), ((), ())), preferred_element_type=f32
    )
    return (
        scores, loss[0, 0], token_grad[None], qkv_out, out_out, gains_out[0], gains_out[1],
        gate_out, up_out, down_out, gains_out[2], gains_out[3],
    )


def solution(mesh):
    shard = P("dp", None)
    lone = P("dp")
    return jax.shard_map(
        local,
        mesh=mesh,
        in_specs=(P("tower", "dp", None), P("tower", "dp"), P("tower", "dp")) + (P(),) * 10,
        out_specs=(
            P(), P(), P("tower", "dp", None), shard, shard, lone, lone, shard, shard, shard, lone, lone,
        ),
        check_vma=False,
    )
```

time: 1410 us -> 382 us (0.27)
  waiting for transfers between devices: 919 us -> 0.02 us
  Pallas kernels: 0 us -> 277 us
  matrix products: 273 us -> 53.3 us
  local copies, waits for them, and re-layouts: 82.1 us -> 27.4 us
  blocking collectives: 43.6 us -> 0 us
  other arithmetic: 55.8 us -> 14 us
  between operations: 17.1 us -> 1.16 us
    reduce_scatter x4 -> x0, waiting for transfers between devices: 523 us -> none  [the longest x1 175 us: local(): lax.psum_scatter(terms[4], 'dp', scatter_dimension=0, tiled=True)]
    pallas_call x0 -> x9, Pallas kernels: none -> 277 us  [the longest x1 101 us: scatter(): pl.pallas_call(functools.partial(scatter_kernel, groups), out_shape=(jax....]
    unnamed x9 -> x0, waiting for transfers between devices: 242 us -> none
    dot_general x102 -> x9, matrix products: 269 us -> 47.2 us  [the longest x4 24 us: nt(): lax.dot_general(a, b, (((1,), (1,)), ((), ())), preferred_element_type=f32)]
    ppermute x10 -> x6, waiting for transfers between devices: 138 us -> 0.02 us  [swapped(): return lax.ppermute(value, 'tower', [(0, 1), (1, 0)])]
    all_gather x2 -> x0, blocking collectives: 39.1 us -> none  [the longest x1 27.2 us: local(): part_sums = lax.all_gather(sums, 'dp', axis=0, tiled=True)]
    psum x1 -> x0, waiting for transfers between devices: 16.2 us -> none  [local(): lax.psum(pieces[0].astype(jnp.bfloat16), 'tower').astype(jnp.float32)]
    while x27 -> x0, local copies, waits for them, and re-layouts: 15.8 us -> none  [the longest x3 15.8 us: local(): lax.map(attend_head, (query_heads, keys_heads, values_heads))]
  transfers between devices with their start and end apart: 17 -> 6, of which waited for: 12 -> 0; matrix products, arithmetic and copies ran while one was open for 18% -> 20% of each run, Pallas kernels for 0% -> 25%
where the time goes in v1:
time: 382 us
  Pallas kernels  277 us (73%)
  matrix products  53.3 us (14%)
  local copies, waits for them, and re-layouts  27.4 us (7%)
  other arithmetic  14 us (4%)
  starting transfers between devices  9.39 us (2%)
    pallas_call x1, Pallas kernels, scatter(): pl.pallas_call(functools.partial(scatter_kernel, groups), out_shape=(jax....  101 us
    pallas_call x1, Pallas kernels, tail(): pl.pallas_call(functools.partial(tail_kernel, groups), out_shape=(jax.Sha...  43.8 us
    pallas_call x1, Pallas kernels, gather(): pl.pallas_call(gather_kernel, out_shape=(jax.ShapeDtypeStruct((SPAN * cou...  29.4 us
    pallas_call x1, Pallas kernels, attn_bwd(): pl.pallas_call(functools.partial(bwd_kernel, KB, QB), out_shape=jax.Shape...  24.7 us
    dot_general x4, matrix products, nt(): lax.dot_general(a, b, (((1,), (1,)), ((), ())), preferred_element_type=f32)  24 us
    pallas_call x1, Pallas kernels, weight_grads(): pl.pallas_call(functools.partial(weights_kernel, shards), out_shape=jax.S...  23.2 us
    pallas_call x1, Pallas kernels, attn_fwd(): pl.pallas_call(functools.partial(fwd_kernel, KB, QB), out_shape=(jax.Shap...  20.7 us
    dot_general x3, matrix products, nn(): lax.dot_general(a, b, (((1,), (0,)), ((), ())), preferred_element_type=f32)  15.3 us
  transfers between devices with their start and end apart: 6, of which 0 were waited for; matrix products, arithmetic and copies ran while one was open for 20% of the time, Pallas kernels for 25%

profile of v1, /device:TPU:25, one launch (start us, length us, event | category | flops | bytes accessed | tf_op | source)
XLA Modules:
  0.0 382.4 jit_solution(173523614211377903)
XLA Ops:
  0.7 5.9 %copy.36 = bf16[768,2304]{0,1:T(8,128)(2,1)} copy(bf16[768,2304]{1,0:T(8,128)(2,1)} %param.19) | data formatting | bytes 7077888 | tf_op args[4]
  7.2 29.4 %gather.7 = (bf16[2048,768]{1,0:T(8,128)(2,1)}, f32[1,2048]{1,0:T(1,128)}) custom-call(bf16[512,768]{1,0:T(8,128)(2,1)} %bitcast.67, f32[1,512]{1,0:T(1,128)} %get-tuple-element.74.code_ref), custom_call_target="tpu_custom_call" | custom-call | tf_op jit(solution)/shard_map/gather/pallas_call | solution.py:136
  36.5 2.2 constant_dynamic-slice_fusion.5
  38.7 20.7 %attn_fwd.1 = (bf16[192,2048]{1,0:T(8,128)(2,1)}, f32[3,2048]{1,0:T(4,128)}, f32[192,2048]{1,0:T(8,128)}, bf16[3,128,2048]{2,1,0:T(8,128)(2,1)}, bf16[3,2048,128...) custom-call(bf16[2048,768]{1,0:T(8,128)(2,1)} %get-tuple-element.28.tok_ref, ...), custom_call_target="tpu_custom_call" | custom-call | flops 8254390272 | bytes 12582912 | tf_op jit(solution)/shard_map/attn_fwd/pallas_call | solution.py:399
  59.4 9.0 %to_tokens.1.aa = bf16[768,512]{1,0:T(8,128)(2,1)} custom-call(bf16[192,2048]{1,0:T(8,128)(2,1)} %get-tuple-element.30.in_ref), custom_call_target="tpu_custom_call" | custom-call | tf_op jit(solution)/shard_map/to_tokens/pallas_call | solution.py:185
  68.3 8.1 %collective-permute-start.4 = (bf16[768,512]{1,0:T(8,128)(2,1)}, bf16[768,512]{1,0:T(8,128)(2,1)}, u32[]{:S(2)}, u32[]{:S(2)}) collective-permute-start(bf16[768,512]{1,0:T(8,128)(2,1)} %to_tokens.1.aa), channel_id=1, source_target_pairs={{0,16},{16,0},{1,17},{17,1},{2,18},{18,2},{3,19},{19,3},{4,20},{20... | collective-permute-start | bytes 2359304 | tf_op jit(solution)/shard_map/ppermute | solution.py:874
  76.4 2.0 fusion.28
  79.6 5.0 %fusion.30 = f32[512,3072]{1,0:T(8,128)S(1)} fusion(bf16[512,768]{1,0:T(8,128)(2,1)S(1)} %fusion.4.ia, bf16[768,3072]{1,0:T(8,128)(2,1)} %param.23), kind=kOutput, calls=%fused_computation.97 | convolution fusion | flops 2415919104 | bytes 11796480 | tf_op jit(solution)/shard_map/dot_general | solution.py:29
  84.7 5.6 %multiply_convert_fusion.2 = (bf16[512,3072]{1,0:T(8,128)(2,1)}, f32[512,3072]{1,0:T(8,128)}) fusion(f32[512,3072]{1,0:T(8,128)S(1)} %fusion.30, bf16[512,768]{1,0:T(8,128)(2,1)S(1)} %fusion.4.ia, bf16[768,3072]{1,0:T(8,128)(2,1)S(1)} %bitcast.74), kind=kOutput, calls=%fused_computation.3 | convolution fusion | flops 2425356288 | bytes 21233664 | tf_op jit(solution)/shard_map/dot_general | solution.py:29
  91.6 4.7 %fusion.29 = (f32[512]{0:T(512)S(1)}, f32[512,768]{1,0:T(8,128)S(1)}) fusion(bf16[512,3072]{1,0:T(8,128)(2,1)} %get-tuple-element.77.ha, bf16[3072,768]{1,0:T(8,128)(2,1)S(1)} %bitcast.72, f32[768]{0:T(1024)S(1)} %copy-done.22, f32[768]{0:T(1024)S(1)} %copy-done.15, f32[512]{0:T(512)S(1)} %add_rsqrt_fusion.1, f32[512,768]{1,0:T(8,128)S(1)} %get-tuple-element.76, ...), kind=kOutput, calls=%fused_computation.96 | convolution fusion | flops 2418277888 | bytes 11022336 | tf_op jit(solution)/shard_map/dot_general | solution.py:29
  101.0 2.4 fusion.1.sums_ref
  104.1 13.5 %contrast.1 = (f32[8,768]{1,0:T(8,128)}, f32[32,32]{1,0:T(8,128)}, f32[8,128]{1,0:T(8,128)}) custom-call(f32[8,768]{1,0:T(8,128)} %fusion.1.sums_ref, f32[32,128]{1,0:T(8,128)} %broadcast_in_dim.9.goal_ref), custom_call_target="tpu_custom_call" | custom-call | tf_op jit(solution)/shard_map/contrast/pallas_call | solution.py:297
  117.6 3.8 %multiply_reduce_fusion = (f32[768]{0:T(1024)}, f32[512]{0:T(512)S(1)}, f32[512]{0:T(512)S(1)}, f32[768]{0:T(1024)}, f32[512,768]{1,0:T(8,128)S(1)}) fusion(f32[512,768]{1,0:T(8,128)} %copy-done.6, f32[512]{0:T(512)S(1)} %copy-done.18, f32[512]{0:T(512)S(1)} %broadcast_multiply_fusion.4, f32[768]{0:T(1024)} %param.26, f32[8,768]{1,0:T(8,128)} %get-tuple-element.33, ...), kind=kOutput, calls=%fused_computation.8 | convolution fusion | flops 41293312 | bytes 3190272 | tf_op jit(solution)/shard_map/dot_general | solution.py:948
  123.1 10.0 %broadcast_select_fusion = (bf16[512,3072]{1,0:T(8,128)(2,1)}, bf16[512,3072]{1,0:T(8,128)(2,1)}, bf16[512,3072]{1,0:T(8,128)(2,1)}) fusion(pred[]{:T(512)S(6)} %eq.45, f32[512,3072]{1,0:T(8,128)} %copy-done.5, f32[512,3072]{1,0:T(8,128)S(1)} %copy-done.29, bf16[512,768]{1,0:T(8,128)(2,1)S(1)} %get-tuple-element.57, bf16[3072,768]{1,0:T(8,128)(2,1)} %param.25), kind=kOutput, calls=%fused_computation.6 | convolution fusion | flops 2437939200 | bytes 27525120 | tf_op jit(solution)/shard_map/dot_general | solution.py:33
  134.6 6.1 %fusion.31 = f32[512,768]{1,0:T(8,128)S(1)} fusion(bf16[512,3072]{1,0:T(8,128)(2,1)} %get-tuple-element.54, bf16[768,3072]{1,0:T(8,128)(2,1)} %param.23), kind=kOutput, calls=%fused_computation.98 | convolution fusion | flops 2415919104 | bytes 9437184 | tf_op jit(solution)/shard_map/dot_general | solution.py:33
  140.7 6.1 %multiply_reduce_fusion.1 = (f32[768]{0:T(1024)}, f32[512]{0:T(512)S(1)}, f32[512]{0:T(512)S(1)}, f32[768]{0:T(1024)S(1)}, f32[512,768]{1,0:T(8,128)S(1)}) fusion(f32[512,768]{1,0:T(8,128)S(1)} %copy-done.3, f32[512]{0:T(512)S(1)} %add_rsqrt_fusion.1, f32[512]{0:T(512)S(1)} %broadcast_multiply_fusion.5, f32[768]{0:T(1024)S(1)} %copy-done.16, ...), kind=kOutput, calls=%fused_computation.9 | convolution fusion | flops 2420241920 | bytes 14173184 | tf_op jit(solution)/shard_map/dot_general | solution.py:33
  151.2 11.9 %to_heads.1.do_ref = bf16[192,2048]{1,0:T(8,128)(2,1)} custom-call(bf16[768,512]{1,0:T(8,128)(2,1)} %fusion.5.in_ref), custom_call_target="tpu_custom_call" | custom-call | tf_op jit(solution)/shard_map/to_heads/pallas_call | solution.py:224
  163.1 24.7 %attn_bwd.1.g_ref = bf16[576,2048]{1,0:T(8,128)(2,1)} custom-call(bf16[192,2048]{1,0:T(8,128)(2,1)} %to_heads.1.do_ref, f32[192,2048]{1,0:T(8,128)} %get-tuple-element.34.o32_ref, f32[3,2048]{1,0:T(4,128)} %get-tuple-element.35.lse_ref, bf16[3,128,2048]{2,1,0:T(8,128)(2,1)} %get-tuple-element.36.qa_ref, bf16[3,2048,128]{2,1,0:T(8,128)(2,1)} %get-tuple-element.37.ka_ref, ...), custom_call_target="tpu_custom_call" | custom-call | flops 16106127360 | bytes 12582912 | tf_op jit(solution)/shard_map/attn_bwd/pallas_call | solution.py:471
  187.8 3.9 %broadcast_select_fusion.1.ga = bf16[512,3072]{1,0:T(8,128)(2,1)} fusion(bf16[512,3072]{1,0:T(8,128)(2,1)} %get-tuple-element.54, bf16[512,3072]{1,0:T(8,128)(2,1)} %get-tuple-element.53, pred[]{:T(512)S(6)} %eq.45), kind=kLoop, calls=%fused_computation.7 | loop fusion | flops 1572864 | bytes 9437185 | tf_op jit(solution)/shard_map/jit(_where)/select_n | solution.py:965
  193.7 43.8 %tail.1 = (bf16[2304,512]{1,0:T(8,128)(2,1)}, bf16[4,48,576]{2,1,0:T(8,128)(2,1)}) custom-call(bf16[576,2048]{1,0:T(8,128)(2,1)} %attn_bwd.1.g_ref, bf16[2048,768]{1,0:T(8,128)(2,1)} %get-tuple-element.28.tok_ref), custom_call_target="tpu_custom_call" | custom-call | tf_op jit(solution)/shard_map/tail/pallas_call | solution.py:854
  240.1 2.2 reshape.209
  244.5 5.9 %add_bitcast_fusion = f32[1,512,768]{2,1,0:T(8,128)} fusion(f32[512,768]{1,0:T(8,128)S(1)} %copy-done.11, bf16[2304,512]{1,0:T(8,128)(2,1)} %get-tuple-element.40, bf16[768,2304]{1,0:T(8,128)(2,1)} %param.19), kind=kOutput, calls=%fused_computation.10 | convolution fusion | flops 1812332544 | bytes 9043968 | tf_op jit(solution)/shard_map/dot_general | solution.py:999
  251.2 23.2 %weight_grads.1.w_ref = bf16[16,624,384]{2,1,0:T(8,128)(2,1)} custom-call(bf16[512,768]{1,0:T(8,128)(2,1)} %copy-done.4, bf16[512,768]{1,0:T(8,128)(2,1)} %collective-permute-done.ib, bf16[512,3072]{1,0:T(8,128)(2,1)} %broadcast_select_fusion.1.ga, bf16[512,3072]{1,0:T(8,128)(2,1)} %collective-permute-done.1.gb, bf16[512,3072]{1,0:T(8,128)(2,1)} %get-tuple-element.77.ha, ...), custom_call_target="tpu_custom_call" | custom-call | tf_op jit(solution)/shard_map/weight_grads/pallas_call | solution.py:521
  274.4 101.1 %scatter.1 = (bf16[2,624,384]{2,1,0:T(8,128)(2,1)}, f32[8,768]{1,0:T(8,128)}) custom-call(bf16[16,624,384]{2,1,0:T(8,128)(2,1)} %weight_grads.1.w_ref, f32[8,768]{1,0:T(8,128)} %concatenate.9.gain_ref), custom_call_target="tpu_custom_call" | custom-call | tf_op jit(solution)/shard_map/scatter/pallas_call | solution.py:735
  (128 shorter events, 30.3 us)
Async XLA Ops:
  0.6 75.7 %copy-start = (bf16[768,768]{1,0:T(8,128)(2,1)S(1)}, bf16[768,768]{1,0:T(8,128)(2,1)}, u32[]{:S(2)}) copy-start(bf16[768,768]{1,0:T(8,128)(2,1)} %param.20) | copy-start | bytes 3538948
  0.7 5.9 %copy-start.19 = (s32[1,512]{1,0:T(1,128)S(1)}, s32[1,512]{1,0:T(1,128)}, u32[]{:S(2)}) copy-start(s32[1,512]{1,0:T(1,128)} %param.17) | copy-start | bytes 6148
  0.7 5.9 %copy-start.27 = (s32[1,512]{1,0:T(1,128)S(1)}, s32[1,512]{1,0:T(1,128)}, u32[]{:S(2)}) copy-start(s32[1,512]{1,0:T(1,128)} %param.16) | copy-start | bytes 6148
  59.4 17.0 %copy-start.13 = (bf16[1,512,768]{2,1,0:T(8,128)(2,1)S(1)}, bf16[1,512,768]{2,1,0:T(8,128)(2,1)}, u32[]{:S(2)}) copy-start(bf16[1,512,768]{2,1,0:T(8,128)(2,1)} %param.15) | copy-start | bytes 2359300
  68.3 182.8 %collective-permute-start.4 = (bf16[768,512]{1,0:T(8,128)(2,1)}, bf16[768,512]{1,0:T(8,128)(2,1)}, u32[]{:S(2)}, u32[]{:S(2)}) collective-permute-start(bf16[768,512]{1,0:T(8,128)(2,1)} %to_tokens.1.aa), channel_id=1, source_target_pairs={{0,16},{16,0},{1,17},{17,1},{2,18},{18,2},{3,19},{19,3},{4,20},{20... | collective-permute-start | bytes 2359304 | tf_op jit(solution)/shard_map/ppermute | solution.py:874
  78.4 13.1 %copy-start.2 = (f32[512,768]{1,0:T(8,128)}, f32[512,768]{1,0:T(8,128)S(1)}, u32[]{:S(2)}) copy-start(f32[512,768]{1,0:T(8,128)S(1)} %get-tuple-element.76) | copy-start | bytes 4718596
  79.2 5.4 %slice-start.2 = ((s8[4718592]{0:T(1024)(128)(4,1)}), s8[4194304]{0:T(1024)(128)(4,1)S(1)}, s32[]{:S(2)}) async-start(s8[4718592]{0:T(1024)(128)(4,1)} %bitcast.73), calls=%async_computation.2 | async-start | bytes 8388608
  79.5 5.1 %slice-start.3 = ((s8[4718592]{0:T(1024)(128)(4,1)}), s8[524288]{0:T(1024)(128)(4,1)S(1)}, s32[]{:S(2)}) async-start(s8[4718592]{0:T(1024)(128)(4,1)} %bitcast.73), calls=%async_computation.3 | async-start | bytes 1048576
  79.5 170.9 %collective-permute-start = (bf16[512,768]{1,0:T(8,128)(2,1)S(1)}, bf16[512,768]{1,0:T(8,128)(2,1)}, u32[]{:S(2)}, u32[]{:S(2)}) collective-permute-start(bf16[512,768]{1,0:T(8,128)(2,1)S(1)} %fusion.4.ia), channel_id=1, source_target_pairs={{0,16},{16,0},{1,17},{17,1},{2,18},{18,2},{3,19},{19,3},{4,20},{20... | collective-permute-start | bytes 2359304 | tf_op jit(solution)/shard_map/ppermute | solution.py:874
  79.6 11.9 %slice-start = ((s8[4718592]{0:T(1024)(128)(4,1)}), s8[4194304]{0:T(1024)(128)(4,1)S(1)}, s32[]{:S(2)}) async-start(s8[4718592]{0:T(1024)(128)(4,1)} %bitcast.71), calls=%async_computation | async-start | bytes 8388608
  84.6 5.7 %copy-start.5 = (f32[512,3072]{1,0:T(8,128)}, f32[512,3072]{1,0:T(8,128)S(1)}, u32[]{:S(2)}) copy-start(f32[512,3072]{1,0:T(8,128)S(1)} %fusion.30) | copy-start | bytes 18874372
  84.6 6.9 %slice-start.1 = ((s8[4718592]{0:T(1024)(128)(4,1)}), s8[524288]{0:T(1024)(128)(4,1)S(1)}, s32[]{:S(2)}) async-start(s8[4718592]{0:T(1024)(128)(4,1)} %bitcast.71), calls=%async_computation.1 | async-start | bytes 1048576
  90.3 160.9 %collective-permute-start.2 = (bf16[512,3072]{1,0:T(8,128)(2,1)}, bf16[512,3072]{1,0:T(8,128)(2,1)}, u32[]{:S(2)}, u32[]{:S(2)}) collective-permute-start(bf16[512,3072]{1,0:T(8,128)(2,1)} %get-tuple-element.77.ha), channel_id=1, source_target_pairs={{0,16},{16,0},{1,17},{17,1},{2,18},{18,2},{3,19},{19,3},{4,20},{20... | collective-permute-start | bytes 9437192 | tf_op jit(solution)/shard_map/ppermute | solution.py:874
  96.2 7.2 %copy-start.6 = (f32[512,768]{1,0:T(8,128)}, f32[512,768]{1,0:T(8,128)S(1)}, u32[]{:S(2)}) copy-start(f32[512,768]{1,0:T(8,128)S(1)} %get-tuple-element.80) | copy-start | bytes 4718596
  99.8 17.7 %copy-start.18 = (f32[512]{0:T(512)S(1)}, f32[512]{0:T(512)}, u32[]{:S(2)}) copy-start(f32[512]{0:T(512)} %add_rsqrt_fusion) | copy-start | bytes 6148
  117.6 5.5 %copy-start.29 = (f32[512,3072]{1,0:T(8,128)S(1)}, f32[512,3072]{1,0:T(8,128)}, u32[]{:S(2)}) copy-start(f32[512,3072]{1,0:T(8,128)} %get-tuple-element.78) | copy-start | bytes 18874372
  133.1 118.1 %collective-permute-start.1 = (bf16[512,3072]{1,0:T(8,128)(2,1)}, bf16[512,3072]{1,0:T(8,128)(2,1)}, u32[]{:S(2)}, u32[]{:S(2)}) collective-permute-start(bf16[512,3072]{1,0:T(8,128)(2,1)} %get-tuple-element.52), channel_id=1, source_target_pairs={{0,16},{16,0},{1,17},{17,1},{2,18},{18,2},{3,19},{19,3},{4,20},{20... | collective-permute-start | bytes 9437192 | tf_op jit(solution)/shard_map/ppermute | solution.py:874
  134.2 109.6 %collective-permute-start.3 = (bf16[512,384]{1,0:T(8,128)(2,1)}, bf16[512,384]{1,0:T(8,128)(2,1)}, u32[]{:S(2)}, u32[]{:S(2)}) collective-permute-start(bf16[512,384]{1,0:T(8,128)(2,1)} %get-tuple-element.67), channel_id=1, source_target_pairs={{0,16},{16,0},{1,17},{17,1},{2,18},{18,2},{3,19},{19,3},{4,20},{20... | collective-permute-start | bytes 1179656 | tf_op jit(solution)/shard_map/ppermute | solution.py:874
  134.6 6.1 %copy-start.3 = (f32[512,768]{1,0:T(8,128)S(1)}, f32[512,768]{1,0:T(8,128)}, u32[]{:S(2)}) copy-start(f32[512,768]{1,0:T(8,128)} %copy-done.2) | copy-start | bytes 4718596
  134.6 6.1 %copy-start.10 = (bf16[512,3072]{1,0:T(8,128)(2,1)S(1)}, bf16[512,3072]{1,0:T(8,128)(2,1)}, u32[]{:S(2)}) copy-start(bf16[512,3072]{1,0:T(8,128)(2,1)} %get-tuple-element.53) | copy-start | bytes 9437188
  134.6 6.1 %copy-start.12 = (f32[512,768]{1,0:T(8,128)S(1)}, f32[512,768]{1,0:T(8,128)}, u32[]{:S(2)}) copy-start(f32[512,768]{1,0:T(8,128)} %get-tuple-element.58) | copy-start | bytes 4718596
  134.6 6.1 %copy-start.16 = (f32[768]{0:T(1024)S(1)}, f32[768]{0:T(1024)}, u32[]{:S(2)}) copy-start(f32[768]{0:T(1024)} %param.21) | copy-start | bytes 9220
  237.5 5.5 %copy-start.9 = (bf16[512,768]{1,0:T(8,128)(2,1)S(1)}, bf16[512,768]{1,0:T(8,128)(2,1)}, u32[]{:S(2)}) copy-start(bf16[512,768]{1,0:T(8,128)(2,1)} %copy-done.8) | copy-start | bytes 2359300
  243.8 6.6 %collective-permute-start.5 = (bf16[512,384]{1,0:T(8,128)(2,1)S(1)}, bf16[512,384]{1,0:T(8,128)(2,1)S(1)}, u32[]{:S(2)}, u32[]{:S(2)}) collective-permute-start(bf16[512,384]{1,0:T(8,128)(2,1)S(1)} %get-tuple-element.65), channel_id=1, source_target_pairs={{0,16},{16,0},{1,17},{17,1},{2,18},{18,2},{3,19},{19,3},{4,20},{20... | collective-permute-start | bytes 1179656 | tf_op jit(solution)/shard_map/ppermute | solution.py:874
  (16 other events, 44.4 us)

commit v2 on v1

--- a/solution.py
+++ b/solution.py
@@ -478,55 +478,148 @@
 
 
 def weights_kernel(
-    shards, ia, ib, ga, gb, ha, hb, ma, mb, aa, ab, ba, bb, out_ref, it_ref
+    groups, ia, ib, ga, gb, ha, hb, ma, mb, aa, ab, ba, bb, in_ref,
+    sa_ref, ka_ref, sb_ref, kb_ref, heads_ref,
+    iv, it, gv, hv, mv, av, bv, gs, ds, os, isem, osem, send, recv, lsem,
 ):
-    width = ia.shape[1]
+    t, p, x, y, g = here()
+    peers = plane_peers()
+    greet(peers)
+    tokens = in_ref.shape[1]
+    me = lax.rem(p, SPAN)
+    mine = pl.ds(pl.multiple_of(me * tokens, tokens), tokens)
+    moves = []
+    for i, peer in enumerate((peers[2], peers[0], peers[1])):
+        m = lax.rem(peer[1], SPAN)
+        moves.append(remote(
+            in_ref.at[pl.ds(pl.multiple_of(m * HW, HW), HW)], heads_ref.at[:, mine],
+            send.at[i], recv.at[i], peer,
+        ))
+    moves.append(pltpu.make_async_copy(
+        in_ref.at[pl.ds(pl.multiple_of(me * HW, HW), HW)], heads_ref.at[:, mine], lsem.at[0]
+    ))
+    for c in moves:
+        c.start()
+    count, width = ia.shape
     half = width // 2
+    tiles = gv.shape[1]
+    shards = SPAN * groups
     one = width // shards
-    steps = ga.shape[1] // half
     down = ha.shape[1] // shards
-    count = ia.shape[0]
-    it_ref[:, :count] = ia[...].T
-    it_ref[:, count:] = ib[...].T
+
+    def load(i, src, dst):
+        return pltpu.make_async_copy(src, dst, isem.at[i])
+
+    def tile(pair, j, buf, base):
+        cols = pl.ds(pl.multiple_of(j * half, half), half)
+        return [load(base + i * tiles + j, a.at[:, cols], buf.at[i, j]) for i, a in enumerate(pair)]
+
+    few = [(ma, mv.at[0]), (mb, mv.at[1]), (aa, av.at[0]), (ab, av.at[1]),
+           (ba, bv.at[0]), (bb, bv.at[1]), (ia, iv.at[0]), (ib, iv.at[1])]
+    few = [load(i, a, b) for i, (a, b) in enumerate(few)]
+    for c in few[:2]:
+        c.start()
+    for j in range(tiles):
+        for c in tile((ha, hb), j, hv, 8):
+            c.start()
+    for c in few[2:]:
+        c.start()
+    for j in range(tiles):
+        for c in tile((ga, gb), j, gv, 8 + 2 * tiles):
+            c.start()
+    for c in few[:2]:
+        c.wait()
+
+    def downward(j, _):
+        for c in tile((ha, hb), j, hv, 8):
+            c.wait()
+        r = tn(hv[0, j], mv[0]) + tn(hv[1, j], mv[1])
+        ds[pl.ds(j * (half // down), half // down)] = r.astype(bf).reshape(half // down, down, half)
+        return 0
+
+    lax.fori_loop(0, tiles, downward, 0)
+    for c in few[2:]:
+        c.wait()
+    r = nn(av[0], bv[0]) + nn(av[1], bv[1])
+    os[...] = r.astype(bf).reshape(shards, one, half)
+    for i in range(2):
+        it[:, i * count : (i + 1) * count] = iv[i].T
+    fours = lambda ref, n: ref.reshape(groups, 2, 2, n, half)
+
+    def put(i, src, dst):
+        return pltpu.make_async_copy(src, dst, osem.at[i])
+
+    last = (tiles - 1) * one
+    outs = []
+    for i, (ref, k) in enumerate(((sb_ref, 1 - y), (kb_ref, y))):
+        outs.append(put(4 * i, fours(ds, down).at[:, k], ref.at[:, :, pl.ds(one, down)]))
+        outs.append(put(4 * i + 1, fours(os, one).at[:, k], ref.at[:, :, pl.ds(one + down, one)]))
+    for c in outs:
+        c.start()
 
     def upward(j, _):
-        cols = pl.ds(pl.multiple_of(j * half, half), half)
-        r = nn(it_ref[:, :count], ga[:, cols]) + nn(it_ref[:, count:], gb[:, cols])
-        out_ref[:, pl.ds(pl.multiple_of(j * one, one), one), :] = r.astype(bf).reshape(
-            shards, one, half
-        )
+        for c in tile((ga, gb), j, gv, 8 + 2 * tiles):
+            c.wait()
+        r = nn(it[:, :count], gv[0, j]) + nn(it[:, count:], gv[1, j])
+        gs[j] = r.astype(bf).reshape(shards, one, half)
         return 0
 
-    lax.fori_loop(0, steps, upward, 0)
-    top = steps * one
-    per = half // down
-
-    def downward(j, _):
-        cols = pl.ds(pl.multiple_of(j * half, half), half)
-        r = tn(ha[:, cols], ma[...]) + tn(hb[:, cols], mb[...])
-        out_ref[pl.ds(j * per, per), top : top + down, :] = r.astype(bf).reshape(per, down, half)
+    def upper(j, _):
+        upward(j, 0)
+        rows = pl.ds(pl.multiple_of(j * one, one), one)
+        piece = fours(gs.at[j], one)
+        put(8 + j, piece.at[:, :, 1 - x], sa_ref.at[:, :, rows]).start()
+        put(8 + tiles + j, piece.at[:, :, x], ka_ref.at[:, :, rows]).start()
         return 0
 
-    lax.fori_loop(0, ha.shape[1] // half, downward, 0)
-    r = nn(aa[...], ba[...]) + nn(ab[...], bb[...])
-    out_ref[:, top + down :, :] = r.astype(bf).reshape(shards, one, half)
-
-
-def weight_grads(shards, *arrays):
-    width = arrays[0].shape[1]
-    count = arrays[0].shape[0]
+    lax.fori_loop(0, tiles - 1, upper, 0)
+    upward(tiles - 1, 0)
+    piece = fours(gs.at[tiles - 1], one)
+    for i, (ref, k) in enumerate(((sb_ref, 1 - y), (kb_ref, y))):
+        c = put(4 * i + 2, piece.at[:, k], ref.at[:, :, pl.ds(0, one)])
+        c.start()
+        outs.append(c)
+
+    def landed(j, _):
+        rows = pl.ds(pl.multiple_of(j * one, one), one)
+        put(8 + j, fours(gs.at[j], one).at[:, :, 0], sa_ref.at[:, :, rows]).wait()
+        put(8 + tiles + j, fours(gs.at[j], one).at[:, :, 0], ka_ref.at[:, :, rows]).wait()
+        return 0
+
+    lax.fori_loop(0, tiles - 1, landed, 0)
+    for c in outs + moves:
+        c.wait()
+
+
+def weight_grads(groups, grad_heads, *arrays):
+    count, width = arrays[0].shape
     half = width // 2
+    shards = SPAN * groups
     one = width // shards
-    rows = one * (arrays[2].shape[1] // half) + arrays[4].shape[1] // shards + one
+    tiles = arrays[2].shape[1] // half
+    down = arrays[4].shape[1] // shards
+    ra = (tiles - 1) * one
+    rb = down + 2 * one
+    part = lambda r: jax.ShapeDtypeStruct((groups, 2, r, half), bf)
+    vm = lambda *n: pltpu.VMEM(n, bf)
     return pl.pallas_call(
-        functools.partial(weights_kernel, shards),
-        out_shape=jax.ShapeDtypeStruct((shards, rows, half), bf),
-        in_specs=[VM] * 12,
-        out_specs=VM,
-        scratch_shapes=[pltpu.VMEM((width, 2 * count), bf)],
-        compiler_params=pltpu.CompilerParams(vmem_limit_bytes=VLIM),
+        functools.partial(weights_kernel, groups),
+        out_shape=(
+            part(ra), part(ra), part(rb), part(rb),
+            jax.ShapeDtypeStruct((HW, SPAN * grad_heads.shape[1]), bf),
+        ),
+        in_specs=[ANY] * 12 + [VM],
+        out_specs=(ANY,) * 5,
+        scratch_shapes=[
+            vm(2, count, width), vm(width, 2 * count), vm(2, tiles, count, half), vm(2, tiles, count, half),
+            vm(2, count, half), vm(2, width, count), vm(2, count, half),
+            vm(tiles, shards, one, half), vm(shards, down, half), vm(shards, one, half),
+            dma_sems(8 + 4 * tiles), dma_sems(8 + 2 * tiles), dma_sems(3), dma_sems(3), dma_sems(1),
+        ],
+        compiler_params=comm_params(2),
         name="weight_grads",
-    )(*arrays)
+        cost_estimate=pl.CostEstimate(flops=int(2 * 2 * count * half * width * 8.5), bytes_accessed=30 << 20, transcendentals=0),
+    )(*arrays, grad_heads)
 
 
 def add_rows(dst, a, b, rows):
@@ -545,27 +638,27 @@
         us, ur, ds, dr = sems
         above = (t, lax.rem(p + SPAN, SPAN * groups))
         below = (t, lax.rem(p + SPAN * (groups - 1), SPAN * groups))
-        self.up_first = remote(part, up, us, ur, above)
-        self.up_next = remote(up, up, us, ur, above)
-        self.down_first = remote(part, down, ds, dr, below)
-        self.down_next = remote(down, down, ds, dr, below)
+        self.up_first = lambda: remote(part, up, us, ur, above)
+        self.up_next = lambda: remote(up, up, us, ur, above)
+        self.down_first = lambda: remote(part, down, ds, dr, below)
+        self.down_next = lambda: remote(down, down, ds, dr, below)
 
     def start(self):
         if self.zt > 0:
-            pl.when(self.z == 0)(lambda: self.up_first.start())
+            pl.when(self.z == 0)(lambda: self.up_first().start())
         if self.zt < self.groups - 1:
-            pl.when(self.z == self.groups - 1)(lambda: self.down_first.start())
+            pl.when(self.z == self.groups - 1)(lambda: self.down_first().start())
 
     def relay(self, hop, rows):
         def up():
-            self.up_next.wait_recv()
+            self.up_next().wait_recv()
             add_rows(self.up, self.up, self.part, rows)
-            self.up_next.start()
+            self.up_next().start()
 
         def down():
-            self.down_next.wait_recv()
+            self.down_next().wait_recv()
             add_rows(self.down, self.down, self.part, rows)
-            self.down_next.start()
+            self.down_next().start()
 
         if 0 < hop < self.zt:
             pl.when(self.z == hop)(up)
@@ -575,9 +668,9 @@
     def finish(self, dst, rows):
         def done():
             if self.zt > 0:
-                self.up_next.wait_recv()
+                self.up_next().wait_recv()
             if self.zt < self.groups - 1:
-                self.down_next.wait_recv()
+                self.down_next().wait_recv()
             if 0 < self.zt < self.groups - 1:
                 add_rows(self.up, self.up, self.down, rows)
             add_rows(dst, self.up if self.zt > 0 else self.down, self.part, rows)
@@ -586,9 +679,9 @@
 
     def drain(self):
         if self.zt > 0:
-            pl.when(self.z < self.zt)(lambda: self.up_first.wait_send())
+            pl.when(self.z < self.zt)(lambda: self.up_first().wait_send())
         if self.zt < self.groups - 1:
-            pl.when(self.z > self.zt)(lambda: self.down_first.wait_send())
+            pl.when(self.z > self.zt)(lambda: self.down_first().wait_send())
 
 
 def outward(groups):
@@ -602,272 +695,233 @@
     return order
 
 
-def scatter_kernel(groups, w_ref, gain_ref, out_ref, sum_ref, r1a, r1b, r2a, r2b, ua, ub, da, db,
-                   s1, q1, s2, q2, us, ur, ds, dr, plane, line, gs, gr, fs, fr):
+def finish_kernel(
+    groups, ka_ref, kb_ref, ra_ref, rb_ref, g_ref, tok_ref, gain_ref,
+    pair_ref, sum_ref, gm_ref, out_ref,
+    kva, kvb, rva, rvb, r2a, r2b, ua, ub, da, db, isem, s2, q2, us, ur, ds, dr,
+    plane, line, gs, gr, fs, fr,
+    w2, sib, ub2, db2, fin, send, recv, ts, tr, us2, ur2, ds2, dr2, ps, pr, lsem,
+):
     t, p, x, y, z = here()
     ex, ey, ed = plane_peers()
+    peers = (ex, ey, ed)
     sibling = (1 - t, p)
     others = [(t, lax.rem(p + SPAN * k, SPAN * groups)) for k in range(1, groups)]
-    greet((ex, ey, ed, sibling) + tuple(others))
-    rows = w_ref.shape[1]
-    ra = r1a.shape[1]
-    rb = rows - ra
+    across = tuple((1 - t, q[1]) for q in peers)
     order = outward(groups)
     colours = (
-        (ex, ey, r1a, r2a, ua, da, pl.ds(0, ra), ra,
-         lambda zt, k: zt * 4 + k * 2 + (1 - x), lambda zt, k: zt * 4 + k * 2 + x, y),
-        (ey, ex, r1b, r2b, ub, db, pl.ds(ra, rb), rb,
-         lambda zt, k: zt * 4 + (1 - y) * 2 + k, lambda zt, k: zt * 4 + y * 2 + k, x),
+        (ey, ka_ref, ra_ref, kva, rva, r2a, ua, da, y),
+        (ex, kb_ref, rb_ref, kvb, rvb, r2b, ub, db, x),
     )
 
-    def first(c, zt, k):
-        one, two, r1, r2, u, d, sl, n, away, own, mine = colours[c]
-        i = (c * groups + zt) * 2 + k
-        return remote(w_ref.at[away(zt, k), sl], r1.at[zt * 2 + k], s1.at[i], q1.at[i], one)
+    def loads(c, zt):
+        peer, kr, rr, kv, rv = colours[c][:5]
+        i = 2 * (c * groups + zt)
+        return (
+            pltpu.make_async_copy(kr.at[zt], kv.at[zt], isem.at[i]),
+            pltpu.make_async_copy(rr.at[zt], rv.at[zt], isem.at[i + 1]),
+        )
+
+    for zt in order:
+        for c in range(2):
+            for d in loads(c, zt):
+                d.start()
+    greet(peers + across + (sibling,) + tuple(others))
+    for i, peer in enumerate(peers):
+        remote(gain_ref, plane.at[i], gs.at[i], gr.at[i], peer).start()
 
     def second(c, zt):
-        one, two, r1, r2, u, d, sl, n, away, own, mine = colours[c]
+        peer, kr, rr, kv, rv, r2, u, d, mine = colours[c]
         i = c * groups + zt
-        return remote(r1.at[zt * 2 + 1 - mine], r2.at[zt], s2.at[i], q2.at[i], two)
+        return remote(rv.at[zt, 1 - mine], r2.at[zt], s2.at[i], q2.at[i], peer)
 
     def chain(c, zt):
-        one, two, r1, r2, u, d, sl, n, away, own, mine = colours[c]
+        peer, kr, rr, kv, rv, r2, u, d, mine = colours[c]
         i = c * groups + zt
         return Line(z, zt, groups, r2.at[zt], u.at[zt], d.at[zt],
                     (us.at[i], ur.at[i], ds.at[i], dr.at[i]), t, p)
 
-    def issue(zt):
-        for k in range(2):
-            for c in range(2):
-                first(c, zt, k).start()
-
-    def half_way(zt):
-        for k in range(2):
-            for c in range(2):
-                one, two, r1, r2, u, d, sl, n, away, own, mine = colours[c]
-                first(c, zt, k).wait_recv()
-                dst = r1.at[zt * 2 + k]
-                add_rows(dst, dst, w_ref.at[own(zt, k), sl], n)
-        for c in range(2):
-            second(c, zt).start()
-
-    def in_plane(zt):
-        for c in range(2):
-            one, two, r1, r2, u, d, sl, n, away, own, mine = colours[c]
-            second(c, zt).wait_recv()
-            dst = r2.at[zt]
-            add_rows(dst, dst, r1.at[zt * 2 + mine], n)
-            chain(c, zt).start()
-
-    def relay(zt, hop):
-        for c in range(2):
-            chain(c, zt).relay(hop, colours[c][7])
-
-    issue(order[0])
-    if groups > 1:
-        issue(order[1])
-    gain_copies = []
-    for i, peer in enumerate((ex, ey, ed)):
-        c = remote(gain_ref, plane.at[i], gs.at[i], gr.at[i], peer)
-        c.start()
-        gain_copies.append(c)
-    todo = []
-    for i, zt in enumerate(order):
-        half_way(zt)
-        if i + 2 < groups:
-            issue(order[i + 2])
-        if i >= 1:
-            in_plane(order[i - 1])
-            todo.append((order[i - 1], 0))
-        if i == 0:
-            for c in gain_copies:
-                c.wait()
-            sum_ref[...] = gain_ref[...] + plane[0]
-            sum_ref[...] = sum_ref[...] + (plane[1] + plane[2])
-            line[0] = sum_ref[...]
-            gain_copies = []
-            for k, peer in enumerate(others):
-                c = remote(line.at[0], line.at[1 + k], gs.at[3 + k], gr.at[3 + k], peer)
-                c.start()
-                gain_copies.append(c)
-        if i == 1:
-            for c in gain_copies:
-                c.wait()
-            total = line[0]
-            for k in range(1, groups):
-                total = total + line[k]
-            line[groups] = total
-            c = remote(line.at[groups], line.at[groups + 1], gs.at[2 + groups], gr.at[2 + groups], sibling)
-            c.start()
-            gain_copies = [c]
-        if i >= 2:
-            for hop in range(1, groups - 1):
-                if hop == 1:
-                    relay(order[i - 2], hop)
-    in_plane(order[groups - 1])
-    for hop in range(1, groups - 1):
-        for i, zt in enumerate(order):
-            if hop > 1 or i >= groups - 2:
-                relay(zt, hop)
+    def size(c):
+        return colours[c][3].shape[2]
+
     for zt in order:
         for c in range(2):
-            sl, n = colours[c][6], colours[c][7]
-            chain(c, zt).finish(out_ref.at[t, sl], n)
-    last = remote(out_ref.at[t], out_ref.at[t], fs.at[0], fr.at[0], sibling)
-    last.start()
-    for c in gain_copies:
-        c.wait()
-    sum_ref[...] = line[groups] + line[groups + 1]
-    for zt in order:
-        for c in range(2):
-            for k in range(2):
-                first(c, zt, k).wait_send()
-            second(c, zt).wait_send()
-            chain(c, zt).drain()
-    last.wait()
-
-
-def scatter(w, gains, groups):
-    rows, half = w.shape[1:]
-    ra = (rows // 32 + 1) * 16 if rows % 32 else rows // 2
-    rb = rows - ra
-    buf = lambda n, r: pltpu.VMEM((n, r, half), bf)
-    return pl.pallas_call(
-        functools.partial(scatter_kernel, groups),
-        out_shape=(
-            jax.ShapeDtypeStruct((2, rows, half), bf),
-            jax.ShapeDtypeStruct(gains.shape, f32),
-        ),
-        in_specs=[VM, VM],
-        out_specs=(VM, VM),
-        scratch_shapes=[
-            buf(2 * groups, ra), buf(2 * groups, rb), buf(groups, ra), buf(groups, rb),
-            buf(groups, ra), buf(groups, rb), buf(groups, ra), buf(groups, rb),
-            dma_sems(4 * groups), dma_sems(4 * groups), dma_sems(2 * groups), dma_sems(2 * groups),
-            dma_sems(2 * groups), dma_sems(2 * groups), dma_sems(2 * groups), dma_sems(2 * groups),
-            pltpu.VMEM((3,) + gains.shape, f32), pltpu.VMEM((groups + 2,) + gains.shape, f32),
-            dma_sems(3 + groups), dma_sems(3 + groups), dma_sems(1), dma_sems(1),
-        ],
-        compiler_params=comm_params(2),
-        name="scatter",
-    )(w, gains)
-
-
-def tail_kernel(groups, g_ref, tok_ref, gm_ref, out_ref, w2, sib, ub, db, fin, send, recv, ts, tr,
-                us, ur, ds, dr, ps, pr, lsem):
-    t, p, x, y, z = here()
+            for d in loads(c, zt):
+                d.wait()
+            peer, kr, rr, kv, rv, r2, u, d, mine = colours[c]
+            away = rv.at[zt, 1 - mine]
+            add_rows(away, away, kv.at[zt, 1 - mine], size(c))
+            second(c, zt).start()
     count = gm_ref.shape[1]
     me = lax.rem(p, SPAN)
-    peers = plane_peers()
-    sibling = (1 - t, p)
-    others = [(t, lax.rem(p + SPAN * k, SPAN * groups)) for k in range(1, groups)]
-    across = [(1 - t, q[1]) for q in peers]
-    greet(tuple(peers) + tuple(across) + (sibling,) + tuple(others))
     width = gm_ref.shape[0] // 3
     copies = []
     for i, peer in enumerate((peers[2], peers[0], peers[1])):
         m = lax.rem(peer[1], SPAN)
         for k in range(3):
-            c = remote(
+            copies.append(remote(
                 g_ref.at[pl.ds(k * HW, HW), pl.ds(pl.multiple_of(m * count, count), count)],
                 gm_ref.at[pl.ds(pl.multiple_of(k * width + me * HW, HW), HW)],
                 send.at[i * 3 + k], recv.at[i * 3 + k], peer,
-            )
-            c.start()
-            copies.append(c)
+            ))
     for k in range(3):
-        c = pltpu.make_async_copy(
+        copies.append(pltpu.make_async_copy(
             g_ref.at[pl.ds(k * HW, HW), pl.ds(pl.multiple_of(me * count, count), count)],
             gm_ref.at[pl.ds(pl.multiple_of(k * width + me * HW, HW), HW)],
             lsem.at[k],
-        )
-        c.start()
-        copies.append(c)
+        ))
+    for c in copies:
+        c.start()
+    for zt in order:
+        for c in range(2):
+            peer, kr, rr, kv, rv, r2, u, d, mine = colours[c]
+            keep = rv.at[zt, mine]
+            add_rows(keep, keep, kv.at[zt, mine], size(c))
+    for i, peer in enumerate(peers):
+        remote(gain_ref, plane.at[i], gs.at[i], gr.at[i], peer).wait()
+    line[0] = (gain_ref[...] + plane[0]) + (plane[1] + plane[2])
+    ring = [remote(line.at[0], line.at[1 + k], gs.at[3 + k], gr.at[3 + k], peer) for k, peer in enumerate(others)]
+    for c in ring:
+        c.start()
+
+    def in_plane(zt):
+        for c in range(2):
+            peer, kr, rr, kv, rv, r2, u, d, mine = colours[c]
+            second(c, zt).wait_recv()
+            dst = r2.at[zt]
+            add_rows(dst, dst, rv.at[zt, mine], size(c))
+            chain(c, zt).start()
+
+    def relay(zt, hop):
+        for c in range(2):
+            chain(c, zt).relay(hop, size(c))
+
+    in_plane(order[0])
     shards = SPAN * groups
     one = width // shards
     half = width // 2
     for h in range(2):
         r = nn(g_ref[...], tok_ref[:, h * half : (h + 1) * half]).T
         w2[h * (shards // 2) : (h + 1) * (shards // 2)] = r.astype(bf).reshape(shards // 2, one, 3 * HW)
-    swaps = []
-    for zt in outward(groups):
-        c = remote(w2.at[pl.ds(zt * 4 + (1 - t) * 2, 2)], sib.at[zt], ts.at[zt], tr.at[zt], sibling)
-        c.start()
-        swaps.append(c)
-
-    def chain(zt, k):
+
+    def swap(zt):
+        return remote(w2.at[pl.ds(zt * 4 + (1 - t) * 2, 2)], sib.at[zt], ts.at[zt], tr.at[zt], sibling)
+
+    for zt in order:
+        swap(zt).start()
+
+    def chain2(zt, k):
         i = zt * 2 + k
-        return Line(z, zt, groups, sib.at[zt, k], ub.at[zt, k], db.at[zt, k],
-                    (us.at[i], ur.at[i], ds.at[i], dr.at[i]), t, p)
-
-    for c, zt in zip(swaps, outward(groups)):
-        c.wait_recv()
+        return Line(z, zt, groups, sib.at[zt, k], ub2.at[zt, k], db2.at[zt, k],
+                    (us2.at[i], ur2.at[i], ds2.at[i], dr2.at[i]), t, p)
+
+    for i, zt in enumerate(order):
+        if i >= 1:
+            in_plane(zt)
+        swap(zt).wait_recv()
         for k in range(2):
             dst = sib.at[zt, k]
             add_rows(dst, dst, w2.at[zt * 4 + t * 2 + k], one)
-            chain(zt, k).start()
+            chain2(zt, k).start()
+        if i >= 1:
+            relay(order[i - 1], 1)
+            for k in range(2):
+                chain2(order[i - 1], k).relay(1, one)
+    for c in ring:
+        c.wait()
+    total = line[0]
+    for k in range(1, groups):
+        total = total + line[k]
+    line[groups] = total
+    both = remote(line.at[groups], line.at[groups + 1], gs.at[2 + groups], gr.at[2 + groups], sibling)
+    both.start()
     for hop in range(1, groups - 1):
-        for zt in outward(groups):
-            for k in range(2):
-                chain(zt, k).relay(hop, one)
-    for zt in outward(groups):
+        for i, zt in enumerate(order):
+            if hop > 1 or i == groups - 1:
+                relay(zt, hop)
+                for k in range(2):
+                    chain2(zt, k).relay(hop, one)
+    for zt in order:
         for k in range(2):
-            chain(zt, k).finish(fin.at[k], one)
+            chain2(zt, k).finish(fin.at[k], one)
     here_id = t * SPAN + me
 
     def hand(k, tt):
         m = t * 2 + k
         peer = (tt, z * SPAN + m)
         i = k * 2 + tt
-        away = remote(fin.at[k], out_ref.at[me], ps.at[i], pr.at[me], peer)
-        stay = pltpu.make_async_copy(fin.at[k], out_ref.at[me], lsem.at[3])
+        away = lambda: remote(fin.at[k], out_ref.at[me], ps.at[i], pr.at[me], peer)
+        stay = lambda: pltpu.make_async_copy(fin.at[k], out_ref.at[me], lsem.at[3])
         return away, stay, (tt * SPAN + m) == here_id
 
     for k in range(2):
         for tt in range(2):
             away, stay, same = hand(k, tt)
-            pl.when(jnp.logical_not(same))(lambda away=away: away.start())
-            pl.when(same)(lambda stay=stay: stay.start())
+            pl.when(jnp.logical_not(same))(lambda away=away: away().start())
+            pl.when(same)(lambda stay=stay: stay().start())
+    for zt in order:
+        for c, sl in ((0, pl.ds(0, size(0))), (1, pl.ds(size(0), size(1)))):
+            chain(c, zt).finish(pair_ref.at[t, sl], size(c))
+    last = remote(pair_ref.at[t], pair_ref.at[t], fs.at[0], fr.at[0], sibling)
+    last.start()
+    both.wait()
+    sum_ref[...] = line[groups] + line[groups + 1]
     for s in range(SPAN):
-        mine = jnp.logical_and(s == me, y == t)
-        got = remote(fin.at[0], out_ref.at[s], ps.at[0], pr.at[s], sibling)
-        pl.when(jnp.logical_not(mine))(lambda got=got: got.wait_recv())
+        from_here = jnp.logical_and(s == me, y == t)
+        pl.when(jnp.logical_not(from_here))(
+            lambda s=s: remote(fin.at[0], out_ref.at[s], ps.at[0], pr.at[s], sibling).wait_recv()
+        )
     for k in range(2):
         for tt in range(2):
             away, stay, same = hand(k, tt)
-            pl.when(jnp.logical_not(same))(lambda away=away: away.wait_send())
-            pl.when(same)(lambda stay=stay: stay.wait())
-    for c in swaps:
-        c.wait_send()
+            pl.when(jnp.logical_not(same))(lambda away=away: away().wait_send())
+            pl.when(same)(lambda stay=stay: stay().wait())
     for zt in range(groups):
+        swap(zt).wait_send()
         for k in range(2):
-            chain(zt, k).drain()
+            chain2(zt, k).drain()
+        for c in range(2):
+            second(c, zt).wait_send()
+            chain(c, zt).drain()
     for c in copies:
         c.wait()
-
-
-def tail(g, tok, groups):
+    last.wait()
+
+
+def finish(ka, kb, ra, rb, g, tok, gains, groups):
     width = tok.shape[1]
     count = tok.shape[0] // SPAN
     one = width // (SPAN * groups)
-    buf = lambda *n: pltpu.VMEM(n + (one, 3 * HW), bf)
+    na, nb = ka.shape[2], kb.shape[2]
+    half = ka.shape[3]
+    buf = lambda *n: pltpu.VMEM(n, bf)
+    mix = lambda *n: pltpu.VMEM(n + (one, 3 * HW), bf)
     return pl.pallas_call(
-        functools.partial(tail_kernel, groups),
+        functools.partial(finish_kernel, groups),
         out_shape=(
+            jax.ShapeDtypeStruct((2, na + nb, half), bf),
+            jax.ShapeDtypeStruct(gains.shape, f32),
             jax.ShapeDtypeStruct((3 * width, count), bf),
             jax.ShapeDtypeStruct((SPAN, one, 3 * HW), bf),
         ),
-        in_specs=[VM, VM],
-        out_specs=(ANY, VM),
+        in_specs=[ANY] * 4 + [VM] * 3,
+        out_specs=(VM, VM, ANY, VM),
         scratch_shapes=[
-            buf(SPAN * groups), buf(groups, 2), buf(groups, 2), buf(groups, 2), buf(2),
+            buf(groups, 2, na, half), buf(groups, 2, nb, half), buf(groups, 2, na, half), buf(groups, 2, nb, half),
+            buf(groups, na, half), buf(groups, nb, half), buf(groups, na, half), buf(groups, nb, half),
+            buf(groups, na, half), buf(groups, nb, half),
+            dma_sems(4 * groups), dma_sems(2 * groups), dma_sems(2 * groups),
+            dma_sems(2 * groups), dma_sems(2 * groups), dma_sems(2 * groups), dma_sems(2 * groups),
+            pltpu.VMEM((3,) + gains.shape, f32), pltpu.VMEM((groups + 2,) + gains.shape, f32),
+            dma_sems(3 + groups), dma_sems(3 + groups), dma_sems(1), dma_sems(1),
+            mix(SPAN * groups), mix(groups, 2), mix(groups, 2), mix(groups, 2), mix(2),
             dma_sems(9), dma_sems(9), dma_sems(groups), dma_sems(groups),
             dma_sems(2 * groups), dma_sems(2 * groups), dma_sems(2 * groups), dma_sems(2 * groups),
             dma_sems(4), dma_sems(SPAN), dma_sems(4),
         ],
         compiler_params=comm_params(3),
-        name="tail",
-    )(g, tok)
+        name="finish",
+    )(ka, kb, ra, rb, g, tok, gains)
 
 
 def swapped(value):
@@ -926,8 +980,8 @@
     )
     goal = jnp.where(slot % 8 < DOCS_GRP, goal // DOCS_GRP * 8 + goal % DOCS_GRP, -1)
     goal = jnp.broadcast_to(goal.astype(f32)[:, None], (groups * 8, 128))
-    w_mine = lax.dynamic_index_in_dim(w_qkv.reshape(width, 3, SPAN, HW), me, 2, keepdims=False)
-    w_mine = w_mine.reshape(width, 3 * HW).T
+    cols = [lax.dynamic_slice_in_dim(w_qkv, k * width + me * HW, HW, 1) for k in range(3)]
+    w_mine = jnp.concatenate(cols, 1).T
     cos, sin = angle_tables(SPAN * count)
     tok_all, codes = gather(rows, code)
     heads_out, lse, exact, qa, ka, va, kt = attn_fwd(tok_all, w_mine, cos, sin, codes)
@@ -964,18 +1018,23 @@
         its = lambda v: lax.dynamic_slice_in_dim(v, (1 - tower) * half, half, 1)
         kept = jnp.where(here_first, grad_gate, grad_up)
         sent = jnp.where(here_first, grad_up, grad_gate)
-        w_parts = weight_grads(
-            places,
-            inner, swapped(inner), kept, swapped(sent), hidden, swapped(hidden),
+        send_a, keep_a, send_b, keep_b, d_heads = weight_grads(
+            groups, grad_attended, inner, swapped(inner), kept, swapped(sent), hidden, swapped(hidden),
             own(grad_mlp), swapped(its(grad_mlp)), attended, swapped(attended),
             own(grad_branch), swapped(its(grad_branch)),
         )
-    d_heads = tokens_to_heads(grad_attended, 5, "to_heads")
+        exchange = lambda v, bit: lax.ppermute(v, "dp", [(i, i ^ bit) for i in range(places)])
+        came_a, came_b = exchange(send_a, 1), exchange(send_b, 2)
+    else:
+        d_heads = tokens_to_heads(grad_attended, 5, "to_heads")
     mixed = attn_bwd(d_heads, exact, lse, qa, ka, va, kt, cos, sin, codes)
     if by_hand:
         one = width // places
         down = w_down.shape[0] // places
-        pair, gain_sums = scatter(w_parts, jnp.concatenate([gains, jnp.zeros_like(gains)], 0), groups)
+        padded = jnp.concatenate([gains, jnp.zeros_like(gains)], 0)
+        pair, gain_sums, grad_mixed, qkv_parts = finish(
+            keep_a, keep_b, came_a, came_b, mixed, tok_all, padded, groups
+        )
         top = pair.shape[1] - down - one
         unfold = lambda v: v.reshape(top // one, one, half).transpose(1, 0, 2).reshape(one, -1)
         sides = lambda v: jnp.concatenate([v[0], v[1]], 1).astype(f32)
@@ -984,7 +1043,6 @@
         down_out = sides(pair[:, top : top + down])
         out_out = sides(pair[:, top + down :])
         gains_out = lax.dynamic_slice_in_dim(gain_sums[:4], place * one, one, 1)
-        grad_mixed, qkv_parts = tail(mixed, tok_all, groups)
         qkv_out = (
             qkv_parts.reshape(SPAN, one, 3, HW).transpose(1, 2, 0, 3).reshape(one, 3 * width).astype(f32)
         )

time: 382 us -> 309 us (0.81)
  Pallas kernels: 277 us -> 214 us
  waiting for transfers between devices: 0.02 us -> 9.73 us
  local copies, waits for them, and re-layouts: 27.4 us -> 18.3 us
  starting transfers between devices: 9.39 us -> 3.13 us
    pallas_call x4 -> x2, Pallas kernels: 180 us -> 99.6 us  [the longest x1 80.6 us: finish(): pl.pallas_call(functools.partial(finish_kernel, groups), out_shape=(jax.S...]
    ppermute x0 -> x2, waiting for transfers between devices: none -> 9.71 us  [local(): lax.ppermute(v, 'dp', [(i, i ^ bit) for i in range(places)])]
    ppermute x6, starting transfers between devices: 9.39 us -> 1.63 us  [swapped(): return lax.ppermute(value, 'tower', [(0, 1), (1, 0)])]
    pallas_call x1, Pallas kernels: 24.7 us -> 32.3 us  [attn_bwd(): pl.pallas_call(functools.partial(bwd_kernel, KB, QB), out_shape=jax.Shape...]
    unnamed x69 -> x73, local copies, waits for them, and re-layouts: 8.8 us -> 3.45 us
    pallas_call x1, Pallas kernels: 20.7 us -> 25.9 us  [attn_fwd(): pl.pallas_call(functools.partial(fwd_kernel, KB, QB), out_shape=(jax.Shap...]
    pallas_call x1, Pallas kernels: 8.95 us -> 13.2 us  [heads_to_tokens(): pl.pallas_call(functools.partial(heads_to_tokens_kernel, parts), out_shap...]
  transfers between devices with their start and end apart: 6 -> 8, of which waited for: 0 -> 2; matrix products, arithmetic and copies ran while one was open for 20% -> 20% of each run, Pallas kernels for 25% -> 15%
where the time goes in v2:
time: 309 us; the launch traced here: 310 us
  Pallas kernels  214 us (69%)
  matrix products  53.3 us (17%)
  local copies, waits for them, and re-layouts  18.3 us (6%)
  other arithmetic  10.8 us (3%)
  waiting for transfers between devices  9.73 us (3%)
  starting transfers between devices  3.13 us (1%)
    pallas_call x1, Pallas kernels, finish(): pl.pallas_call(functools.partial(finish_kernel, groups), out_shape=(jax.S...  80.6 us
    pallas_call x1, Pallas kernels, attn_bwd(): pl.pallas_call(functools.partial(bwd_kernel, KB, QB), out_shape=jax.Shape...  32.3 us
    pallas_call x1, Pallas kernels, gather(): pl.pallas_call(gather_kernel, out_shape=(jax.ShapeDtypeStruct((SPAN * cou...  29.3 us
    pallas_call x1, Pallas kernels, attn_fwd(): pl.pallas_call(functools.partial(fwd_kernel, KB, QB), out_shape=(jax.Shap...  25.9 us
    dot_general x4, matrix products, nt(): lax.dot_general(a, b, (((1,), (1,)), ((), ())), preferred_element_type=f32)  24.1 us
    pallas_call x1, Pallas kernels, weight_grads(): pl.pallas_call(functools.partial(weights_kernel, groups), out_shape=(part...  18.9 us
    dot_general x3, matrix products, nn(): lax.dot_general(a, b, (((1,), (0,)), ((), ())), preferred_element_type=f32)  16.1 us
    pallas_call x1, Pallas kernels, heads_to_tokens(): pl.pallas_call(functools.partial(heads_to_tokens_kernel, parts), out_shap...  13.2 us
  transfers between devices with their start and end apart: 8, of which 2 were waited for; matrix products, arithmetic and copies ran while one was open for 20% of the time, Pallas kernels for 15%

profile of v2, /device:TPU:25, one launch (start us, length us, event | category | flops | bytes accessed | tf_op | source)
XLA Modules:
  0.0 310.1 jit_solution(14815180481529319839)
XLA Ops:
  0.7 2.1 constant_dynamic-slice_fusion.7
  4.6 29.3 %gather.7 = (bf16[2048,768]{1,0:T(8,128)(2,1)}, f32[1,2048]{1,0:T(1,128)}) custom-call(bf16[512,768]{1,0:T(8,128)(2,1)} %bitcast.65, f32[1,512]{1,0:T(1,128)} %get-tuple-element.87.code_ref), custom_call_target="tpu_custom_call" | custom-call | tf_op jit(solution)/shard_map/gather/pallas_call | solution.py:136
  33.9 1.9 maximum_bitcast_fusion.wt_ref
  35.8 25.9 %attn_fwd.1 = (bf16[192,2048]{1,0:T(8,128)(2,1)}, f32[3,2048]{1,0:T(4,128)}, f32[192,2048]{1,0:T(8,128)}, bf16[3,128,2048]{2,1,0:T(8,128)(2,1)}, bf16[3,2048,128...) custom-call(bf16[2048,768]{1,0:T(8,128)(2,1)} %get-tuple-element.33.tok_ref, ...), custom_call_target="tpu_custom_call" | custom-call | flops 8254390272 | bytes 12582912 | tf_op jit(solution)/shard_map/attn_fwd/pallas_call | solution.py:399
  61.8 13.2 %to_tokens.1.aa = bf16[768,512]{1,0:T(8,128)(2,1)} custom-call(bf16[192,2048]{1,0:T(8,128)(2,1)} %get-tuple-element.35.in_ref), custom_call_target="tpu_custom_call" | custom-call | tf_op jit(solution)/shard_map/to_tokens/pallas_call | solution.py:185
  75.7 2.6 fusion.28
  80.3 4.1 %fusion.30 = f32[512,3072]{1,0:T(8,128)S(1)} fusion(bf16[512,768]{1,0:T(8,128)(2,1)} %fusion.4.ia, bf16[768,3072]{1,0:T(8,128)(2,1)S(1)} %bitcast.61), kind=kOutput, calls=%fused_computation.100 | convolution fusion | flops 2415919104 | bytes 11796480 | tf_op jit(solution)/shard_map/dot_general | solution.py:29
  84.4 7.3 %multiply_convert_fusion.2 = (bf16[512,3072]{1,0:T(8,128)(2,1)}, f32[512,3072]{1,0:T(8,128)}) fusion(f32[512,3072]{1,0:T(8,128)S(1)} %fusion.30, bf16[512,768]{1,0:T(8,128)(2,1)} %fusion.4.ia, bf16[768,3072]{1,0:T(8,128)(2,1)S(1)} %bitcast.72), kind=kOutput, calls=%fused_computation.3 | convolution fusion | flops 2425356288 | bytes 21233664 | tf_op jit(solution)/shard_map/dot_general | solution.py:29
  92.0 4.7 %fusion.29 = (f32[512]{0:T(512)S(1)}, f32[512,768]{1,0:T(8,128)S(1)}) fusion(bf16[512,3072]{1,0:T(8,128)(2,1)} %get-tuple-element.90.ha, bf16[3072,768]{1,0:T(8,128)(2,1)S(1)} %bitcast.70, f32[768]{0:T(1024)S(1)} %copy-done.16, f32[768]{0:T(1024)S(1)} %copy-done.11, f32[512]{0:T(512)S(1)} %add_rsqrt_fusion.1, f32[512,768]{1,0:T(8,128)S(1)} %get-tuple-element.89, ...), kind=kOutput, calls=%fused_computation.99 | convolution fusion | flops 2418277888 | bytes 11022336 | tf_op jit(solution)/shard_map/dot_general | solution.py:29
  98.2 1.6 fusion.1.sums_ref
  100.4 13.2 %contrast.1 = (f32[8,768]{1,0:T(8,128)}, f32[32,32]{1,0:T(8,128)}, f32[8,128]{1,0:T(8,128)}) custom-call(f32[8,768]{1,0:T(8,128)} %fusion.1.sums_ref, f32[32,128]{1,0:T(8,128)} %broadcast_in_dim.9.goal_ref), custom_call_target="tpu_custom_call" | custom-call | tf_op jit(solution)/shard_map/contrast/pallas_call | solution.py:297
  113.6 3.8 %multiply_reduce_fusion = (f32[768]{0:T(1024)}, f32[512]{0:T(512)S(1)}, f32[512]{0:T(512)S(1)}, f32[768]{0:T(1024)}, f32[512,768]{1,0:T(8,128)S(1)}) fusion(f32[512,768]{1,0:T(8,128)} %copy-done.5, f32[512]{0:T(512)S(1)} %add_rsqrt_fusion, f32[512]{0:T(512)S(1)} %broadcast_multiply_fusion.4, f32[768]{0:T(1024)S(1)} %copy-done.17, ...), kind=kOutput, calls=%fused_computation.9 | convolution fusion | flops 41293312 | bytes 3190272 | tf_op jit(solution)/shard_map/dot_general | solution.py:1002
  118.7 10.1 %broadcast_select_fusion = (bf16[512,3072]{1,0:T(8,128)(2,1)}, bf16[512,3072]{1,0:T(8,128)(2,1)}, bf16[512,3072]{1,0:T(8,128)(2,1)}) fusion(pred[]{:T(512)S(6)} %eq.45, f32[512,3072]{1,0:T(8,128)} %copy-done.4, f32[512,3072]{1,0:T(8,128)S(1)} %copy-done.28, bf16[512,768]{1,0:T(8,128)(2,1)S(1)} %get-tuple-element.67, bf16[3072,768]{1,0:T(8,128)(2,1)} %param.25), kind=kOutput, calls=%fused_computation.6 | convolution fusion | flops 2437939200 | bytes 27525120 | tf_op jit(solution)/shard_map/dot_general | solution.py:33
  130.2 6.1 %fusion.31 = f32[512,768]{1,0:T(8,128)S(1)} fusion(bf16[512,3072]{1,0:T(8,128)(2,1)} %get-tuple-element.66, bf16[768,3072]{1,0:T(8,128)(2,1)} %param.23), kind=kOutput, calls=%fused_computation.101 | convolution fusion | flops 2415919104 | bytes 9437184 | tf_op jit(solution)/shard_map/dot_general | solution.py:33
  136.3 6.2 %multiply_reduce_fusion.1 = (f32[768]{0:T(1024)}, f32[512]{0:T(512)S(1)}, f32[512]{0:T(512)S(1)}, f32[768]{0:T(1024)}, f32[512,768]{1,0:T(8,128)S(1)}) fusion(f32[512,768]{1,0:T(8,128)S(1)} %copy-done.3, f32[512]{0:T(512)S(1)} %add_rsqrt_fusion.1, f32[512]{0:T(512)S(1)} %broadcast_multiply_fusion.5, f32[768]{0:T(1024)S(1)} %copy-done.11, ...), kind=kOutput, calls=%fused_computation.10 | convolution fusion | flops 2420241920 | bytes 14173184 | tf_op jit(solution)/shard_map/dot_general | solution.py:33
  142.5 1.6 fusion.25
  145.1 2.0 broadcast_select_fusion.1.ga
  147.1 1.7 fusion.5.in_ref
  149.6 18.9 %weight_grads.1 = (bf16[4,2,336,384]{3,2,1,0:T(8,128)(2,1)}, bf16[4,2,336,384]{3,2,1,0:T(8,128)(2,1)}, bf16[4,2,288,384]{3,2,1,0:T(8,128)(2,1)}, bf16[4,2,288,384]{3,2,1,0:T(8,128)(2,1)}, bf16[192,2048]{1,0:T(8,128)(2,1)}) custom-call(bf16[512,768]{1,0:T(8,128)(2,1)} %fusion.4.ia, bf16[512,768]{1,0:T(8,128)(2,1)} %collective-permute-done.ib, ...), custom_call_target="tpu_custom_call" | custom-call | flops 5133828096 | bytes 31457280 | tf_op jit(solution)/shard_map/weight_grads/pallas_call | solution.py:605
  172.7 32.3 %attn_bwd.1.g_ref = bf16[576,2048]{1,0:T(8,128)(2,1)} custom-call(bf16[192,2048]{1,0:T(8,128)(2,1)} %get-tuple-element.43.do_ref, f32[192,2048]{1,0:T(8,128)} %get-tuple-element.44.o32_ref, f32[3,2048]{1,0:T(4,128)} %get-tuple-element.45.lse_ref, bf16[3,128,2048]{2,1,0:T(8,128)(2,1)} %get-tuple-element.46.qa_ref, ...), custom_call_target="tpu_custom_call" | custom-call | flops 16106127360 | bytes 12582912 | tf_op jit(solution)/shard_map/attn_bwd/pallas_call | solution.py:471
  205.0 3.4 %collective-permute-done.7.rb_ref = bf16[4,2,288,384]{3,2,1,0:T(8,128)(2,1)} collective-permute-done((bf16[4,2,288,384]{3,2,1,0:T(8,128)(2,1)}, bf16[4,2,288,384]{3,2,1,0:T(8,128)(2,1)}, u32[]{:S(2)}, u32[]{:S(2)}) %collective-permute-start.7) | collective-permute-done | bytes 1769504 | tf_op jit(solution)/shard_map/ppermute | solution.py:1026
  208.4 6.3 %collective-permute-done.6.ra_ref = bf16[4,2,336,384]{3,2,1,0:T(8,128)(2,1)} collective-permute-done((bf16[4,2,336,384]{3,2,1,0:T(8,128)(2,1)}, bf16[4,2,336,384]{3,2,1,0:T(8,128)(2,1)}, u32[]{:S(2)}, u32[]{:S(2)}) %collective-permute-start.6) | collective-permute-done | bytes 2064416 | tf_op jit(solution)/shard_map/ppermute | solution.py:1026
  214.7 80.6 %finish.1 = (bf16[2,624,384]{2,1,0:T(8,128)(2,1)}, f32[8,768]{1,0:T(8,128)}, bf16[2304,512]{1,0:T(8,128)(2,1)}, bf16[4,48,576]{2,1,0:T(8,128)(2,1)}) custom-call(bf16[4,2,336,384]{3,2,1,0:T(8,128)(2,1)} %get-tuple-element.39.ka_ref, bf16[4,2,288,384]{3,2,1,0:T(8,128)(2,1)} %get-tuple-element.40.kb_ref, ...), custom_call_target="tpu_custom_call" | custom-call | tf_op jit(solution)/shard_map/finish/pallas_call | solution.py:899
  303.4 5.2 %add_bitcast_fusion = f32[1,512,768]{2,1,0:T(8,128)} fusion(f32[512,768]{1,0:T(8,128)S(1)} %copy-done.9, bf16[2304,512]{1,0:T(8,128)(2,1)S(1)} %copy-done.24, bf16[768,2304]{1,0:T(8,128)(2,1)} %param.19), kind=kOutput, calls=%fused_computation.8 | convolution fusion | flops 1812332544 | bytes 9043968 | tf_op jit(solution)/shard_map/dot_general | solution.py:1057
  (136 shorter events, 24.7 us)
Async XLA Ops:
  0.6 75.0 %copy-start = (bf16[768,768]{1,0:T(8,128)(2,1)S(1)}, bf16[768,768]{1,0:T(8,128)(2,1)}, u32[]{:S(2)}) copy-start(bf16[768,768]{1,0:T(8,128)(2,1)} %param.20) | copy-start | bytes 3538948
  61.8 18.5 %slice-start = ((s8[4718592]{0:T(1024)(128)(4,1)}), s8[524288]{0:T(1024)(128)(4,1)S(1)}, s32[]{:S(2)}) async-start(s8[4718592]{0:T(1024)(128)(4,1)} %bitcast.60), calls=%async_computation | async-start | bytes 1048576
  75.0 5.2 %slice-start.1 = ((s8[4718592]{0:T(1024)(128)(4,1)}), s8[4194304]{0:T(1024)(128)(4,1)S(1)}, s32[]{:S(2)}) async-start(s8[4718592]{0:T(1024)(128)(4,1)} %bitcast.60), calls=%async_computation.1 | async-start | bytes 8388608
  75.0 73.8 %collective-permute-start.4 = (bf16[768,512]{1,0:T(8,128)(2,1)}, bf16[768,512]{1,0:T(8,128)(2,1)}, u32[]{:S(2)}, u32[]{:S(2)}) collective-permute-start(bf16[768,512]{1,0:T(8,128)(2,1)} %to_tokens.1.aa), channel_id=1, source_target_pairs={{0,16},{16,0},{1,17},{17,1},{2,18},{18,2},{3,19},{19,3},{4,20},{20... | collective-permute-start | bytes 2359304 | tf_op jit(solution)/shard_map/ppermute | solution.py:928
  78.3 13.7 %copy-start.2 = (f32[512,768]{1,0:T(8,128)}, f32[512,768]{1,0:T(8,128)S(1)}, u32[]{:S(2)}) copy-start(f32[512,768]{1,0:T(8,128)S(1)} %get-tuple-element.89) | copy-start | bytes 4718596
  79.0 5.3 %slice-start.4 = ((s8[4718592]{0:T(1024)(128)(4,1)}), s8[4194304]{0:T(1024)(128)(4,1)S(1)}, s32[]{:S(2)}) async-start(s8[4718592]{0:T(1024)(128)(4,1)} %bitcast.71), calls=%async_computation.4 | async-start | bytes 8388608
  80.2 68.5 %collective-permute-start = (bf16[512,768]{1,0:T(8,128)(2,1)}, bf16[512,768]{1,0:T(8,128)(2,1)}, u32[]{:S(2)}, u32[]{:S(2)}) collective-permute-start(bf16[512,768]{1,0:T(8,128)(2,1)} %fusion.4.ia), channel_id=1, source_target_pairs={{0,16},{16,0},{1,17},{17,1},{2,18},{18,2},{3,19},{19,3},{4,20},{20... | collective-permute-start | bytes 2359304 | tf_op jit(solution)/shard_map/ppermute | solution.py:928
  80.3 11.8 %slice-start.2 = ((s8[4718592]{0:T(1024)(128)(4,1)}), s8[4194304]{0:T(1024)(128)(4,1)S(1)}, s32[]{:S(2)}) async-start(s8[4718592]{0:T(1024)(128)(4,1)} %bitcast.69), calls=%async_computation.2 | async-start | bytes 8388608
  84.4 7.3 %copy-start.4 = (f32[512,3072]{1,0:T(8,128)}, f32[512,3072]{1,0:T(8,128)S(1)}, u32[]{:S(2)}) copy-start(f32[512,3072]{1,0:T(8,128)S(1)} %fusion.30) | copy-start | bytes 18874372
  84.4 7.6 %slice-start.3 = ((s8[4718592]{0:T(1024)(128)(4,1)}), s8[524288]{0:T(1024)(128)(4,1)S(1)}, s32[]{:S(2)}) async-start(s8[4718592]{0:T(1024)(128)(4,1)} %bitcast.69), calls=%async_computation.3 | async-start | bytes 1048576
  91.7 57.1 %collective-permute-start.2 = (bf16[512,3072]{1,0:T(8,128)(2,1)}, bf16[512,3072]{1,0:T(8,128)(2,1)}, u32[]{:S(2)}, u32[]{:S(2)}) collective-permute-start(bf16[512,3072]{1,0:T(8,128)(2,1)} %get-tuple-element.90.ha), channel_id=1, source_target_pairs={{0,16},{16,0},{1,17},{17,1},{2,18},{18,2},{3,19},{19,3},{4,20},{20... | collective-permute-start | bytes 9437192 | tf_op jit(solution)/shard_map/ppermute | solution.py:928
  97.1 20.4 %copy-start.13 = (f32[512]{0:T(512)}, f32[512]{0:T(512)S(1)}, u32[]{:S(2)}) copy-start(f32[512]{0:T(512)S(1)} %add_rsqrt_fusion) | copy-start | bytes 6148
  128.8 20.0 %collective-permute-start.1 = (bf16[512,3072]{1,0:T(8,128)(2,1)}, bf16[512,3072]{1,0:T(8,128)(2,1)}, u32[]{:S(2)}, u32[]{:S(2)}) collective-permute-start(bf16[512,3072]{1,0:T(8,128)(2,1)} %get-tuple-element.64), channel_id=1, source_target_pairs={{0,16},{16,0},{1,17},{17,1},{2,18},{18,2},{3,19},{19,3},{4,20},{20... | collective-permute-start | bytes 9437192 | tf_op jit(solution)/shard_map/ppermute | solution.py:928
  129.8 15.1 %collective-permute-start.3 = (bf16[512,384]{1,0:T(8,128)(2,1)S(1)}, bf16[512,384]{1,0:T(8,128)(2,1)S(1)}, u32[]{:S(2)}, u32[]{:S(2)}) collective-permute-start(bf16[512,384]{1,0:T(8,128)(2,1)S(1)} %get-tuple-element.80), channel_id=1, source_target_pairs={{0,16},{16,0},{1,17},{17,1},{2,18},{18,2},{3,19},{19,3},{4,20},{20... | collective-permute-start | bytes 1179656 | tf_op jit(solution)/shard_map/ppermute | solution.py:928
  130.2 6.1 %copy-start.3 = (f32[512,768]{1,0:T(8,128)S(1)}, f32[512,768]{1,0:T(8,128)}, u32[]{:S(2)}) copy-start(f32[512,768]{1,0:T(8,128)} %copy-done.2) | copy-start | bytes 4718596
  130.2 6.1 %copy-start.7 = (bf16[512,3072]{1,0:T(8,128)(2,1)S(1)}, bf16[512,3072]{1,0:T(8,128)(2,1)}, u32[]{:S(2)}) copy-start(bf16[512,3072]{1,0:T(8,128)(2,1)} %get-tuple-element.65) | copy-start | bytes 9437188
  144.9 3.9 %collective-permute-start.5 = (bf16[512,384]{1,0:T(8,128)(2,1)S(1)}, bf16[512,384]{1,0:T(8,128)(2,1)S(1)}, u32[]{:S(2)}, u32[]{:S(2)}) collective-permute-start(bf16[512,384]{1,0:T(8,128)(2,1)S(1)} %get-tuple-element.78), channel_id=1, source_target_pairs={{0,16},{16,0},{1,17},{17,1},{2,18},{18,2},{3,19},{19,3},{4,20},{20... | collective-permute-start | bytes 1179656 | tf_op jit(solution)/shard_map/ppermute | solution.py:928
  149.5 20.5 %copy-start.12 = (f32[32,32]{1,0:T(8,128)S(1)}, f32[32,32]{1,0:T(8,128)}, u32[]{:S(2)}) copy-start(f32[32,32]{1,0:T(8,128)} %get-tuple-element.36) | copy-start | bytes 12292
  149.5 22.5 %copy-start.22 = (f32[768]{0:T(1024)S(1)}, f32[768]{0:T(1024)}, u32[]{:S(2)}) copy-start(f32[768]{0:T(1024)} %get-tuple-element.56) | copy-start | bytes 9220
  149.5 22.5 %copy-start.21 = (f32[768]{0:T(1024)S(1)}, f32[768]{0:T(1024)}, u32[]{:S(2)}) copy-start(f32[768]{0:T(1024)} %get-tuple-element.61) | copy-start | bytes 9220
  149.5 22.5 %copy-start.20 = (f32[768]{0:T(1024)S(1)}, f32[768]{0:T(1024)}, u32[]{:S(2)}) copy-start(f32[768]{0:T(1024)} %get-tuple-element.54) | copy-start | bytes 9220
  149.5 22.5 %copy-start.19 = (f32[768]{0:T(1024)S(1)}, f32[768]{0:T(1024)}, u32[]{:S(2)}) copy-start(f32[768]{0:T(1024)} %get-tuple-element.60) | copy-start | bytes 9220
  168.5 46.2 %collective-permute-start.6 = (bf16[4,2,336,384]{3,2,1,0:T(8,128)(2,1)}, bf16[4,2,336,384]{3,2,1,0:T(8,128)(2,1)}, u32[]{:S(2)}, u32[]{:S(2)}) collective-permute-start(bf16[4,2,336,384]{3,2,1,0:T(8,128)(2,1)} %get-tuple-element.41), channel_id=1, source_target_pairs={{0,1},{1,0},{2,3},{3,2},{4,5},{5,4},{6,7},{7,6},{8,9},{9,8},{10,11... | collective-permute-start | bytes 6193160 | tf_op jit(solution)/shard_map/ppermute | solution.py:1026
  168.9 39.5 %collective-permute-start.7 = (bf16[4,2,288,384]{3,2,1,0:T(8,128)(2,1)}, bf16[4,2,288,384]{3,2,1,0:T(8,128)(2,1)}, u32[]{:S(2)}, u32[]{:S(2)}) collective-permute-start(bf16[4,2,288,384]{3,2,1,0:T(8,128)(2,1)} %get-tuple-element.42), channel_id=1, source_target_pairs={{0,2},{1,3},{2,0},{3,1},{4,6},{5,7},{6,4},{7,5},{8,10},{9,11},{10,... | collective-permute-start | bytes 5308424 | tf_op jit(solution)/shard_map/ppermute | solution.py:1026
  (19 other events, 42.0 us)

commit v3 on v2

--- a/solution.py
+++ b/solution.py
@@ -230,89 +230,6 @@
         compiler_params=comm_params(cid),
         name=name,
     )(a)
-
-
-def loss_kernel(groups, sums_ref, goal_ref, gp_ref, scores_ref, loss_ref, plane, allp, ge, send, recv):
-    t, p, x, y, g = here()
-    docs = groups * DOCS_GRP
-    me = lax.rem(p, SPAN)
-    peers = plane_peers()
-    sibling = (1 - t, p)
-    line = [(t, lax.rem(p + SPAN * k, SPAN * groups)) for k in range(1, groups)]
-    greet(tuple(peers) + tuple(line) + (sibling,))
-    copies = []
-    for i, peer in enumerate(peers):
-        c = remote(sums_ref, plane.at[i], send.at[i], recv.at[i], peer)
-        c.start()
-        copies.append(c)
-    for c in copies:
-        c.wait()
-    own = sums_ref[...] + plane[0]
-    own = own + (plane[1] + plane[2])
-    allp[t, g] = own
-    rows = allp.at[t, g]
-    copies = []
-    for i, peer in enumerate(line):
-        c = remote(rows, rows, send.at[3 + i], recv.at[3 + i], peer)
-        c.start()
-        copies.append(c)
-    for c in copies:
-        c.wait()
-    c = remote(allp.at[t], allp.at[t], send.at[2 + groups], recv.at[2 + groups], sibling)
-    c.start()
-    c.wait()
-    width = sums_ref.shape[1]
-    size = groups * 8
-    pools = [allp[k].reshape(size, width) for k in range(2)]
-    invs = [lax.rsqrt(jnp.sum(v * v, -1, keepdims=True) + 1e-06) for v in pools]
-    embeds = [v * r for v, r in zip(pools, invs)]
-    dot = functools.partial(lax.dot_general, precision=precise, preferred_element_type=f32)
-    scores = dot(embeds[0], embeds[1], (((1,), (1,)), ((), ()))) * 50.0
-    col = lax.broadcasted_iota(jnp.int32, (size, size), 1)
-    row = lax.broadcasted_iota(jnp.int32, (size, size), 0)
-    live = lax.rem(col, 8) < DOCS_GRP
-    alive = lax.rem(row, 8) < DOCS_GRP
-    masked = jnp.where(live, scores, -1e30)
-    top = jnp.max(masked, -1, keepdims=True)
-    total = jnp.sum(jnp.exp(masked - top), -1, keepdims=True)
-    log_sums = top + jnp.log(total)
-    hot = jnp.where(col.astype(f32) == goal_ref[:, 0:1], 1.0, 0.0)
-    chosen = jnp.sum(hot * scores, -1, keepdims=True)
-    each = jnp.where(alive[:, 0:1], log_sums - chosen, 0.0)
-    loss_ref[...] = jnp.broadcast_to(jnp.sum(each, 0, keepdims=True) / docs, loss_ref.shape)
-    scores_ref[...] = scores
-    gs = jnp.where(alive & live, (jnp.exp(masked - log_sums) - hot) / docs, 0.0)
-    gq = dot(gs, embeds[1], (((1,), (0,)), ((), ())))
-    gd = dot(gs, embeds[0], (((0,), (0,)), ((), ())))
-    ge[...] = jnp.where(t == 0, gq, gd) * 50.0
-    mine = ge[pl.ds(pl.multiple_of(g * 8, 8), 8), :]
-    pooled = allp[t, g]
-    inv = lax.rsqrt(jnp.sum(pooled * pooled, -1, keepdims=True) + 1e-06)
-    gp_ref[...] = inv * mine - inv * inv * inv * pooled * jnp.sum(pooled * mine, -1, keepdims=True)
-
-
-def contrast(sums, goal, groups):
-    size = groups * 8
-    width = sums.shape[1]
-    return pl.pallas_call(
-        functools.partial(loss_kernel, groups),
-        out_shape=(
-            jax.ShapeDtypeStruct((8, width), f32),
-            jax.ShapeDtypeStruct((size, size), f32),
-            jax.ShapeDtypeStruct((8, 128), f32),
-        ),
-        in_specs=[VM, VM],
-        out_specs=(VM, VM, VM),
-        scratch_shapes=[
-            pltpu.VMEM((3, 8, width), f32),
-            pltpu.VMEM((2, groups, 8, width), f32),
-            pltpu.VMEM((size, width), f32),
-            dma_sems(3 + groups),
-            dma_sems(3 + groups),
-        ],
-        compiler_params=comm_params(1),
-        name="contrast",
-    )(sums, goal)
 
 
 def doc_limits(code):
@@ -477,8 +394,278 @@
         cost_estimate=pl.CostEstimate(flops=int(10*T*T*128*3), bytes_accessed=12<<20, transcendentals=T*T*3))(do, o32, lse, qa, ka, va, kt, cos, sin, code)
 
 
+def contrast_part(groups, sums, goals_ref, plane, allp, ge, send, recv, scores_ref, loss_ref):
+    t, p, x, y, g = here()
+    docs = groups * DOCS_GRP
+    size = groups * 8
+    peers = plane_peers()
+    line = [(t, lax.rem(p + SPAN * k, SPAN * groups)) for k in range(1, groups)]
+    plane[3] = sums
+    copies = [remote(plane.at[3], plane.at[i], send.at[i], recv.at[i], q) for i, q in enumerate(peers)]
+    for c in copies:
+        c.start()
+    col = lax.broadcasted_iota(jnp.int32, (size, size), 1)
+    row = lax.broadcasted_iota(jnp.int32, (size, size), 0)
+
+    def mark(i, hot):
+        goal = goals_ref[i]
+        at = (row == i // DOCS_GRP * 8 + i % DOCS_GRP) & (col == goal // DOCS_GRP * 8 + goal % DOCS_GRP)
+        return hot + jnp.where(at, 1.0, 0.0)
+
+    hot = lax.fori_loop(0, docs, mark, jnp.zeros((size, size), f32))
+    for c in copies:
+        c.wait()
+    own = (plane[3] + plane[0]) + (plane[1] + plane[2])
+    allp[t, g] = own
+    rows = allp.at[t, g]
+    copies = [remote(rows, rows, send.at[3 + i], recv.at[3 + i], q) for i, q in enumerate(line)]
+    for c in copies:
+        c.start()
+    for c in copies:
+        c.wait()
+    c = remote(allp.at[t], allp.at[t], send.at[2 + groups], recv.at[2 + groups], (1 - t, p))
+    c.start()
+    c.wait()
+    width = allp.shape[3]
+    pools = [allp[k].reshape(size, width) for k in range(2)]
+    embeds = [v * lax.rsqrt(jnp.sum(v * v, -1, keepdims=True) + 1e-06) for v in pools]
+    dot = functools.partial(lax.dot_general, precision=precise, preferred_element_type=f32)
+    scores = dot(embeds[0], embeds[1], (((1,), (1,)), ((), ()))) * 50.0
+    live = lax.rem(col, 8) < DOCS_GRP
+    alive = lax.rem(row, 8) < DOCS_GRP
+    masked = jnp.where(live, scores, -1e30)
+    top = jnp.max(masked, -1, keepdims=True)
+    total = jnp.sum(jnp.exp(masked - top), -1, keepdims=True)
+    log_sums = top + jnp.log(total)
+    chosen = jnp.sum(hot * scores, -1, keepdims=True)
+    each = jnp.where(alive[:, 0:1], log_sums - chosen, 0.0)
+    loss_ref[...] = jnp.broadcast_to(jnp.sum(each, 0, keepdims=True) / docs, loss_ref.shape)
+    scores_ref[...] = scores
+    gs = jnp.where(alive & live, (jnp.exp(masked - log_sums) - hot) / docs, 0.0)
+    gq = dot(gs, embeds[1], (((1,), (0,)), ((), ())))
+    gd = dot(gs, embeds[0], (((0,), (0,)), ((), ())))
+    ge[...] = jnp.where(t == 0, gq, gd) * 50.0
+    mine = ge[pl.ds(pl.multiple_of(g * 8, 8), 8), :]
+    pooled = allp[t, g]
+    inv = lax.rsqrt(jnp.sum(pooled * pooled, -1, keepdims=True) + 1e-06)
+    return inv * mine - inv * inv * inv * pooled * jnp.sum(pooled * mine, -1, keepdims=True)
+
+
+def block_kernel(
+    groups, heads_ref, rows_ref, code_ref, goals_ref, norms_ref, wo_h, wg_h, wu_h, wd_h,
+    att_o, inner_o, hid_o, gm_o, gg_o, gb_o, ga_o, gh1_o, gains_o, scores_o, loss_o,
+    att, wo, wg, wu, wd, inner, x1, s1, acc, hid, ab, x2, s2, sec, gm, gm2, gb, gb2, plane, allp, ge,
+    wsem, send, recv, lsem, tsend, trecv, osem, csend, crecv,
+):
+    t, p, x, y, g = here()
+    peers = plane_peers()
+    sibling = (1 - t, p)
+    line = tuple((t, lax.rem(p + SPAN * k, SPAN * groups)) for k in range(1, groups))
+    count, width = rows_ref.shape
+    half = width // 2
+    tiles = wg.shape[0]
+    me = lax.rem(p, SPAN)
+
+    def weight(j, k):
+        cols = pl.ds(j * width, width)
+        src, dst = ((wg_h.at[:, cols], wg.at[j]), (wu_h.at[:, cols], wu.at[j]), (wd_h.at[cols], wd.at[j]))[k]
+        return pltpu.make_async_copy(src, dst, wsem.at[1 + 3 * j + k])
+
+    first_load = pltpu.make_async_copy(wo_h, wo, wsem.at[0])
+    first_load.start()
+    for j in range(tiles):
+        for k in range(3):
+            weight(j, k).start()
+    greet(peers + (sibling,) + line)
+    moves = []
+    for i, peer in enumerate((peers[2], peers[0], peers[1])):
+        m = lax.rem(peer[1], SPAN)
+        moves.append(remote(
+            heads_ref.at[:, pl.ds(pl.multiple_of(m * count, count), count)],
+            att.at[pl.ds(pl.multiple_of(me * HW, HW), HW)], send.at[i], recv.at[i], peer,
+        ))
+    moves.append(pltpu.make_async_copy(
+        heads_ref.at[:, pl.ds(pl.multiple_of(me * count, count), count)],
+        att.at[pl.ds(pl.multiple_of(me * HW, HW), HW)], lsem.at[0],
+    ))
+    for c in moves:
+        c.start()
+    code = code_ref[...]
+    zero = jnp.zeros((8 - DOCS_GRP, count), f32)
+    mem = jnp.concatenate([jnp.where(code == float(d), 1.0, 0.0) for d in range(DOCS_GRP)] + [zero], 0)
+    mem = jnp.concatenate([mem, mem, mem, jnp.zeros((8, count), f32)], 0).astype(bf)
+    first_load.wait()
+    for c in moves:
+        c.wait()
+
+    def pair(i, mine, its, out):
+        return (
+            pltpu.make_async_copy(mine, out.at[0], osem.at[i]),
+            remote(its, out.at[1], tsend.at[i], trecv.at[i], sibling),
+        )
+
+    def both(i, mine, its, out):
+        for c in pair(i, mine, its, out):
+            c.start()
+
+    both(0, att, att, att_o)
+    acc[...] = tn(att[...], wo[...])
+    step = 64
+    gain1, bias1 = norms_ref[0:1, :], norms_ref[1:2, :]
+    gain2, bias2 = norms_ref[2:3, :], norms_ref[3:4, :]
+
+    def chunk(i):
+        return pl.ds(pl.multiple_of(i * step, step), step)
+
+    def norm(h, sl, xs, ss):
+        c = h - jnp.mean(h, -1, keepdims=True)
+        s = lax.rsqrt(jnp.mean(c * c, -1, keepdims=True) + norm_eps)
+        xh = c * s
+        xs[sl, :] = xh
+        ss[sl, :] = s
+        return xh
+
+    def norm_one(i, _):
+        sl = chunk(i)
+        xh = norm(rows_ref[sl, :].astype(f32) + acc[sl, :], sl, x1, s1)
+        v = xh * gain1 + bias1
+        inner[sl, :] = v.astype(bf)
+        acc[sl, :] = v
+        return 0
+
+    lax.fori_loop(0, count // step, norm_one, 0)
+    both(1, inner, inner, inner_o)
+
+    def tile_of(j, i, mine, its, out):
+        return (
+            pltpu.make_async_copy(mine, out.at[0, j], osem.at[i + j]),
+            remote(its, out.at[1, j], tsend.at[i + j], trecv.at[i + j], sibling),
+        )
+
+    for j in range(tiles):
+        for k in range(3):
+            weight(j, k).wait()
+        gate = nn(inner[...], wg[j])
+        upper = nn(inner[...], wu[j])
+        sig = jax.nn.sigmoid(gate)
+        silu = gate * sig
+        hid[j] = (silu * upper).astype(bf)
+        ab[0, j] = (upper * (sig * (1.0 + gate * (1.0 - sig)))).astype(bf)
+        ab[1, j] = silu.astype(bf)
+        for c in tile_of(j, 2, hid.at[j], hid.at[j], hid_o):
+            c.start()
+        acc[...] += nn(hid[j], wd[j])
+
+    def norm_two(i, _):
+        sl = chunk(i)
+        v = norm(acc[sl, :], sl, x2, s2) * gain2 + bias2
+        for k, part in enumerate(split3(v)):
+            sec[k, sl, :] = part.astype(bf)
+        return 0
+
+    lax.fori_loop(0, count // step, norm_two, 0)
+    sums = (nn(mem[:16], sec[0]) + nn(mem[:16], sec[1]) + nn(mem[:16], sec[2]))[:8]
+    top = lax.broadcasted_iota(jnp.int32, sums.shape, 0) < DOCS_GRP
+    sums = jnp.where(top, sums, 0.0)
+    gp = contrast_part(groups, sums, goals_ref, plane, allp, ge, csend, crecv, scores_o, loss_o)
+    gp3 = jnp.concatenate(split3(gp) + [jnp.zeros_like(gp)], 0).astype(bf)
+    acc[...] = tn(mem, gp3)
+
+    def fold(v):
+        return jnp.sum(v.reshape(step // 8, 8, width), 0)
+
+    def norm_back(gr, xh, s, gain):
+        e = gr * gain
+        v = e - jnp.mean(e, -1, keepdims=True) - xh * jnp.mean(e * xh, -1, keepdims=True)
+        return v * s
+
+    zeros = jnp.zeros((8, width), f32)
+
+    def back_two(i, sums):
+        sl = chunk(i)
+        gr, xh = acc[sl, :], x2[sl, :]
+        v = norm_back(gr, xh, s2[sl, :], gain2)
+        acc[sl, :] = v
+        low = v.astype(bf)
+        gm[sl, :] = low
+        gm2[0, sl, :] = low[:, :half]
+        gm2[1, sl, :] = low[:, half:]
+        return sums[0] + fold(gr * xh), sums[1] + fold(gr)
+
+    g2, b2 = lax.fori_loop(0, count // step, back_two, (zeros, zeros))
+    both(2 + 2 * tiles, gm2.at[t], gm2.at[1 - t], gm_o)
+    for j in range(tiles):
+        gh = nt(gm[...], wd[j])
+        gg = (gh * ab[0, j].astype(f32)).astype(bf)
+        gu = (gh * ab[1, j].astype(f32)).astype(bf)
+        ab[0, j] = gg
+        ab[1, j] = gu
+        for c in tile_of(j, 2 + tiles, ab.at[t, j], ab.at[1 - t, j], gg_o):
+            c.start()
+        acc[...] += nt(gg, wg[j]) + nt(gu, wu[j])
+
+    def back_one(i, sums):
+        sl = chunk(i)
+        gr, xh = acc[sl, :], x1[sl, :]
+        v = norm_back(gr, xh, s1[sl, :], gain1)
+        gh1_o[sl, :] = v
+        low = v.astype(bf)
+        gb[sl, :] = low
+        gb2[0, sl, :] = low[:, :half]
+        gb2[1, sl, :] = low[:, half:]
+        return sums[0] + fold(gr * xh), sums[1] + fold(gr)
+
+    g1, b1 = lax.fori_loop(0, count // step, back_one, (zeros, zeros))
+    both(3 + 2 * tiles, gb2.at[t], gb2.at[1 - t], gb_o)
+    flat = [jnp.sum(v, 0, keepdims=True) for v in (g1, b1, g2, b2)]
+    gains_o[...] = jnp.concatenate(flat + [jnp.zeros((4, width), f32)], 0)
+    ga_o[...] = nt(wo[...], gb[...]).astype(bf)
+    done = [pair(0, att, att, att_o), pair(1, inner, inner, inner_o)]
+    for j in range(tiles):
+        done.append(tile_of(j, 2, hid.at[j], hid.at[j], hid_o))
+        done.append(tile_of(j, 2 + tiles, ab.at[t, j], ab.at[1 - t, j], gg_o))
+    done.append(pair(2 + 2 * tiles, gm2.at[t], gm2.at[1 - t], gm_o))
+    done.append(pair(3 + 2 * tiles, gb2.at[t], gb2.at[1 - t], gb_o))
+    for c in done:
+        for d in c:
+            d.wait()
+
+
+def block(heads, rows, code, goals, norms, w_out, w_gate, w_up, w_down, groups):
+    count, width = rows.shape
+    tiles = w_gate.shape[1] // width
+    half = width // 2
+    size = groups * 8
+    sds = jax.ShapeDtypeStruct
+    vm = lambda *n: pltpu.VMEM(n, bf)
+    vf = lambda *n: pltpu.VMEM(n, f32)
+    return pl.pallas_call(
+        functools.partial(block_kernel, groups),
+        out_shape=(
+            sds((2, width, count), bf), sds((2, count, width), bf), sds((2, tiles, count, width), bf),
+            sds((2, count, half), bf), sds((2, tiles, count, width), bf), sds((2, count, half), bf),
+            sds((width, count), bf), sds((count, width), f32), sds((8, width), f32),
+            sds((size, size), f32), sds((8, 128), f32),
+        ),
+        in_specs=[VM, VM, VM, pl.BlockSpec(memory_space=pltpu.SMEM), VM] + [ANY] * 4,
+        out_specs=(ANY,) * 6 + (VM,) * 5,
+        scratch_shapes=[
+            vm(width, count), vm(width, width), vm(tiles, width, width), vm(tiles, width, width),
+            vm(tiles, width, width), vm(count, width), vf(count, width), vf(count, 1), vf(count, width),
+            vm(tiles, count, width), vm(2, tiles, count, width), vf(count, width), vf(count, 1),
+            vm(3, count, width), vm(count, width), vm(2, count, half), vm(count, width), vm(2, count, half),
+            vf(4, 8, width), vf(2, groups, 8, width), vf(size, width),
+            dma_sems(1 + 3 * tiles), dma_sems(3), dma_sems(3), dma_sems(1),
+            dma_sems(4 + 2 * tiles), dma_sems(4 + 2 * tiles), dma_sems(4 + 2 * tiles),
+            dma_sems(3 + groups), dma_sems(3 + groups),
+        ],
+        compiler_params=comm_params(1),
+        name="block",
+    )(heads, rows, code, goals, norms, w_out, w_gate, w_up, w_down)
+
+
 def weights_kernel(
-    groups, ia, ib, ga, gb, ha, hb, ma, mb, aa, ab, ba, bb, in_ref,
+    groups, i_ref, g_ref, h_ref, m_ref, a_ref, b_ref, in_ref,
     sa_ref, ka_ref, sb_ref, kb_ref, heads_ref,
     iv, it, gv, hv, mv, av, bv, gs, ds, os, isem, osem, send, recv, lsem,
 ):
@@ -500,45 +687,37 @@
     ))
     for c in moves:
         c.start()
-    count, width = ia.shape
+    count, width = i_ref.shape[1:]
     half = width // 2
     tiles = gv.shape[1]
     shards = SPAN * groups
     one = width // shards
-    down = ha.shape[1] // shards
+    down = ds.shape[1]
 
     def load(i, src, dst):
         return pltpu.make_async_copy(src, dst, isem.at[i])
 
-    def tile(pair, j, buf, base):
-        cols = pl.ds(pl.multiple_of(j * half, half), half)
-        return [load(base + i * tiles + j, a.at[:, cols], buf.at[i, j]) for i, a in enumerate(pair)]
-
-    few = [(ma, mv.at[0]), (mb, mv.at[1]), (aa, av.at[0]), (ab, av.at[1]),
-           (ba, bv.at[0]), (bb, bv.at[1]), (ia, iv.at[0]), (ib, iv.at[1])]
-    few = [load(i, a, b) for i, (a, b) in enumerate(few)]
-    for c in few[:2]:
-        c.start()
+    def tile(ref, j, buf, base):
+        return load(base + j, ref.at[:, j], buf.at[:, j])
+
+    few = [load(i, a, b) for i, (a, b) in enumerate(((m_ref, mv), (a_ref, av), (b_ref, bv), (i_ref, iv)))]
+    few[0].start()
     for j in range(tiles):
-        for c in tile((ha, hb), j, hv, 8):
-            c.start()
-    for c in few[2:]:
+        tile(h_ref, j, hv, 4).start()
+    for c in few[1:]:
         c.start()
     for j in range(tiles):
-        for c in tile((ga, gb), j, gv, 8 + 2 * tiles):
-            c.start()
-    for c in few[:2]:
-        c.wait()
+        tile(g_ref, j, gv, 4 + tiles).start()
+    few[0].wait()
 
     def downward(j, _):
-        for c in tile((ha, hb), j, hv, 8):
-            c.wait()
+        tile(h_ref, j, hv, 4).wait()
         r = tn(hv[0, j], mv[0]) + tn(hv[1, j], mv[1])
-        ds[pl.ds(j * (half // down), half // down)] = r.astype(bf).reshape(half // down, down, half)
+        ds[pl.ds(j * (width // down), width // down)] = r.astype(bf).reshape(width // down, down, half)
         return 0
 
     lax.fori_loop(0, tiles, downward, 0)
-    for c in few[2:]:
+    for c in few[1:]:
         c.wait()
     r = nn(av[0], bv[0]) + nn(av[1], bv[1])
     os[...] = r.astype(bf).reshape(shards, one, half)
@@ -549,7 +728,6 @@
     def put(i, src, dst):
         return pltpu.make_async_copy(src, dst, osem.at[i])
 
-    last = (tiles - 1) * one
     outs = []
     for i, (ref, k) in enumerate(((sb_ref, 1 - y), (kb_ref, y))):
         outs.append(put(4 * i, fours(ds, down).at[:, k], ref.at[:, :, pl.ds(one, down)]))
@@ -557,48 +735,41 @@
     for c in outs:
         c.start()
 
-    def upward(j, _):
-        for c in tile((ga, gb), j, gv, 8 + 2 * tiles):
-            c.wait()
-        r = nn(it[:, :count], gv[0, j]) + nn(it[:, count:], gv[1, j])
-        gs[j] = r.astype(bf).reshape(shards, one, half)
-        return 0
-
-    def upper(j, _):
-        upward(j, 0)
+    def top(j):
         rows = pl.ds(pl.multiple_of(j * one, one), one)
         piece = fours(gs.at[j], one)
-        put(8 + j, piece.at[:, :, 1 - x], sa_ref.at[:, :, rows]).start()
-        put(8 + tiles + j, piece.at[:, :, x], ka_ref.at[:, :, rows]).start()
-        return 0
-
-    lax.fori_loop(0, tiles - 1, upper, 0)
-    upward(tiles - 1, 0)
-    piece = fours(gs.at[tiles - 1], one)
+        return (
+            put(8 + j, piece.at[:, :, 1 - x], sa_ref.at[:, :, rows]),
+            put(8 + 2 * tiles + j, piece.at[:, :, x], ka_ref.at[:, :, rows]),
+        )
+
+    for j in range(tiles):
+        tile(g_ref, j, gv, 4 + tiles).wait()
+        r = (nn(it[:, :count], gv[0, j]) + nn(it[:, count:], gv[1, j])).astype(bf)
+        for h in range(2):
+            k = 2 * j + h
+            gs[k] = r[:, h * half : (h + 1) * half].reshape(shards, one, half)
+            if k < 2 * tiles - 1:
+                outs.extend(top(k))
+                for c in outs[-2:]:
+                    c.start()
+    piece = fours(gs.at[2 * tiles - 1], one)
     for i, (ref, k) in enumerate(((sb_ref, 1 - y), (kb_ref, y))):
         c = put(4 * i + 2, piece.at[:, k], ref.at[:, :, pl.ds(0, one)])
         c.start()
         outs.append(c)
-
-    def landed(j, _):
-        rows = pl.ds(pl.multiple_of(j * one, one), one)
-        put(8 + j, fours(gs.at[j], one).at[:, :, 0], sa_ref.at[:, :, rows]).wait()
-        put(8 + tiles + j, fours(gs.at[j], one).at[:, :, 0], ka_ref.at[:, :, rows]).wait()
-        return 0
-
-    lax.fori_loop(0, tiles - 1, landed, 0)
     for c in outs + moves:
         c.wait()
 
 
-def weight_grads(groups, grad_heads, *arrays):
-    count, width = arrays[0].shape
+def weight_grads(groups, grad_heads, inner, grads, hidden, grad_mlp, attended, grad_branch):
+    count, width = inner.shape[1:]
     half = width // 2
     shards = SPAN * groups
     one = width // shards
-    tiles = arrays[2].shape[1] // half
-    down = arrays[4].shape[1] // shards
-    ra = (tiles - 1) * one
+    tiles = grads.shape[1]
+    down = tiles * one
+    ra = (2 * tiles - 1) * one
     rb = down + 2 * one
     part = lambda r: jax.ShapeDtypeStruct((groups, 2, r, half), bf)
     vm = lambda *n: pltpu.VMEM(n, bf)
@@ -608,18 +779,20 @@
             part(ra), part(ra), part(rb), part(rb),
             jax.ShapeDtypeStruct((HW, SPAN * grad_heads.shape[1]), bf),
         ),
-        in_specs=[ANY] * 12 + [VM],
+        in_specs=[ANY] * 6 + [VM],
         out_specs=(ANY,) * 5,
         scratch_shapes=[
-            vm(2, count, width), vm(width, 2 * count), vm(2, tiles, count, half), vm(2, tiles, count, half),
+            vm(2, count, width), vm(width, 2 * count), vm(2, tiles, count, width), vm(2, tiles, count, width),
             vm(2, count, half), vm(2, width, count), vm(2, count, half),
-            vm(tiles, shards, one, half), vm(shards, down, half), vm(shards, one, half),
-            dma_sems(8 + 4 * tiles), dma_sems(8 + 2 * tiles), dma_sems(3), dma_sems(3), dma_sems(1),
+            vm(2 * tiles, shards, one, half), vm(shards, down, half), vm(shards, one, half),
+            dma_sems(4 + 2 * tiles), dma_sems(8 + 4 * tiles), dma_sems(3), dma_sems(3), dma_sems(1),
         ],
         compiler_params=comm_params(2),
         name="weight_grads",
-        cost_estimate=pl.CostEstimate(flops=int(2 * 2 * count * half * width * 8.5), bytes_accessed=30 << 20, transcendentals=0),
-    )(*arrays, grad_heads)
+        cost_estimate=pl.CostEstimate(
+            flops=int(2 * 2 * count * half * width * 8.5), bytes_accessed=30 << 20, transcendentals=0
+        ),
+    )(inner, grads, hidden, grad_mlp, attended, grad_branch, grad_heads)
 
 
 def add_rows(dst, a, b, rows):
@@ -924,28 +1097,6 @@
     )(ka, kb, ra, rb, g, tok, gains)
 
 
-def swapped(value):
-    return lax.ppermute(value, "tower", [(0, 1), (1, 0)])
-
-
-def norm_rows(values, gain, bias):
-    centred = values - jnp.mean(values, -1, keepdims=True)
-    spread = jnp.mean(centred * centred, -1, keepdims=True)
-    scale = lax.rsqrt(spread + norm_eps)
-    normed = centred * scale
-    return normed * gain + bias, normed, scale
-
-
-def norm_back(grad, normed, scale, gain):
-    shaped = grad * gain
-    inner = (
-        shaped
-        - jnp.mean(shaped, -1, keepdims=True)
-        - normed * jnp.mean(shaped * normed, -1, keepdims=True)
-    )
-    return inner * scale, jnp.sum(grad * normed, 0), jnp.sum(grad, 0)
-
-
 def angle_tables(total):
     half = HEAD_DIM // 2
     freqs = np.float32(1000.0) ** (-np.arange(half, dtype=np.float32) / np.float32(half))
@@ -974,54 +1125,20 @@
     live = pad_mask[0] == 1
     code = jnp.where(live, member_of, member_of + 4).astype(f32)[None, :]
     docs = groups * DOCS_GRP
-    slot = jnp.arange(groups * 8)
-    goal = jnp.where(
-        slot % 8 < DOCS_GRP, targets[jnp.minimum(slot // 8 * DOCS_GRP + slot % 8, docs - 1)], 0
-    )
-    goal = jnp.where(slot % 8 < DOCS_GRP, goal // DOCS_GRP * 8 + goal % DOCS_GRP, -1)
-    goal = jnp.broadcast_to(goal.astype(f32)[:, None], (groups * 8, 128))
     cols = [lax.dynamic_slice_in_dim(w_qkv, k * width + me * HW, HW, 1) for k in range(3)]
     w_mine = jnp.concatenate(cols, 1).T
     cos, sin = angle_tables(SPAN * count)
     tok_all, codes = gather(rows, code)
     heads_out, lse, exact, qa, ka, va, kt = attn_fwd(tok_all, w_mine, cos, sin, codes)
-    attended = heads_to_tokens(heads_out, 4, "to_tokens")
-    branch = tn(attended, w_out)
-    first, normed_one, scale_one = norm_rows(rows.astype(f32) + branch, ln1_gain, ln1_bias)
-    inner = first.astype(bf)
-    gate = nn(inner, w_gate)
-    upper = nn(inner, w_up)
-    sigmoid = jax.nn.sigmoid(gate)
-    activated = gate * sigmoid
-    hidden = (activated * upper).astype(bf)
-    second, normed_two, scale_two = norm_rows(first + nn(hidden, w_down), ln2_gain, ln2_bias)
-    member = ((member_of[:, None] == jnp.arange(8)[None, :]) & live[:, None]).astype(f32)
-    sums = jnp.dot(member.T, second, precision=precise)
-    grad_pool, scores_all, loss = contrast(sums, goal, groups)
+    norms = jnp.stack([ln1_gain, ln1_bias, ln2_gain, ln2_bias] + [jnp.zeros_like(ln1_gain)] * 4, 0)
+    (
+        attended, inner, hidden, grad_mlp, grads, grad_branch, grad_attended, grad_h1, gains, scores_all, loss
+    ) = block(heads_out, rows, code, targets, norms, w_out, w_gate, w_up, w_down, groups)
     scores = scores_all.reshape(groups, 8, groups, 8)[:, :DOCS_GRP, :, :DOCS_GRP].reshape(docs, docs)
-    grad_second = jnp.dot(member, grad_pool, precision=precise)
-    grad_h2, gain_two, bias_two = norm_back(grad_second, normed_two, scale_two, ln2_gain)
-    grad_mlp = grad_h2.astype(bf)
-    grad_hidden = nt(grad_mlp, w_down)
-    grad_gate = (grad_hidden * upper * sigmoid * (1.0 + gate * (1.0 - sigmoid))).astype(bf)
-    grad_up = (grad_hidden * activated).astype(bf)
-    grad_first = grad_h2 + nt(grad_gate, w_gate) + nt(grad_up, w_up)
-    grad_h1, gain_one, bias_one = norm_back(grad_first, normed_one, scale_one, ln1_gain)
-    grad_branch = grad_h1.astype(bf)
-    grad_attended = nt(w_out, grad_branch).astype(bf)
-    gains = jnp.stack([gain_one, bias_one, gain_two, bias_two], 0)
-    here_first = tower == 0
     by_hand = width % (16 * places) == 0
     if by_hand:
-        half = width // 2
-        own = lambda v: lax.dynamic_slice_in_dim(v, tower * half, half, 1)
-        its = lambda v: lax.dynamic_slice_in_dim(v, (1 - tower) * half, half, 1)
-        kept = jnp.where(here_first, grad_gate, grad_up)
-        sent = jnp.where(here_first, grad_up, grad_gate)
         send_a, keep_a, send_b, keep_b, d_heads = weight_grads(
-            groups, grad_attended, inner, swapped(inner), kept, swapped(sent), hidden, swapped(hidden),
-            own(grad_mlp), swapped(its(grad_mlp)), attended, swapped(attended),
-            own(grad_branch), swapped(its(grad_branch)),
+            groups, grad_attended, inner, grads, hidden, grad_mlp, attended, grad_branch
         )
         exchange = lambda v, bit: lax.ppermute(v, "dp", [(i, i ^ bit) for i in range(places)])
         came_a, came_b = exchange(send_a, 1), exchange(send_b, 2)
@@ -1029,11 +1146,11 @@
         d_heads = tokens_to_heads(grad_attended, 5, "to_heads")
     mixed = attn_bwd(d_heads, exact, lse, qa, ka, va, kt, cos, sin, codes)
     if by_hand:
+        half = width // 2
         one = width // places
         down = w_down.shape[0] // places
-        padded = jnp.concatenate([gains, jnp.zeros_like(gains)], 0)
         pair, gain_sums, grad_mixed, qkv_parts = finish(
-            keep_a, keep_b, came_a, came_b, mixed, tok_all, padded, groups
+            keep_a, keep_b, came_a, came_b, mixed, tok_all, gains, groups
         )
         top = pair.shape[1] - down - one
         unfold = lambda v: v.reshape(top // one, one, half).transpose(1, 0, 2).reshape(one, -1)
@@ -1049,11 +1166,15 @@
     else:
         grad_mixed = heads_to_tokens(mixed, 6, "to_tokens_back")
         qkv_out = spread_sum(tn(rows, grad_mixed.T))
-        out_out = spread_sum(nn(attended, grad_branch))
-        gate_out = spread_sum(tn(inner, grad_gate))
-        up_out = spread_sum(tn(inner, grad_up))
-        down_out = spread_sum(tn(hidden, grad_mlp))
-        gains_out = spread_sum(gains.T).T
+        side = lambda v: lax.psum_scatter(v, "dp", scatter_dimension=0, tiled=True)
+        halves = lambda v: lax.all_gather(side(v).astype(bf), "tower", axis=1, tiled=True).astype(f32)
+        both = lambda a, b: tn(a[0], b[0]) + tn(a[1], b[1])
+        flat = lambda v: v.transpose(0, 2, 1, 3).reshape(2, count, -1)
+        out_out = halves(nn(attended[0], grad_branch[0]) + nn(attended[1], grad_branch[1]))
+        two = lax.all_gather(side(both(inner, flat(grads))).astype(bf), "tower").astype(f32)
+        gate_out, up_out = two[0], two[1]
+        down_out = halves(both(flat(hidden), grad_mlp))
+        gains_out = spread_sum(gains[:4].T).T
     token_grad = grad_h1 + lax.dot_general(
         grad_mixed, w_qkv, (((0,), (1,)), ((), ())), preferred_element_type=f32
     )

time: 309 us -> 276 us (0.89)
  matrix products: 53.3 us -> 6.35 us
  Pallas kernels: 214 us -> 238 us
  other arithmetic: 10.8 us -> 3.18 us
  local copies, waits for them, and re-layouts: 18.3 us -> 15 us
    dot_general x10 -> x0, matrix products: 48.1 us -> none  [the longest x4 24.1 us: nt(): lax.dot_general(a, b, (((1,), (1,)), ((), ())), preferred_element_type=f32)]
    pallas_call x2 -> x1, Pallas kernels: 26.4 us -> 53.3 us  [block(): pl.pallas_call(functools.partial(block_kernel, groups), out_shape=(sds((2...]
    convert_element_type x4 -> x1, other arithmetic: 4.03 us -> 0.59 us  [local(): code = jnp.where(live, member_of, member_of + 4).astype(f32)[None, :]]
    another operation x4 -> x6, local copies, waits for them, and re-layouts: 0.02 us -> 3.4 us  [local(): jnp.stack([ln1_gain, ln1_bias, ln2_gain, ln2_bias] + [jnp.zeros_like(ln1_...]
  transfers between devices with their start and end apart: 8 -> 2, of which waited for: 2 -> 2; matrix products, arithmetic and copies ran while one was open for 20% -> 1% of each run, Pallas kernels for 15% -> 11%
where the time goes in v3:
time: 276 us; the launch traced here: 277 us
  Pallas kernels  238 us (86%)
  local copies, waits for them, and re-layouts  15 us (5%)
  waiting for transfers between devices  11.7 us (4%)
  matrix products  6.35 us (2%)
  other arithmetic  3.18 us (1%)
    pallas_call x1, Pallas kernels, finish(): pl.pallas_call(functools.partial(finish_kernel, groups), out_shape=(jax.S...  81.4 us
    pallas_call x1, Pallas kernels, block(): pl.pallas_call(functools.partial(block_kernel, groups), out_shape=(sds((2...  53.3 us
    pallas_call x1, Pallas kernels, attn_bwd(): pl.pallas_call(functools.partial(bwd_kernel, KB, QB), out_shape=jax.Shape...  31.1 us
    pallas_call x1, Pallas kernels, gather(): pl.pallas_call(gather_kernel, out_shape=(jax.ShapeDtypeStruct((SPAN * cou...  29.3 us
    pallas_call x1, Pallas kernels, attn_fwd(): pl.pallas_call(functools.partial(fwd_kernel, KB, QB), out_shape=(jax.Shap...  25.2 us
    pallas_call x1, Pallas kernels, weight_grads(): pl.pallas_call(functools.partial(weights_kernel, groups), out_shape=(part...  18 us
    ppermute x2, waiting for transfers between devices, local(): lax.ppermute(v, 'dp', [(i, i ^ bit) for i in range(places)])  11.7 us
    dot_general x1, matrix products, local(): lax.dot_general(grad_mixed, w_qkv, (((0,), (1,)), ((), ())), preferred_el...  6.35 us
  transfers between devices with their start and end apart: 2, of which 2 were waited for; matrix products, arithmetic and copies ran while one was open for 1% of the time, Pallas kernels for 11%

profile of v3, /device:TPU:25, one launch (start us, length us, event | category | flops | bytes accessed | tf_op | source)
XLA Modules:
  0.0 276.8 jit_solution(6928374145248260894)
XLA Ops:
  0.7 0.7 stack.18
  1.3 0.7 stack.19
  2.0 0.7 stack.20
  2.7 0.7 stack.21
  3.4 2.0 constant_dynamic-slice_fusion.3
  6.5 29.3 %gather.1 = (bf16[2048,768]{1,0:T(8,128)(2,1)}, f32[1,2048]{1,0:T(1,128)}) custom-call(bf16[512,768]{1,0:T(8,128)(2,1)} %bitcast.37, f32[1,512]{1,0:T(1,128)} %fusion.code_ref), custom_call_target="tpu_custom_call" | custom-call | tf_op jit(solution)/shard_map/gather/pallas_call | solution.py:136
  35.9 1.0 maximum_bitcast_fusion.wt_ref
  37.5 25.2 %attn_fwd.1 = (bf16[192,2048]{1,0:T(8,128)(2,1)}, f32[3,2048]{1,0:T(4,128)}, f32[192,2048]{1,0:T(8,128)}, bf16[3,128,2048]{2,1,0:T(8,128)(2,1)}, bf16[3,2048,128...) custom-call(bf16[2048,768]{1,0:T(8,128)(2,1)} %get-tuple-element.41.tok_ref, ...), custom_call_target="tpu_custom_call" | custom-call | flops 8254390272 | bytes 12582912 | tf_op jit(solution)/shard_map/attn_fwd/pallas_call | solution.py:316
  62.7 53.3 %block.1 = (bf16[2,768,512]{2,1,0:T(8,128)(2,1)}, bf16[2,512,768]{2,1,0:T(8,128)(2,1)}, bf16[2,4,512,768]{3,2,1,0:T(8,128)(2,1)}, bf16[2,512,384]{2,1,0:T(8,128)...) custom-call(bf16[192,2048]{1,0:T(8,128)(2,1)} %get-tuple-element.43., ...), custom_call_target="tpu_custom_call" | custom-call | tf_op jit(solution)/shard_map/block/pallas_call | solution.py:642
  116.0 18.0 %weight_grads.1 = (bf16[4,2,336,384]{3,2,1,0:T(8,128)(2,1)}, bf16[4,2,336,384]{3,2,1,0:T(8,128)(2,1)}, bf16[4,2,288,384]{3,2,1,0:T(8,128)(2,1)}, bf16[4,2,288,384]{3,2,1,0:T(8,128)(2,1)}, bf16[192,2048]{1,0:T(8,128)(2,1)}) custom-call(bf16[2,512,768]{2,1,0:T(8,128)(2,1)} %get-tuple-element.47.i_ref, bf16[2,4,512,768]{3,2,1,0:T(8,128)(2,1)} %get-tuple-element.48.g_ref, ...), custom_call_target="tpu_custom_call" | custom-call | flops 5133828096 | bytes 31457280 | tf_op jit(solution)/shard_map/weight_grads/pallas_call | solution.py:776
  134.4 1.2 collective-permute-start.1
  135.5 1.2 slice.46
  137.5 31.1 %attn_bwd.1.g_ref = bf16[576,2048]{1,0:T(8,128)(2,1)} custom-call(bf16[192,2048]{1,0:T(8,128)(2,1)} %get-tuple-element.58.do_ref, f32[192,2048]{1,0:T(8,128)} %get-tuple-element.59.o32_ref, f32[3,2048]{1,0:T(4,128)} %get-tuple-element.60.lse_ref, bf16[3,128,2048]{2,1,0:T(8,128)(2,1)} %get-tuple-element.61.qa_ref, ...), custom_call_target="tpu_custom_call" | custom-call | flops 16106127360 | bytes 12582912 | tf_op jit(solution)/shard_map/attn_bwd/pallas_call | solution.py:388
  168.6 5.3 %collective-permute-done.1.rb_ref = bf16[4,2,288,384]{3,2,1,0:T(8,128)(2,1)S(1)} collective-permute-done((bf16[4,2,288,384]{3,2,1,0:T(8,128)(2,1)}, bf16[4,2,288,384]{3,2,1,0:T(8,128)(2,1)S(1)}, u32[]{:S(2)}, u32[]{:S(2)}) %collective-permute-start.1) | collective-permute-done | bytes 1769504 | tf_op jit(solution)/shard_map/ppermute | solution.py:1143
  173.9 6.4 %collective-permute-done.ra_ref = bf16[4,2,336,384]{3,2,1,0:T(8,128)(2,1)} collective-permute-done((bf16[4,2,336,384]{3,2,1,0:T(8,128)(2,1)}, bf16[4,2,336,384]{3,2,1,0:T(8,128)(2,1)}, u32[]{:S(2)}, u32[]{:S(2)}) %collective-permute-start) | collective-permute-done | bytes 2064416 | tf_op jit(solution)/shard_map/ppermute | solution.py:1143
  180.2 81.4 %finish.1 = (bf16[2,624,384]{2,1,0:T(8,128)(2,1)}, f32[8,768]{1,0:T(8,128)}, bf16[2304,512]{1,0:T(8,128)(2,1)}, bf16[4,48,576]{2,1,0:T(8,128)(2,1)}) custom-call(bf16[4,2,336,384]{3,2,1,0:T(8,128)(2,1)} %get-tuple-element.54.ka_ref, bf16[4,2,288,384]{3,2,1,0:T(8,128)(2,1)} %get-tuple-element.55.kb_ref, bf16[4,2,336,384]{3,2,1,0:T(8,128)(2,1)} %collective-permute-done.ra_ref, ...), custom_call_target="tpu_custom_call" | custom-call | tf_op jit(solution)/shard_map/finish/pallas_call | solution.py:1072
  261.6 0.8 slice_bitcast_fusion.3
  262.4 1.0 slice_bitcast_fusion.1
  263.4 1.1 fusion.1
  265.2 0.9 copy.47
  266.2 0.9 copy.48
  267.8 1.1 reshape.48
  268.9 6.3 %add_bitcast_fusion = f32[1,512,768]{2,1,0:T(8,128)} fusion(f32[512,768]{1,0:T(8,128)} %get-tuple-element.46, bf16[2304,512]{1,0:T(8,128)(2,1)} %get-tuple-element.66, bf16[768,2304]{1,0:T(8,128)(2,1)} %param.19), kind=kOutput, calls=%fused_computation | convolution fusion | flops 1812332544 | bytes 9043968 | tf_op jit(solution)/shard_map/dot_general | solution.py:1178
  275.9 0.9 maximum_convert_fusion
  (30 shorter events, 5.0 us)
Async XLA Ops:
  3.4 2.5 copy-start.4
  3.4 2.5 copy-start.5
  116.0 20.7 %copy-start.2 = (f32[32,32]{1,0:T(8,128)S(1)}, f32[32,32]{1,0:T(8,128)}, u32[]{:S(2)}) copy-start(f32[32,32]{1,0:T(8,128)} %get-tuple-element.44) | copy-start | bytes 12292
  134.0 46.2 %collective-permute-start = (bf16[4,2,336,384]{3,2,1,0:T(8,128)(2,1)}, bf16[4,2,336,384]{3,2,1,0:T(8,128)(2,1)}, u32[]{:S(2)}, u32[]{:S(2)}) collective-permute-start(bf16[4,2,336,384]{3,2,1,0:T(8,128)(2,1)} %get-tuple-element.56), channel_id=1, source_target_pairs={{0,1},{1,0},{2,3},{3,2},{4,5},{5,4},{6,7},{7,6},{8,9},{9,8},{10,11... | collective-permute-start | bytes 6193160 | tf_op jit(solution)/shard_map/ppermute | solution.py:1143
  134.4 39.5 %collective-permute-start.1 = (bf16[4,2,288,384]{3,2,1,0:T(8,128)(2,1)}, bf16[4,2,288,384]{3,2,1,0:T(8,128)(2,1)S(1)}, u32[]{:S(2)}, u32[]{:S(2)}) collective-permute-start(bf16[4,2,288,384]{3,2,1,0:T(8,128)(2,1)} %get-tuple-element.57), channel_id=1, source_target_pairs={{0,2},{1,3},{2,0},{3,1},{4,6},{5,7},{6,4},{7,5},{8,10},{9,11},{10,... | collective-permute-start | bytes 5308424 | tf_op jit(solution)/shard_map/ppermute | solution.py:1143
  173.9 6.4 %copy-start = (bf16[4,2,288,384]{3,2,1,0:T(8,128)(2,1)}, bf16[4,2,288,384]{3,2,1,0:T(8,128)(2,1)S(1)}, u32[]{:S(2)}) copy-start(bf16[4,2,288,384]{3,2,1,0:T(8,128)(2,1)S(1)} %collective-permute-done.1.rb_ref) | copy-start | bytes 5308420
  261.6 2.9 %copy-start.3 = (f32[8,768]{1,0:T(8,128)S(1)}, f32[8,768]{1,0:T(8,128)}, u32[]{:S(2)}) copy-start(f32[8,768]{1,0:T(8,128)} %get-tuple-element.69) | copy-start | bytes 73732
  265.2 1.8 copy-start.1

commit v4 on v3

--- a/solution.py
+++ b/solution.py
@@ -81,70 +81,125 @@
     return pltpu.CompilerParams(collective_id=cid, has_side_effects=True, vmem_limit_bytes=VLIM)
 
 
-def gather_kernel(tok_ref, code_ref, out_ref, codes_ref, send, recv, csend, crecv, lsem):
+def gather_kernel(
+    tok_ref, code_ref, cos_ref, sin_ref, w_ref, out_ref, codes_ref, qa_ref, ka_ref, va_ref, kt_ref,
+    toks, codes, wraw, wturn, wt, qa, ka, va, kt, send, recv, csend, crecv, wsem, osem,
+):
     t, p, x, y, g = here()
-    count = tok_ref.shape[0]
+    count, width = tok_ref.shape
     half = count // 2
     me = lax.rem(p, SPAN)
+    odd = lax.rem(me, 2)
+    wide = wraw.shape[2]
+    loads = []
+    for k in range(3):
+        at = pl.multiple_of(k * width + me * HW - odd * HEAD_DIM, 128)
+        loads.append(pltpu.make_async_copy(w_ref.at[:, pl.ds(at, wide)], wraw.at[k], wsem.at[k]))
+        loads[-1].start()
     ex, ey, ed = plane_peers()
-    mx = lax.rem(ex[1], SPAN)
-    my = lax.rem(ey[1], SPAN)
+    mx, my, md = (lax.rem(q[1], SPAN) for q in (ex, ey, ed))
 
     def rows(m, h):
         return pl.ds(pl.multiple_of(m * count + h * half, half), half)
 
-    def lanes(m):
+    def whole(m):
         return pl.ds(pl.multiple_of(m * count, count), count)
 
     greet((ex, ey, ed))
     first = []
     for i, (peer, h) in enumerate(((ex, 0), (ey, 1), (ex, 1), (ey, 0))):
-        c = remote(
-            tok_ref.at[pl.ds(h * half, half)], out_ref.at[rows(me, h)], send.at[i], recv.at[i], peer
-        )
+        c = remote(tok_ref.at[pl.ds(h * half, half)], toks.at[rows(me, h)], send.at[i], recv.at[i], peer)
         c.start()
         first.append(c)
     small = []
     for i, peer in enumerate((ex, ey, ed)):
-        c = remote(code_ref, codes_ref.at[:, lanes(me)], csend.at[i], crecv.at[i], peer)
+        c = remote(code_ref, codes.at[:, whole(me)], csend.at[i], crecv.at[i], peer)
         c.start()
         small.append(c)
-    own = pltpu.make_async_copy(tok_ref, out_ref.at[lanes(me)], lsem.at[0])
-    own.start()
-    own_code = pltpu.make_async_copy(code_ref, codes_ref.at[:, lanes(me)], lsem.at[1])
-    own_code.start()
+    codes[:, whole(me)] = code_ref[...]
+    for k in range(3):
+        loads[k].wait()
+        wturn[...] = wraw[k].T
+        wt[k * HW : (k + 1) * HW, :] = wturn[pl.ds(pl.multiple_of(odd * HEAD_DIM, HEAD_DIM), HW), :]
+
+    def project(rows_ref, m, n):
+        sl = whole(m)
+        mx = nt(wt[...], rows_ref[...])
+        cos, sin = cos_ref[:, sl], sin_ref[:, sl]
+        cd = codes[:, sl]
+        mem = jnp.where(cd >= 4.0, cd - 4.0, cd)
+        pad = [jnp.zeros((13, count), f32)]
+        hot = jnp.concatenate([jnp.where(mem == float(d), 1.0, 0.0) for d in range(DOCS_GRP)] + pad, 0)
+        neg = jnp.concatenate([jnp.where(cd == float(d), 0.0, -1e30) for d in range(DOCS_GRP)] + pad, 0)
+        rest = jnp.zeros((48, count), f32)
+        one = jnp.concatenate([jnp.ones((1, count), f32), jnp.zeros((63, count), f32)], 0)
+
+        def rope(u):
+            a, b = u[:32], u[32:]
+            return jnp.concatenate([a * cos - b * sin, b * cos + a * sin], 0)
+
+        for h in range(NH):
+            q = rope(mx[h * HEAD_DIM : (h + 1) * HEAD_DIM]).astype(bf).astype(f32) * 0.125
+            k = rope(mx[HW + h * HEAD_DIM : HW + (h + 1) * HEAD_DIM])
+            v = mx[2 * HW + h * HEAD_DIM : 2 * HW + (h + 1) * HEAD_DIM]
+            qa[h, :, sl] = jnp.concatenate([q, hot, rest], 0).astype(bf)
+            ka[h, sl, :] = jnp.concatenate([k, neg, rest], 0).T.astype(bf)
+            va[h, :, sl] = jnp.concatenate([v, one], 0).astype(bf)
+            kt[h, :, sl] = k.astype(bf)
+        puts = (
+            (rows_ref, out_ref.at[sl]),
+            (qa.at[:, :, sl], qa_ref.at[:, :, sl]),
+            (ka.at[:, sl, :], ka_ref.at[:, sl, :]),
+            (va.at[:, :, sl], va_ref.at[:, :, sl]),
+            (kt.at[:, :, sl], kt_ref.at[:, :, sl]),
+        )
+        puts = [pltpu.make_async_copy(a, b, osem.at[5 * n + i]) for i, (a, b) in enumerate(puts)]
+        for c in puts:
+            c.start()
+        return puts
+
+    done = project(tok_ref, me, 0)
     first[0].wait_recv()
-    f0 = remote(out_ref.at[rows(mx, 0)], out_ref.at[rows(mx, 0)], send.at[4], recv.at[4], ey)
+    f0 = remote(toks.at[rows(mx, 0)], toks.at[rows(mx, 0)], send.at[4], recv.at[4], ey)
     f0.start()
     first[1].wait_recv()
-    f1 = remote(out_ref.at[rows(my, 1)], out_ref.at[rows(my, 1)], send.at[5], recv.at[5], ex)
+    f1 = remote(toks.at[rows(my, 1)], toks.at[rows(my, 1)], send.at[5], recv.at[5], ex)
     f1.start()
+    for c in small:
+        c.wait()
     first[2].wait_recv()
+    done += project(toks.at[whole(mx)], mx, 1)
     first[3].wait_recv()
+    done += project(toks.at[whole(my)], my, 2)
     f0.wait_recv()
     f1.wait_recv()
+    done += project(toks.at[whole(md)], md, 3)
+    codes_ref[...] = codes[...]
     for c in first + [f0, f1]:
         c.wait_send()
-    for c in small:
+    for c in done:
         c.wait()
-    own.wait()
-    own_code.wait()
-
-
-def gather(tok, code):
+
+
+def gather(tok, code, cos, sin, w_qkv):
     count, width = tok.shape
+    total = SPAN * count
+    shapes = ((NH, 128, total), (NH, total, 128), (NH, 128, total), (NH, HEAD_DIM, total))
     return pl.pallas_call(
         gather_kernel,
-        out_shape=(
-            jax.ShapeDtypeStruct((SPAN * count, width), bf),
-            jax.ShapeDtypeStruct((1, SPAN * count), f32),
-        ),
-        in_specs=[VM, VM],
-        out_specs=(ANY, ANY),
-        scratch_shapes=[dma_sems(6), dma_sems(6), dma_sems(3), dma_sems(3), dma_sems(2)],
+        out_shape=(jax.ShapeDtypeStruct((total, width), bf), jax.ShapeDtypeStruct((1, total), f32))
+        + tuple(jax.ShapeDtypeStruct(s, bf) for s in shapes),
+        in_specs=[VM] * 4 + [ANY],
+        out_specs=(ANY, VM) + (ANY,) * 4,
+        scratch_shapes=[
+            pltpu.VMEM((total, width), bf), pltpu.VMEM((1, total), f32), pltpu.VMEM((3, width, 256), bf),
+            pltpu.VMEM((256, width), bf), pltpu.VMEM((3 * HW, width), bf),
+        ]
+        + [pltpu.VMEM(s, bf) for s in shapes]
+        + [dma_sems(6), dma_sems(6), dma_sems(3), dma_sems(3), dma_sems(3), dma_sems(20)],
         compiler_params=comm_params(0),
         name="gather",
-    )(tok, code)
+    )(tok, code, cos, sin, w_qkv)
 
 
 def heads_to_tokens_kernel(parts, in_ref, out_ref, send, recv, lsem):
@@ -252,36 +307,10 @@
         dead = dead | ((first <= d) & (d <= last) & (l[d] == 0))
     return jnp.where(dead, 0, lo), jnp.where(dead, total, hi)
 
-def fwd_kernel(KB, QB, tok_ref, wt_ref, cos_ref, sin_ref, code_ref, out_ref, lse_ref, o32_ref, qa_ref, ka_ref, va_ref,
-               kt_ref, acc_ref):
-    T = tok_ref.shape[0]
-    CH = 512
-    hw = HW
-    code = code_ref[...]
-    lims = doc_limits(code)
-    def proj(c, _):
-        sl = pl.ds(pl.multiple_of(c*CH, CH), CH)
-        mx = nt(wt_ref[...], tok_ref[sl, :])
-        cos = cos_ref[:, sl]; sin = sin_ref[:, sl]
-        cd = code_ref[:, sl]
-        mem = jnp.where(cd >= 4.0, cd-4.0, cd)
-        hot = jnp.concatenate([jnp.where(mem == float(d), 1.0, 0.0) for d in range(3)] + [jnp.zeros((13, CH), f32)], 0)
-        neg = jnp.concatenate([jnp.where(cd == float(d), 0.0, -1e30) for d in range(3)] + [jnp.zeros((13, CH), f32)], 0)
-        zer = jnp.zeros((48, CH), f32)
-        one = jnp.concatenate([jnp.ones((1, CH), f32), jnp.zeros((63, CH), f32)], 0)
-        def rope(u):
-            a = u[:32]; b = u[32:]
-            return jnp.concatenate([a*cos - b*sin, b*cos + a*sin], 0)
-        for h in range(NH):
-            q = rope(mx[h*HEAD_DIM:(h+1)*HEAD_DIM]).astype(bf).astype(f32)*0.125
-            k = rope(mx[hw+h*HEAD_DIM:hw+(h+1)*HEAD_DIM])
-            v = mx[2*hw+h*HEAD_DIM:2*hw+(h+1)*HEAD_DIM]
-            qa_ref[h, :, sl] = jnp.concatenate([q, hot, zer], 0).astype(bf)
-            ka_ref[h, sl, :] = jnp.concatenate([k, neg, zer], 0).T.astype(bf)
-            va_ref[h, :, sl] = jnp.concatenate([v, one], 0).astype(bf)
-            kt_ref[h, :, sl] = k.astype(bf)
-        return 0
-    lax.fori_loop(0, T//CH, proj, 0)
+def fwd_kernel(KB, QB, code_ref, qa_ref, ka_ref, va_ref, out_ref, lse_ref, o32_ref, acc_ref):
+    T = code_ref.shape[1]
+    lims = doc_limits(code_ref[...])
+
     def qblock(i, _):
         a = i*QB
         qs = pl.ds(pl.multiple_of(a, QB), QB)
@@ -311,15 +340,19 @@
         return 0
     lax.fori_loop(0, T//QB, qblock, 0)
 
-def attn_fwd(tok, wt, cos, sin, code, KB=512, QB=256):
-    T = tok.shape[0]
-    return pl.pallas_call(functools.partial(fwd_kernel, KB, QB),
-        out_shape=(jax.ShapeDtypeStruct((NH*HEAD_DIM, T), bf), jax.ShapeDtypeStruct((NH, T), f32), jax.ShapeDtypeStruct((NH*HEAD_DIM, T), f32),
-                   jax.ShapeDtypeStruct((NH,128,T), bf), jax.ShapeDtypeStruct((NH,T,128), bf), jax.ShapeDtypeStruct((NH,128,T), bf), jax.ShapeDtypeStruct((NH,HEAD_DIM,T), bf)),
-        in_specs=[pl.BlockSpec(memory_space=pltpu.VMEM)]*5, out_specs=tuple([pl.BlockSpec(memory_space=pltpu.VMEM)]*7),
-        scratch_shapes=[pltpu.VMEM((NH,80,QB), f32)],
-        compiler_params=pltpu.CompilerParams(vmem_limit_bytes=VLIM), name="attn_fwd",
-        cost_estimate=pl.CostEstimate(flops=int(2*T*768*576+4*T*T*128*3), bytes_accessed=12<<20, transcendentals=T*T*3))(tok, wt, cos, sin, code)
+def attn_fwd(code, qa, ka, va, KB=512, QB=256):
+    T = code.shape[1]
+    sds = jax.ShapeDtypeStruct
+    return pl.pallas_call(
+        functools.partial(fwd_kernel, KB, QB),
+        out_shape=(sds((HW, T), bf), sds((NH, T), f32), sds((HW, T), f32)),
+        in_specs=[VM] * 4,
+        out_specs=(VM,) * 3,
+        scratch_shapes=[pltpu.VMEM((NH, 80, QB), f32)],
+        compiler_params=pltpu.CompilerParams(vmem_limit_bytes=VLIM),
+        name="attn_fwd",
+    )(code, qa, ka, va)
+
 
 def bwd_kernel(KB, QB, do_ref, o32_ref, lse_ref, qa_ref, ka_ref, va_ref, kt_ref, cos_ref, sin_ref, code_ref, g_ref,
                vn_ref, dn_ref, da_ref, qb_ref, acc_ref, dq_ref):
@@ -665,13 +698,18 @@
 
 
 def weights_kernel(
-    groups, i_ref, g_ref, h_ref, m_ref, a_ref, b_ref, in_ref,
-    sa_ref, ka_ref, sb_ref, kb_ref, heads_ref,
-    iv, it, gv, hv, mv, av, bv, gs, ds, os, isem, osem, send, recv, lsem,
+    groups, i_ref, g_ref, h_ref, m_ref, a_ref, b_ref, in_ref, gain_ref,
+    sa_ref, ka_ref, sb_ref, kb_ref, heads_ref, sum_ref,
+    iv, it, gv, hv, mv, av, bv, gs, ds, os, plane, line, isem, osem, send, recv, lsem, nsend, nrecv,
 ):
     t, p, x, y, g = here()
     peers = plane_peers()
-    greet(peers)
+    sibling = (1 - t, p)
+    others = tuple((t, lax.rem(p + SPAN * k, SPAN * groups)) for k in range(1, groups))
+    greet(peers + (sibling,) + others)
+    around = [remote(gain_ref, plane.at[i], nsend.at[i], nrecv.at[i], q) for i, q in enumerate(peers)]
+    for c in around:
+        c.start()
     tokens = in_ref.shape[1]
     me = lax.rem(p, SPAN)
     mine = pl.ds(pl.multiple_of(me * tokens, tokens), tokens)
@@ -717,8 +755,14 @@
         return 0
 
     lax.fori_loop(0, tiles, downward, 0)
-    for c in few[1:]:
+    for c in few[1:] + around:
         c.wait()
+    line[0] = (gain_ref[...] + plane[0]) + (plane[1] + plane[2])
+    ring = [
+        remote(line.at[0], line.at[1 + k], nsend.at[3 + k], nrecv.at[3 + k], q) for k, q in enumerate(others)
+    ]
+    for c in ring:
+        c.start()
     r = nn(av[0], bv[0]) + nn(av[1], bv[1])
     os[...] = r.astype(bf).reshape(shards, one, half)
     for i in range(2):
@@ -753,16 +797,26 @@
                 outs.extend(top(k))
                 for c in outs[-2:]:
                     c.start()
+    for c in ring:
+        c.wait()
+    total = line[0]
+    for k in range(1, groups):
+        total = total + line[k]
+    line[groups] = total
+    last = remote(line.at[groups], line.at[groups + 1], nsend.at[2 + groups], nrecv.at[2 + groups], sibling)
+    last.start()
     piece = fours(gs.at[2 * tiles - 1], one)
     for i, (ref, k) in enumerate(((sb_ref, 1 - y), (kb_ref, y))):
         c = put(4 * i + 2, piece.at[:, k], ref.at[:, :, pl.ds(0, one)])
         c.start()
         outs.append(c)
+    last.wait()
+    sum_ref[...] = line[groups] + line[groups + 1]
     for c in outs + moves:
         c.wait()
 
 
-def weight_grads(groups, grad_heads, inner, grads, hidden, grad_mlp, attended, grad_branch):
+def weight_grads(groups, grad_heads, gains, inner, grads, hidden, grad_mlp, attended, grad_branch):
     count, width = inner.shape[1:]
     half = width // 2
     shards = SPAN * groups
@@ -777,31 +831,35 @@
         functools.partial(weights_kernel, groups),
         out_shape=(
             part(ra), part(ra), part(rb), part(rb),
-            jax.ShapeDtypeStruct((HW, SPAN * grad_heads.shape[1]), bf),
+            jax.ShapeDtypeStruct((HW, SPAN * grad_heads.shape[1]), bf), jax.ShapeDtypeStruct(gains.shape, f32),
         ),
-        in_specs=[ANY] * 6 + [VM],
-        out_specs=(ANY,) * 5,
+        in_specs=[ANY] * 6 + [VM] * 2,
+        out_specs=(ANY,) * 5 + (VM,),
         scratch_shapes=[
             vm(2, count, width), vm(width, 2 * count), vm(2, tiles, count, width), vm(2, tiles, count, width),
             vm(2, count, half), vm(2, width, count), vm(2, count, half),
             vm(2 * tiles, shards, one, half), vm(shards, down, half), vm(shards, one, half),
+            pltpu.VMEM((3,) + gains.shape, f32), pltpu.VMEM((groups + 2,) + gains.shape, f32),
             dma_sems(4 + 2 * tiles), dma_sems(8 + 4 * tiles), dma_sems(3), dma_sems(3), dma_sems(1),
+            dma_sems(3 + groups), dma_sems(3 + groups),
         ],
         compiler_params=comm_params(2),
         name="weight_grads",
         cost_estimate=pl.CostEstimate(
             flops=int(2 * 2 * count * half * width * 8.5), bytes_accessed=30 << 20, transcendentals=0
         ),
-    )(inner, grads, hidden, grad_mlp, attended, grad_branch, grad_heads)
+    )(inner, grads, hidden, grad_mlp, attended, grad_branch, grad_heads, gains)
 
 
 def add_rows(dst, a, b, rows):
-    def step(i, _):
-        sl = pl.ds(pl.multiple_of(i * 16, 16), 16)
-        dst[sl, :] = (a[sl, :].astype(f32) + b[sl, :].astype(f32)).astype(bf)
+    step = rows // 3 if rows % 48 == 0 and rows > 48 else rows
+
+    def part(i, _):
+        sl = pl.ds(pl.multiple_of(i * step, step), step)
+        dst[sl, :] = a[sl, :] + b[sl, :]
         return 0
 
-    lax.fori_loop(0, rows // 16, step, 0)
+    lax.fori_loop(0, rows // step, part, 0)
 
 
 class Line:
@@ -869,10 +927,10 @@
 
 
 def finish_kernel(
-    groups, ka_ref, kb_ref, ra_ref, rb_ref, g_ref, tok_ref, gain_ref,
-    pair_ref, sum_ref, gm_ref, out_ref,
+    groups, ka_ref, kb_ref, ra_ref, rb_ref, wq_ref, gh_ref, g_ref, tok_ref,
+    pair_ref, tg_ref, out_ref,
     kva, kvb, rva, rvb, r2a, r2b, ua, ub, da, db, isem, s2, q2, us, ur, ds, dr,
-    plane, line, gs, gr, fs, fr,
+    gm_ref, wq, gh, wsem, fs, fr,
     w2, sib, ub2, db2, fin, send, recv, ts, tr, us2, ur2, ds2, dr2, ps, pr, lsem,
 ):
     t, p, x, y, z = here()
@@ -899,9 +957,10 @@
         for c in range(2):
             for d in loads(c, zt):
                 d.start()
+    more = (pltpu.make_async_copy(wq_ref, wq, wsem.at[0]), pltpu.make_async_copy(gh_ref, gh, wsem.at[1]))
+    for c in more:
+        c.start()
     greet(peers + across + (sibling,) + tuple(others))
-    for i, peer in enumerate(peers):
-        remote(gain_ref, plane.at[i], gs.at[i], gr.at[i], peer).start()
 
     def second(c, zt):
         peer, kr, rr, kv, rv, r2, u, d, mine = colours[c]
@@ -950,12 +1009,6 @@
             peer, kr, rr, kv, rv, r2, u, d, mine = colours[c]
             keep = rv.at[zt, mine]
             add_rows(keep, keep, kv.at[zt, mine], size(c))
-    for i, peer in enumerate(peers):
-        remote(gain_ref, plane.at[i], gs.at[i], gr.at[i], peer).wait()
-    line[0] = (gain_ref[...] + plane[0]) + (plane[1] + plane[2])
-    ring = [remote(line.at[0], line.at[1 + k], gs.at[3 + k], gr.at[3 + k], peer) for k, peer in enumerate(others)]
-    for c in ring:
-        c.start()
 
     def in_plane(zt):
         for c in range(2):
@@ -1000,14 +1053,6 @@
             relay(order[i - 1], 1)
             for k in range(2):
                 chain2(order[i - 1], k).relay(1, one)
-    for c in ring:
-        c.wait()
-    total = line[0]
-    for k in range(1, groups):
-        total = total + line[k]
-    line[groups] = total
-    both = remote(line.at[groups], line.at[groups + 1], gs.at[2 + groups], gr.at[2 + groups], sibling)
-    both.start()
     for hop in range(1, groups - 1):
         for i, zt in enumerate(order):
             if hop > 1 or i == groups - 1:
@@ -1037,8 +1082,10 @@
             chain(c, zt).finish(pair_ref.at[t, sl], size(c))
     last = remote(pair_ref.at[t], pair_ref.at[t], fs.at[0], fr.at[0], sibling)
     last.start()
-    both.wait()
-    sum_ref[...] = line[groups] + line[groups + 1]
+    for c in copies + list(more):
+        c.wait()
+    turned = nn(wq[...], gm_ref[...]).T
+    tg_ref[...] = gh[...] + turned
     for s in range(SPAN):
         from_here = jnp.logical_and(s == me, y == t)
         pl.when(jnp.logical_not(from_here))(
@@ -1056,12 +1103,10 @@
         for c in range(2):
             second(c, zt).wait_send()
             chain(c, zt).drain()
-    for c in copies:
-        c.wait()
     last.wait()
 
 
-def finish(ka, kb, ra, rb, g, tok, gains, groups):
+def finish(ka, kb, ra, rb, wq, gh, g, tok, groups):
     width = tok.shape[1]
     count = tok.shape[0] // SPAN
     one = width // (SPAN * groups)
@@ -1073,20 +1118,19 @@
         functools.partial(finish_kernel, groups),
         out_shape=(
             jax.ShapeDtypeStruct((2, na + nb, half), bf),
-            jax.ShapeDtypeStruct(gains.shape, f32),
-            jax.ShapeDtypeStruct((3 * width, count), bf),
+            jax.ShapeDtypeStruct((count, width), f32),
             jax.ShapeDtypeStruct((SPAN, one, 3 * HW), bf),
         ),
-        in_specs=[ANY] * 4 + [VM] * 3,
-        out_specs=(VM, VM, ANY, VM),
+        in_specs=[ANY] * 6 + [VM] * 2,
+        out_specs=(VM,) * 3,
         scratch_shapes=[
             buf(groups, 2, na, half), buf(groups, 2, nb, half), buf(groups, 2, na, half), buf(groups, 2, nb, half),
             buf(groups, na, half), buf(groups, nb, half), buf(groups, na, half), buf(groups, nb, half),
             buf(groups, na, half), buf(groups, nb, half),
             dma_sems(4 * groups), dma_sems(2 * groups), dma_sems(2 * groups),
             dma_sems(2 * groups), dma_sems(2 * groups), dma_sems(2 * groups), dma_sems(2 * groups),
-            pltpu.VMEM((3,) + gains.shape, f32), pltpu.VMEM((groups + 2,) + gains.shape, f32),
-            dma_sems(3 + groups), dma_sems(3 + groups), dma_sems(1), dma_sems(1),
+            buf(3 * width, count), buf(width, 3 * width), pltpu.VMEM((count, width), f32), dma_sems(2),
+            dma_sems(1), dma_sems(1),
             mix(SPAN * groups), mix(groups, 2), mix(groups, 2), mix(groups, 2), mix(2),
             dma_sems(9), dma_sems(9), dma_sems(groups), dma_sems(groups),
             dma_sems(2 * groups), dma_sems(2 * groups), dma_sems(2 * groups), dma_sems(2 * groups),
@@ -1094,7 +1138,42 @@
         ],
         compiler_params=comm_params(3),
         name="finish",
-    )(ka, kb, ra, rb, g, tok, gains)
+    )(ka, kb, ra, rb, wq, gh, g, tok)
+
+
+def unfold_kernel(pair_ref, part_ref, gate_ref, up_ref, down_ref, out_ref, qkv_ref):
+    one = out_ref.shape[0]
+    half = pair_ref.shape[2]
+    steps = gate_ref.shape[1] // half
+    down = down_ref.shape[0]
+    for j in range(steps):
+        for k, ref in enumerate((gate_ref, up_ref)):
+            ref[:, j * half : (j + 1) * half] = pair_ref[k, j * one : (j + 1) * one, :].astype(f32)
+    top = (steps - 1) * one
+    for k in range(2):
+        cols = slice(k * half, (k + 1) * half)
+        down_ref[:, cols] = pair_ref[k, top + one : top + one + down, :].astype(f32)
+        out_ref[:, cols] = pair_ref[k, top + one + down :, :].astype(f32)
+    for k in range(3):
+        row = [part_ref[s, :, k * HW : (k + 1) * HW].astype(f32) for s in range(SPAN)]
+        qkv_ref[:, k * SPAN * HW : (k + 1) * SPAN * HW] = jnp.concatenate(row, 1)
+
+
+def unfold(pair, parts, tiles):
+    one = parts.shape[1]
+    half = pair.shape[2]
+    width = 2 * half
+    sds = jax.ShapeDtypeStruct
+    return pl.pallas_call(
+        unfold_kernel,
+        out_shape=(
+            sds((one, tiles * width), f32), sds((one, tiles * width), f32), sds((tiles * one, width), f32),
+            sds((one, width), f32), sds((one, 3 * width), f32),
+        ),
+        in_specs=[VM] * 2,
+        out_specs=(VM,) * 5,
+        name="unfold",
+    )(pair, parts)
 
 
 def angle_tables(total):
@@ -1125,11 +1204,9 @@
     live = pad_mask[0] == 1
     code = jnp.where(live, member_of, member_of + 4).astype(f32)[None, :]
     docs = groups * DOCS_GRP
-    cols = [lax.dynamic_slice_in_dim(w_qkv, k * width + me * HW, HW, 1) for k in range(3)]
-    w_mine = jnp.concatenate(cols, 1).T
     cos, sin = angle_tables(SPAN * count)
-    tok_all, codes = gather(rows, code)
-    heads_out, lse, exact, qa, ka, va, kt = attn_fwd(tok_all, w_mine, cos, sin, codes)
+    tok_all, codes, qa, ka, va, kt = gather(rows, code, cos, sin, w_qkv)
+    heads_out, lse, exact = attn_fwd(codes, qa, ka, va)
     norms = jnp.stack([ln1_gain, ln1_bias, ln2_gain, ln2_bias] + [jnp.zeros_like(ln1_gain)] * 4, 0)
     (
         attended, inner, hidden, grad_mlp, grads, grad_branch, grad_attended, grad_h1, gains, scores_all, loss
@@ -1137,8 +1214,8 @@
     scores = scores_all.reshape(groups, 8, groups, 8)[:, :DOCS_GRP, :, :DOCS_GRP].reshape(docs, docs)
     by_hand = width % (16 * places) == 0
     if by_hand:
-        send_a, keep_a, send_b, keep_b, d_heads = weight_grads(
-            groups, grad_attended, inner, grads, hidden, grad_mlp, attended, grad_branch
+        send_a, keep_a, send_b, keep_b, d_heads, gain_sums = weight_grads(
+            groups, grad_attended, gains, inner, grads, hidden, grad_mlp, attended, grad_branch
         )
         exchange = lambda v, bit: lax.ppermute(v, "dp", [(i, i ^ bit) for i in range(places)])
         came_a, came_b = exchange(send_a, 1), exchange(send_b, 2)
@@ -1146,23 +1223,12 @@
         d_heads = tokens_to_heads(grad_attended, 5, "to_heads")
     mixed = attn_bwd(d_heads, exact, lse, qa, ka, va, kt, cos, sin, codes)
     if by_hand:
-        half = width // 2
         one = width // places
-        down = w_down.shape[0] // places
-        pair, gain_sums, grad_mixed, qkv_parts = finish(
-            keep_a, keep_b, came_a, came_b, mixed, tok_all, gains, groups
+        gains_out = lax.dynamic_slice_in_dim(gain_sums[:4], place * one, one, 1)
+        pair, token_grad, qkv_parts = finish(
+            keep_a, keep_b, came_a, came_b, w_qkv, grad_h1, mixed, tok_all, groups
         )
-        top = pair.shape[1] - down - one
-        unfold = lambda v: v.reshape(top // one, one, half).transpose(1, 0, 2).reshape(one, -1)
-        sides = lambda v: jnp.concatenate([v[0], v[1]], 1).astype(f32)
-        gate_out = unfold(pair[0, :top]).astype(f32)
-        up_out = unfold(pair[1, :top]).astype(f32)
-        down_out = sides(pair[:, top : top + down])
-        out_out = sides(pair[:, top + down :])
-        gains_out = lax.dynamic_slice_in_dim(gain_sums[:4], place * one, one, 1)
-        qkv_out = (
-            qkv_parts.reshape(SPAN, one, 3, HW).transpose(1, 2, 0, 3).reshape(one, 3 * width).astype(f32)
-        )
+        gate_out, up_out, down_out, out_out, qkv_out = unfold(pair, qkv_parts, w_gate.shape[1] // width)
     else:
         grad_mixed = heads_to_tokens(mixed, 6, "to_tokens_back")
         qkv_out = spread_sum(tn(rows, grad_mixed.T))
@@ -1175,9 +1241,9 @@
         gate_out, up_out = two[0], two[1]
         down_out = halves(both(flat(hidden), grad_mlp))
         gains_out = spread_sum(gains[:4].T).T
-    token_grad = grad_h1 + lax.dot_general(
-        grad_mixed, w_qkv, (((0,), (1,)), ((), ())), preferred_element_type=f32
-    )
+        token_grad = grad_h1 + lax.dot_general(
+            grad_mixed, w_qkv, (((0,), (1,)), ((), ())), preferred_element_type=f32
+        )
     return (
         scores, loss[0, 0], token_grad[None], qkv_out, out_out, gains_out[0], gains_out[1],
         gate_out, up_out, down_out, gains_out[2], gains_out[3],

time: 276 us -> 265 us (0.960)
  matrix products: 6.35 us -> 0 us
  local copies, waits for them, and re-layouts: 15 us -> 9.36 us
  Pallas kernels: 238 us -> 242 us
    dot_general x1 -> x0, matrix products: 6.35 us -> none  [local(): lax.dot_general(grad_mixed, w_qkv, (((0,), (1,)), ((), ())), preferred_el...]
    convert_element_type x5 -> x0, local copies, waits for them, and re-layouts: 3.58 us -> none  [the longest x3 1.87 us: local(): qkv_parts.reshape(SPAN, one, 3, HW).transpose(1, 2, 0, 3)]
    pallas_call x2 -> x3, Pallas kernels: 54.6 us -> 55.9 us  [the longest x1 32 us: gather(): pl.pallas_call(gather_kernel, out_shape=(jax.ShapeDtypeStruct((total, wid...]
  transfers between devices with their start and end apart: 2 -> 2, of which waited for: 2 -> 2; matrix products, arithmetic and copies ran while one was open for 1% -> 1% of each run, Pallas kernels for 11% -> 12%
where the time goes in v4:
time: 265 us
  Pallas kernels  242 us (91%)
  waiting for transfers between devices  9.78 us (4%)
  local copies, waits for them, and re-layouts  9.36 us (4%)
    pallas_call x1, Pallas kernels, finish(): pl.pallas_call(functools.partial(finish_kernel, groups), out_shape=(jax.S...  79.1 us
    pallas_call x1, Pallas kernels, block(): pl.pallas_call(functools.partial(block_kernel, groups), out_shape=(sds((2...  55.8 us
    pallas_call x1, Pallas kernels, attn_bwd(): pl.pallas_call(functools.partial(bwd_kernel, KB, QB), out_shape=jax.Shape...  32.1 us
    pallas_call x1, Pallas kernels, gather(): pl.pallas_call(gather_kernel, out_shape=(jax.ShapeDtypeStruct((total, wid...  32 us
    pallas_call x1, Pallas kernels, attn_fwd(): pl.pallas_call(functools.partial(fwd_kernel, KB, QB), out_shape=(sds((HW,...  21.3 us
    pallas_call x1, Pallas kernels, weight_grads(): pl.pallas_call(functools.partial(weights_kernel, groups), out_shape=(part...  19.1 us
    ppermute x2, waiting for transfers between devices, local(): lax.ppermute(v, 'dp', [(i, i ^ bit) for i in range(places)])  9.78 us
  transfers between devices with their start and end apart: 2, of which 2 were waited for; matrix products, arithmetic and copies ran while one was open for 1% of the time, Pallas kernels for 12%

profile of v4, /device:TPU:25, one launch (start us, length us, event | category | flops | bytes accessed | tf_op | source)
XLA Modules:
  0.0 265.0 jit_solution(13065000581482661065)
XLA Ops:
  0.6 0.7 stack.18
  1.3 0.7 stack.19
  2.0 0.7 stack.20
  2.7 0.7 stack.21
  3.4 1.3 fusion.code_ref
  4.7 32.0 %gather.1 = (bf16[2048,768]{1,0:T(8,128)(2,1)}, f32[1,2048]{1,0:T(1,128)}, bf16[3,128,2048]{2,1,0:T(8,128)(2,1)}, bf16[3,2048,128]{2,1,0:T(8,128)(2,1)}, bf16[3,...) custom-call(bf16[512,768]{1,0:T(8,128)(2,1)} %bitcast.11, f32[1,512]{1,0:T(1,128)} %fusion.code_ref, ...), custom_call_target="tpu_custom_call" | custom-call | tf_op jit(solution)/shard_map/gather/pallas_call | solution.py:188
  36.7 21.3 %attn_fwd.1 = (bf16[192,2048]{1,0:T(8,128)(2,1)}, f32[3,2048]{1,0:T(4,128)}, f32[192,2048]{1,0:T(8,128)}) custom-call(f32[1,2048]{1,0:T(1,128)} %get-tuple-element.46.code_ref, bf16[3,128,2048]{2,1,0:T(8,128)(2,1)} %get-tuple-element.47.qa_ref, bf16[3,2048,128]{2,1,0:T(8,128)(2,1)} %get-tuple-element.48.ka_ref, bf16[3,128,2048]{2,1,0:T(8,128)(2,1)} %get-tuple-element.49.va_ref), custom_call_target="tpu_custom_call" | custom-call | tf_op jit(solution)/shard_map/attn_fwd/pallas_call | solution.py:346
  57.9 0.6 stack.23.norms_ref
  58.6 55.8 %block.1 = (bf16[2,768,512]{2,1,0:T(8,128)(2,1)}, bf16[2,512,768]{2,1,0:T(8,128)(2,1)}, bf16[2,4,512,768]{3,2,1,0:T(8,128)(2,1)}, bf16[2,512,384]{2,1,0:T(8,128)...) custom-call(bf16[192,2048]{1,0:T(8,128)(2,1)} %get-tuple-element.50., ...), custom_call_target="tpu_custom_call" | custom-call | tf_op jit(solution)/shard_map/block/pallas_call | solution.py:675
  114.4 19.1 %weight_grads.1 = (bf16[4,2,336,384]{3,2,1,0:T(8,128)(2,1)}, bf16[4,2,336,384]{3,2,1,0:T(8,128)(2,1)}, bf16[4,2,288,384]{3,2,1,0:T(8,128)(2,1)}, bf16[4,2,288,38...) custom-call(bf16[2,512,768]{2,1,0:T(8,128)(2,1)} %get-tuple-element.53.i_ref, ...), custom_call_target="tpu_custom_call" | custom-call | flops 5133828096 | bytes 31457280 | tf_op jit(solution)/shard_map/weight_grads/pallas_call | solution.py:830
  133.5 1.7 collective-permute-start
  135.2 0.1 collective-permute-start.1
  135.3 0.7 slice.23
  136.0 0.1 constant_dynamic-slice_fusion
  136.1 0.1 reshape.30
  136.2 0.7 reshape.31
  136.9 1.2 slice.22
  138.1 0.5 slice_bitcast_fusion
  138.6 32.1 %attn_bwd.1.g_ref = bf16[576,2048]{1,0:T(8,128)(2,1)} custom-call(bf16[192,2048]{1,0:T(8,128)(2,1)} %get-tuple-element.66.do_ref, f32[192,2048]{1,0:T(8,128)} %get-tuple-element.67.o32_ref, f32[3,2048]{1,0:T(4,128)} %get-tuple-element.68.lse_ref, bf16[3,128,2048]{2,1,0:T(8,128)(2,1)} %get-tuple-element.47.qa_ref, ...), custom_call_target="tpu_custom_call" | custom-call | flops 16106127360 | bytes 12582912 | tf_op jit(solution)/shard_map/attn_bwd/pallas_call | solution.py:421
  170.7 4.4 %collective-permute-done.1.rb_ref = bf16[4,2,288,384]{3,2,1,0:T(8,128)(2,1)S(1)} collective-permute-done((bf16[4,2,288,384]{3,2,1,0:T(8,128)(2,1)}, bf16[4,2,288,384]{3,2,1,0:T(8,128)(2,1)S(1)}, u32[]{:S(2)}, u32[]{:S(2)}) %collective-permute-start.1) | collective-permute-done | bytes 1769504 | tf_op jit(solution)/shard_map/ppermute | solution.py:1220
  175.1 5.4 %collective-permute-done.ra_ref = bf16[4,2,336,384]{3,2,1,0:T(8,128)(2,1)} collective-permute-done((bf16[4,2,336,384]{3,2,1,0:T(8,128)(2,1)}, bf16[4,2,336,384]{3,2,1,0:T(8,128)(2,1)}, u32[]{:S(2)}, u32[]{:S(2)}) %collective-permute-start) | collective-permute-done | bytes 2064416 | tf_op jit(solution)/shard_map/ppermute | solution.py:1220
  180.5 79.1 %finish.1 = (bf16[2,624,384]{2,1,0:T(8,128)(2,1)}, f32[512,768]{1,0:T(8,128)}, bf16[4,48,576]{2,1,0:T(8,128)(2,1)}) custom-call(bf16[4,2,336,384]{3,2,1,0:T(8,128)(2,1)} %get-tuple-element.61.ka_ref, bf16[4,2,288,384]{3,2,1,0:T(8,128)(2,1)} %get-tuple-element.62.kb_ref, bf16[4,2,336,384]{3,2,1,0:T(8,128)(2,1)} %collective-permute-done.ra_ref, ...), custom_call_target="tpu_custom_call" | custom-call | tf_op jit(solution)/shard_map/finish/pallas_call | solution.py:1117
  259.6 2.7 %unfold.1 = (f32[48,3072]{1,0:T(8,128)}, f32[48,3072]{1,0:T(8,128)}, f32[192,768]{1,0:T(8,128)}, f32[48,768]{1,0:T(8,128)}, f32[48,2304]{1,0:T(8,128)}) custom-call(bf16[2,624,384]{2,1,0:T(8,128)(2,1)} %get-tuple-element.72.pair_ref, bf16[4,48,576]{2,1,0:T(8,128)(2,1)} %get-tuple-element.73.part_ref), custom_call_target="tpu_custom_call" | custom-call | tf_op jit(solution)/shard_map/unfold/pallas_call | solution.py:1167
  262.3 2.7 %copy.28 = f32[1,512,768]{2,1,0:T(8,128)} copy(f32[1,512,768]{2,1,0:T(8,128)} %bitcast.13) | data formatting | bytes 3145728
  (6 shorter events, 0.0 us)
Async XLA Ops:
  114.4 21.7 %copy-start.1 = (f32[32,32]{1,0:T(8,128)S(1)}, f32[32,32]{1,0:T(8,128)}, u32[]{:S(2)}) copy-start(f32[32,32]{1,0:T(8,128)} %get-tuple-element.51) | copy-start | bytes 12292
  133.5 47.0 %collective-permute-start = (bf16[4,2,336,384]{3,2,1,0:T(8,128)(2,1)}, bf16[4,2,336,384]{3,2,1,0:T(8,128)(2,1)}, u32[]{:S(2)}, u32[]{:S(2)}) collective-permute-start(bf16[4,2,336,384]{3,2,1,0:T(8,128)(2,1)} %get-tuple-element.63), channel_id=1, source_target_pairs={{0,1},{1,0},{2,3},{3,2},{4,5},{5,4},{6,7},{7,6},{8,9},{9,8},{10,11... | collective-permute-start | bytes 6193160 | tf_op jit(solution)/shard_map/ppermute | solution.py:1220
  135.2 40.0 %collective-permute-start.1 = (bf16[4,2,288,384]{3,2,1,0:T(8,128)(2,1)}, bf16[4,2,288,384]{3,2,1,0:T(8,128)(2,1)S(1)}, u32[]{:S(2)}, u32[]{:S(2)}) collective-permute-start(bf16[4,2,288,384]{3,2,1,0:T(8,128)(2,1)} %get-tuple-element.64), channel_id=1, source_target_pairs={{0,2},{1,3},{2,0},{3,1},{4,6},{5,7},{6,4},{7,5},{8,10},{9,11},{10,... | collective-permute-start | bytes 5308424 | tf_op jit(solution)/shard_map/ppermute | solution.py:1220
  175.1 5.4 %copy-start = (bf16[4,2,288,384]{3,2,1,0:T(8,128)(2,1)}, bf16[4,2,288,384]{3,2,1,0:T(8,128)(2,1)S(1)}, u32[]{:S(2)}) copy-start(bf16[4,2,288,384]{3,2,1,0:T(8,128)(2,1)S(1)} %collective-permute-done.1.rb_ref) | copy-start | bytes 5308420

commit v5 on v4

--- a/solution.py
+++ b/solution.py
@@ -14,7 +14,7 @@
 DOCS_GRP = 3
 NH = HEADS // SPAN
 HW = NH * HEAD_DIM
-CHUNK = 512
+UPWARD = 3
 VLIM = 62 * 2**20
 MESH = pl.DeviceIdType.MESH
 f32 = jnp.float32
@@ -82,8 +82,8 @@
 
 
 def gather_kernel(
-    tok_ref, code_ref, cos_ref, sin_ref, w_ref, out_ref, codes_ref, qa_ref, ka_ref, va_ref, kt_ref,
-    toks, codes, wraw, wturn, wt, qa, ka, va, kt, send, recv, csend, crecv, wsem, osem,
+    tok_ref, ids_ref, pads_ref, cos_ref, sin_ref, w_ref, out_ref, codes_ref, qa_ref, ka_ref, va_ref, kt_ref,
+    toks, code_ref, codes, wraw, wturn, wt, qa, ka, va, kt, send, recv, csend, crecv, wsem, osem,
 ):
     t, p, x, y, g = here()
     count, width = tok_ref.shape
@@ -96,6 +96,7 @@
         at = pl.multiple_of(k * width + me * HW - odd * HEAD_DIM, 128)
         loads.append(pltpu.make_async_copy(w_ref.at[:, pl.ds(at, wide)], wraw.at[k], wsem.at[k]))
         loads[-1].start()
+    code_ref[...] = lax.rem(ids_ref[...], DOCS_GRP).astype(f32) + 4.0 * (1 - pads_ref[...]).astype(f32)
     ex, ey, ed = plane_peers()
     mx, my, md = (lax.rem(q[1], SPAN) for q in (ex, ey, ed))
 
@@ -181,7 +182,7 @@
         c.wait()
 
 
-def gather(tok, code, cos, sin, w_qkv):
+def gather(tok, ids, pads, cos, sin, w_qkv):
     count, width = tok.shape
     total = SPAN * count
     shapes = ((NH, 128, total), (NH, total, 128), (NH, 128, total), (NH, HEAD_DIM, total))
@@ -189,17 +190,17 @@
         gather_kernel,
         out_shape=(jax.ShapeDtypeStruct((total, width), bf), jax.ShapeDtypeStruct((1, total), f32))
         + tuple(jax.ShapeDtypeStruct(s, bf) for s in shapes),
-        in_specs=[VM] * 4 + [ANY],
+        in_specs=[VM] * 5 + [ANY],
         out_specs=(ANY, VM) + (ANY,) * 4,
         scratch_shapes=[
-            pltpu.VMEM((total, width), bf), pltpu.VMEM((1, total), f32), pltpu.VMEM((3, width, 256), bf),
+            pltpu.VMEM((total, width), bf), pltpu.VMEM((1, count), f32), pltpu.VMEM((1, total), f32), pltpu.VMEM((3, width, 256), bf),
             pltpu.VMEM((256, width), bf), pltpu.VMEM((3 * HW, width), bf),
         ]
         + [pltpu.VMEM(s, bf) for s in shapes]
         + [dma_sems(6), dma_sems(6), dma_sems(3), dma_sems(3), dma_sems(3), dma_sems(20)],
         compiler_params=comm_params(0),
         name="gather",
-    )(tok, code, cos, sin, w_qkv)
+    )(tok, ids, pads, cos, sin, w_qkv)
 
 
 def heads_to_tokens_kernel(parts, in_ref, out_ref, send, recv, lsem):
@@ -307,40 +308,61 @@
         dead = dead | ((first <= d) & (d <= last) & (l[d] == 0))
     return jnp.where(dead, 0, lo), jnp.where(dead, total, hi)
 
-def fwd_kernel(KB, QB, code_ref, qa_ref, ka_ref, va_ref, out_ref, lse_ref, o32_ref, acc_ref):
+def fwd_kernel(KB, QB, code_ref, qa_ref, ka_ref, va_ref, out_ref, lse_ref, o32_ref, acc_ref, even_ref, odd_ref):
     T = code_ref.shape[1]
+    blocks = T // KB
     lims = doc_limits(code_ref[...])
 
+    def keys(j):
+        return pl.ds(pl.multiple_of(j * KB, KB), KB)
+
     def qblock(i, _):
-        a = i*QB
+        a = i * QB
         qs = pl.ds(pl.multiple_of(a, QB), QB)
         lo, hi = block_range(lims, a, QB, T)
-        jlo = lo//KB; jhi = (hi+KB-1)//KB
+        jlo = lo // KB
+        pairs = ((hi + KB - 1) // KB - jlo + 1) // 2
+        jlo = jnp.minimum(jlo, blocks - 2 * pairs)
+
+        def scores(j, h, ref):
+            ref[h] = nn(ka_ref[h, keys(j), :], qa_ref[h, :, qs])
+
+        def absorb(j, h, ref, m):
+            s = ref[h]
+            mn = jnp.maximum(m, jnp.max(s, 0, keepdims=True))
+            p = jnp.exp(s - mn).astype(bf)
+            acc_ref[h] = acc_ref[h] * jnp.exp(m - mn) + nn(va_ref[h, :80, keys(j)], p)
+            return mn
+
         for h in range(NH):
             acc_ref[h] = jnp.zeros_like(acc_ref[h])
-        def kv(j, ms):
-            ks = pl.ds(pl.multiple_of(j*KB, KB), KB)
-            new = []
-            ss = [nn(ka_ref[h, ks, :], qa_ref[h, :, qs]) for h in range(NH)]
+            scores(jlo, h, even_ref)
+
+        def kv(n, ms):
+            j = jlo + 2 * n
+            ms = list(ms)
             for h in range(NH):
-                s = ss[h]
-                mn = jnp.maximum(ms[h], jnp.max(s, 0, keepdims=True))
-                p = jnp.exp(s - mn).astype(bf)
-                al = jnp.exp(ms[h]-mn)
-                acc_ref[h] = acc_ref[h]*al + nn(va_ref[h, :80, ks], p)
-                new.append(mn)
-            return tuple(new)
-        ms = lax.fori_loop(jlo, jhi, kv, tuple(jnp.full((1, QB), -3e38, f32) for _ in range(NH)))
+                scores(j + 1, h, odd_ref)
+                ms[h] = absorb(j, h, even_ref, ms[h])
+            after = jnp.minimum(j + 2, blocks - 1)
+            for h in range(NH):
+                scores(after, h, even_ref)
+                ms[h] = absorb(j + 1, h, odd_ref, ms[h])
+            return tuple(ms)
+
+        ms = lax.fori_loop(0, pairs, kv, tuple(jnp.full((1, QB), -3e38, f32) for _ in range(NH)))
         for h in range(NH):
             tot = acc_ref[h, 64:65, :]
-            o = acc_ref[h, :64, :]/tot
-            o32_ref[h*HEAD_DIM:(h+1)*HEAD_DIM, qs] = o
-            lse_ref[h:h+1, qs] = jnp.where(ms[h] < -1e29, 0.0, ms[h] + jnp.log(tot))
-            out_ref[h*HEAD_DIM:(h+1)*HEAD_DIM, qs] = o.astype(bf)
+            o = acc_ref[h, :64, :] / tot
+            o32_ref[h * HEAD_DIM : (h + 1) * HEAD_DIM, qs] = o
+            lse_ref[h : h + 1, qs] = jnp.where(ms[h] < -1e29, 0.0, ms[h] + jnp.log(tot))
+            out_ref[h * HEAD_DIM : (h + 1) * HEAD_DIM, qs] = o.astype(bf)
         return 0
-    lax.fori_loop(0, T//QB, qblock, 0)
-
-def attn_fwd(code, qa, ka, va, KB=512, QB=256):
+
+    lax.fori_loop(0, T // QB, qblock, 0)
+
+
+def attn_fwd(code, qa, ka, va, KB=256, QB=512):
     T = code.shape[1]
     sds = jax.ShapeDtypeStruct
     return pl.pallas_call(
@@ -348,7 +370,7 @@
         out_shape=(sds((HW, T), bf), sds((NH, T), f32), sds((HW, T), f32)),
         in_specs=[VM] * 4,
         out_specs=(VM,) * 3,
-        scratch_shapes=[pltpu.VMEM((NH, 80, QB), f32)],
+        scratch_shapes=[pltpu.VMEM((NH, 80, QB), f32)] + [pltpu.VMEM((NH, KB, QB), f32)] * 2,
         compiler_params=pltpu.CompilerParams(vmem_limit_bytes=VLIM),
         name="attn_fwd",
     )(code, qa, ka, va)
@@ -485,7 +507,7 @@
 
 
 def block_kernel(
-    groups, heads_ref, rows_ref, code_ref, goals_ref, norms_ref, wo_h, wg_h, wu_h, wd_h,
+    groups, heads_ref, rows_ref, codes_ref, goals_ref, gain1_ref, bias1_ref, gain2_ref, bias2_ref, wo_h, wg_h, wu_h, wd_h,
     att_o, inner_o, hid_o, gm_o, gg_o, gb_o, ga_o, gh1_o, gains_o, scores_o, loss_o,
     att, wo, wg, wu, wd, inner, x1, s1, acc, hid, ab, x2, s2, sec, gm, gm2, gb, gb2, plane, allp, ge,
     wsem, send, recv, lsem, tsend, trecv, osem, csend, crecv,
@@ -523,7 +545,7 @@
     ))
     for c in moves:
         c.start()
-    code = code_ref[...]
+    code = codes_ref[:, pl.ds(pl.multiple_of(me * count, count), count)]
     zero = jnp.zeros((8 - DOCS_GRP, count), f32)
     mem = jnp.concatenate([jnp.where(code == float(d), 1.0, 0.0) for d in range(DOCS_GRP)] + [zero], 0)
     mem = jnp.concatenate([mem, mem, mem, jnp.zeros((8, count), f32)], 0).astype(bf)
@@ -544,8 +566,7 @@
     both(0, att, att, att_o)
     acc[...] = tn(att[...], wo[...])
     step = 64
-    gain1, bias1 = norms_ref[0:1, :], norms_ref[1:2, :]
-    gain2, bias2 = norms_ref[2:3, :], norms_ref[3:4, :]
+    gain1, bias1, gain2, bias2 = (r[...].reshape(1, width) for r in (gain1_ref, bias1_ref, gain2_ref, bias2_ref))
 
     def chunk(i):
         return pl.ds(pl.multiple_of(i * step, step), step)
@@ -664,7 +685,7 @@
             d.wait()
 
 
-def block(heads, rows, code, goals, norms, w_out, w_gate, w_up, w_down, groups):
+def block(heads, rows, codes, goals, norms, w_out, w_gate, w_up, w_down, groups):
     count, width = rows.shape
     tiles = w_gate.shape[1] // width
     half = width // 2
@@ -680,7 +701,7 @@
             sds((width, count), bf), sds((count, width), f32), sds((8, width), f32),
             sds((size, size), f32), sds((8, 128), f32),
         ),
-        in_specs=[VM, VM, VM, pl.BlockSpec(memory_space=pltpu.SMEM), VM] + [ANY] * 4,
+        in_specs=[VM, VM, VM, pl.BlockSpec(memory_space=pltpu.SMEM)] + [VM] * 4 + [ANY] * 4,
         out_specs=(ANY,) * 6 + (VM,) * 5,
         scratch_shapes=[
             vm(width, count), vm(width, width), vm(tiles, width, width), vm(tiles, width, width),
@@ -694,15 +715,16 @@
         ],
         compiler_params=comm_params(1),
         name="block",
-    )(heads, rows, code, goals, norms, w_out, w_gate, w_up, w_down)
+    )(heads, rows, codes, goals, *norms, w_out, w_gate, w_up, w_down)
 
 
 def weights_kernel(
     groups, i_ref, g_ref, h_ref, m_ref, a_ref, b_ref, in_ref, gain_ref,
-    sa_ref, ka_ref, sb_ref, kb_ref, heads_ref, sum_ref,
+    sa_ref, ka_ref, sb_ref, kb_ref, sc_ref, kc_ref, heads_ref, sum_ref,
     iv, it, gv, hv, mv, av, bv, gs, ds, os, plane, line, isem, osem, send, recv, lsem, nsend, nrecv,
 ):
     t, p, x, y, g = here()
+    level = lax.rem(g, 2)
     peers = plane_peers()
     sibling = (1 - t, p)
     others = tuple((t, lax.rem(p + SPAN * k, SPAN * groups)) for k in range(1, groups))
@@ -774,17 +796,25 @@
 
     outs = []
     for i, (ref, k) in enumerate(((sb_ref, 1 - y), (kb_ref, y))):
-        outs.append(put(4 * i, fours(ds, down).at[:, k], ref.at[:, :, pl.ds(one, down)]))
-        outs.append(put(4 * i + 1, fours(os, one).at[:, k], ref.at[:, :, pl.ds(one + down, one)]))
+        outs.append(put(4 * i, fours(ds, down).at[:, k], ref.at[:, :, pl.ds(0, down)]))
+        outs.append(put(4 * i + 1, fours(os, one).at[:, k], ref.at[:, :, pl.ds(down, one)]))
     for c in outs:
         c.start()
 
+    sideways = sa_ref.shape[2] // one
+
     def top(j):
-        rows = pl.ds(pl.multiple_of(j * one, one), one)
-        piece = fours(gs.at[j], one)
+        if j < sideways:
+            rows = pl.ds(j * one, one)
+            piece = fours(gs.at[j], one)
+            went, kept = (piece.at[:, :, 1 - x], sa_ref), (piece.at[:, :, x], ka_ref)
+        else:
+            rows = pl.ds((j - sideways) * one, one)
+            piece = gs.at[j].reshape(groups // 2, 2, SPAN, one, half)
+            went, kept = (piece.at[:, 1 - level], sc_ref), (piece.at[:, level], kc_ref)
         return (
-            put(8 + j, piece.at[:, :, 1 - x], sa_ref.at[:, :, rows]),
-            put(8 + 2 * tiles + j, piece.at[:, :, x], ka_ref.at[:, :, rows]),
+            put(8 + j, went[0], went[1].at[:, :, rows]),
+            put(8 + 2 * tiles + j, kept[0], kept[1].at[:, :, rows]),
         )
 
     for j in range(tiles):
@@ -793,10 +823,9 @@
         for h in range(2):
             k = 2 * j + h
             gs[k] = r[:, h * half : (h + 1) * half].reshape(shards, one, half)
-            if k < 2 * tiles - 1:
-                outs.extend(top(k))
-                for c in outs[-2:]:
-                    c.start()
+            outs.extend(top(k))
+            for c in outs[-2:]:
+                c.start()
     for c in ring:
         c.wait()
     total = line[0]
@@ -805,11 +834,6 @@
     line[groups] = total
     last = remote(line.at[groups], line.at[groups + 1], nsend.at[2 + groups], nrecv.at[2 + groups], sibling)
     last.start()
-    piece = fours(gs.at[2 * tiles - 1], one)
-    for i, (ref, k) in enumerate(((sb_ref, 1 - y), (kb_ref, y))):
-        c = put(4 * i + 2, piece.at[:, k], ref.at[:, :, pl.ds(0, one)])
-        c.start()
-        outs.append(c)
     last.wait()
     sum_ref[...] = line[groups] + line[groups + 1]
     for c in outs + moves:
@@ -823,18 +847,19 @@
     one = width // shards
     tiles = grads.shape[1]
     down = tiles * one
-    ra = (2 * tiles - 1) * one
-    rb = down + 2 * one
+    ra = (2 * tiles - UPWARD) * one
+    rb = down + one
     part = lambda r: jax.ShapeDtypeStruct((groups, 2, r, half), bf)
+    level = jax.ShapeDtypeStruct((groups // 2, SPAN, UPWARD * one, half), bf)
     vm = lambda *n: pltpu.VMEM(n, bf)
     return pl.pallas_call(
         functools.partial(weights_kernel, groups),
         out_shape=(
-            part(ra), part(ra), part(rb), part(rb),
+            part(ra), part(ra), part(rb), part(rb), level, level,
             jax.ShapeDtypeStruct((HW, SPAN * grad_heads.shape[1]), bf), jax.ShapeDtypeStruct(gains.shape, f32),
         ),
         in_specs=[ANY] * 6 + [VM] * 2,
-        out_specs=(ANY,) * 5 + (VM,),
+        out_specs=(ANY,) * 7 + (VM,),
         scratch_shapes=[
             vm(2, count, width), vm(width, 2 * count), vm(2, tiles, count, width), vm(2, tiles, count, width),
             vm(2, count, half), vm(2, width, count), vm(2, count, half),
@@ -927,10 +952,10 @@
 
 
 def finish_kernel(
-    groups, ka_ref, kb_ref, ra_ref, rb_ref, wq_ref, gh_ref, g_ref, tok_ref,
+    groups, ka_ref, kb_ref, kc_ref, ra_ref, rb_ref, rc_ref, wq_ref, gh_ref, gin_ref, tin_ref,
     pair_ref, tg_ref, out_ref,
-    kva, kvb, rva, rvb, r2a, r2b, ua, ub, da, db, isem, s2, q2, us, ur, ds, dr,
-    gm_ref, wq, gh, wsem, fs, fr,
+    kvc, rvc, r2c, r3c, r4c, csem, cs, cr, kva, kvb, rva, rvb, r2a, r2b, ua, ub, da, db, isem, s2, q2, us, ur, ds, dr,
+    gm_ref, wq, gh, g_ref, tok_ref, wsem, fs, fr,
     w2, sib, ub2, db2, fin, send, recv, ts, tr, us2, ur2, ds2, dr2, ps, pr, lsem,
 ):
     t, p, x, y, z = here()
@@ -953,10 +978,21 @@
             pltpu.make_async_copy(rr.at[zt], rv.at[zt], isem.at[i + 1]),
         )
 
-    for zt in order:
+    level_loads = [
+        [pltpu.make_async_copy(a.at[i], b.at[i], csem.at[2 * i + j]) for j, (a, b) in enumerate(((kc_ref, kvc), (rc_ref, rvc)))]
+        for i in range(2)
+    ]
+    for pair in level_loads:
+        for d in pair:
+            d.start()
+    mixed_loads = (pltpu.make_async_copy(gin_ref, g_ref, wsem.at[2]), pltpu.make_async_copy(tin_ref, tok_ref, wsem.at[3]))
+    for i, zt in enumerate(order):
         for c in range(2):
             for d in loads(c, zt):
                 d.start()
+        if i == 1:
+            for c in mixed_loads:
+                c.start()
     more = (pltpu.make_async_copy(wq_ref, wq, wsem.at[0]), pltpu.make_async_copy(gh_ref, gh, wsem.at[1]))
     for c in more:
         c.start()
@@ -976,17 +1012,67 @@
     def size(c):
         return colours[c][3].shape[2]
 
-    for zt in order:
+    up = kvc.shape[2]
+
+    def third(i, k):
+        at = (k * 2 + 1 - x, (1 - y) * 2 + k)[i]
+        n = 2 * i + k
+        return remote(rvc.at[i, at], r2c.at[i, k], cs.at[n], cr.at[n], (ex, ey)[i])
+
+    def fourth(i):
+        at = (1 - y, 1 - x)[i]
+        return remote(r2c.at[i, at], r3c.at[i], cs.at[4 + i], cr.at[4 + i], (ey, ex)[i])
+
+    top = lax.div(z, 2)
+    fifth = remote(r3c.at[1 - top], r4c, cs.at[6], cr.at[6], (t, p + 2 * SPAN - 4 * SPAN * top))
+
+    def plus(dst, src, n):
+        add_rows(dst, dst, src, n)
+
+    def send_second(zt):
         for c in range(2):
             for d in loads(c, zt):
                 d.wait()
             peer, kr, rr, kv, rv, r2, u, d, mine = colours[c]
-            away = rv.at[zt, 1 - mine]
-            add_rows(away, away, kv.at[zt, 1 - mine], size(c))
+            plus(rv.at[zt, 1 - mine], kv.at[zt, 1 - mine], size(c))
             second(c, zt).start()
+
+    for i in range(2):
+        for d in level_loads[i]:
+            d.wait()
+        for k in range(2):
+            at = (k * 2 + 1 - x, (1 - y) * 2 + k)[i]
+            plus(rvc.at[i, at], kvc.at[i, at], up)
+            third(i, k).start()
+    send_second(order[0])
+    send_second(order[1])
+    width = gm_ref.shape[0] // 3
+    shards = SPAN * groups
+    one = width // shards
+    half = width // 2
+    for c in mixed_loads:
+        c.wait()
+    for h in range(2):
+        r = nn(g_ref[...], tok_ref[:, h * half : (h + 1) * half]).T
+        w2[h * (shards // 2) : (h + 1) * (shards // 2)] = r.astype(bf).reshape(shards // 2, one, 3 * HW)
+
+    def swap(zt):
+        return remote(w2.at[pl.ds(zt * 4 + (1 - t) * 2, 2)], sib.at[zt], ts.at[zt], tr.at[zt], sibling)
+
+    for zt in order:
+        swap(zt).start()
+
+    for i in range(2):
+        for k in range(2):
+            at = (k * 2 + x, y * 2 + k)[i]
+            plus(rvc.at[i, at], kvc.at[i, at], up)
+            third(i, k).wait_recv()
+            plus(r2c.at[i, k], rvc.at[i, at], up)
+        fourth(i).start()
+    send_second(order[2])
+    send_second(order[3])
     count = gm_ref.shape[1]
     me = lax.rem(p, SPAN)
-    width = gm_ref.shape[0] // 3
     copies = []
     for i, peer in enumerate((peers[2], peers[0], peers[1])):
         m = lax.rem(peer[1], SPAN)
@@ -1004,6 +1090,17 @@
         ))
     for c in copies:
         c.start()
+    def chain2(zt, k):
+        i = zt * 2 + k
+        return Line(z, zt, groups, sib.at[zt, k], ub2.at[zt, k], db2.at[zt, k],
+                    (us2.at[i], ur2.at[i], ds2.at[i], dr2.at[i]), t, p)
+
+    for zt in order:
+        swap(zt).wait_recv()
+        for k in range(2):
+            dst = sib.at[zt, k]
+            add_rows(dst, dst, w2.at[zt * 4 + t * 2 + k], one)
+            chain2(zt, k).start()
     for zt in order:
         for c in range(2):
             peer, kr, rr, kv, rv, r2, u, d, mine = colours[c]
@@ -1022,43 +1119,28 @@
         for c in range(2):
             chain(c, zt).relay(hop, size(c))
 
+
+    def relay2(hop):
+        for zt in order:
+            for k in range(2):
+                chain2(zt, k).relay(hop, one)
+
     in_plane(order[0])
-    shards = SPAN * groups
-    one = width // shards
-    half = width // 2
-    for h in range(2):
-        r = nn(g_ref[...], tok_ref[:, h * half : (h + 1) * half]).T
-        w2[h * (shards // 2) : (h + 1) * (shards // 2)] = r.astype(bf).reshape(shards // 2, one, 3 * HW)
-
-    def swap(zt):
-        return remote(w2.at[pl.ds(zt * 4 + (1 - t) * 2, 2)], sib.at[zt], ts.at[zt], tr.at[zt], sibling)
-
-    for zt in order:
-        swap(zt).start()
-
-    def chain2(zt, k):
-        i = zt * 2 + k
-        return Line(z, zt, groups, sib.at[zt, k], ub2.at[zt, k], db2.at[zt, k],
-                    (us2.at[i], ur2.at[i], ds2.at[i], dr2.at[i]), t, p)
-
-    for i, zt in enumerate(order):
-        if i >= 1:
-            in_plane(zt)
-        swap(zt).wait_recv()
-        for k in range(2):
-            dst = sib.at[zt, k]
-            add_rows(dst, dst, w2.at[zt * 4 + t * 2 + k], one)
-            chain2(zt, k).start()
-        if i >= 1:
-            relay(order[i - 1], 1)
-            for k in range(2):
-                chain2(order[i - 1], k).relay(1, one)
-    for hop in range(1, groups - 1):
-        for i, zt in enumerate(order):
-            if hop > 1 or i == groups - 1:
-                relay(zt, hop)
-                for k in range(2):
-                    chain2(zt, k).relay(hop, one)
+    relay2(1)
+    in_plane(order[1])
+    for i in range(2):
+        fourth(i).wait_recv()
+        plus(r3c.at[i], r2c.at[i, (y, x)[i]], up)
+    fifth.start()
+    relay(order[0], 1)
+    relay2(2)
+    in_plane(order[2])
+    relay(order[1], 1)
+    in_plane(order[3])
+    relay(order[0], 2)
+    relay(order[2], 1)
+    relay(order[1], 2)
+    relay(order[3], 1)
     for zt in order:
         for k in range(2):
             chain2(zt, k).finish(fin.at[k], one)
@@ -1077,6 +1159,8 @@
             away, stay, same = hand(k, tt)
             pl.when(jnp.logical_not(same))(lambda away=away: away().start())
             pl.when(same)(lambda stay=stay: stay().start())
+    fifth.wait_recv()
+    add_rows(pair_ref.at[t, pl.ds(size(0) + size(1), up)], r3c.at[top], r4c, up)
     for zt in order:
         for c, sl in ((0, pl.ds(0, size(0))), (1, pl.ds(size(0), size(1)))):
             chain(c, zt).finish(pair_ref.at[t, sl], size(c))
@@ -1103,33 +1187,41 @@
         for c in range(2):
             second(c, zt).wait_send()
             chain(c, zt).drain()
+    for i in range(2):
+        for k in range(2):
+            third(i, k).wait_send()
+        fourth(i).wait_send()
+    fifth.wait_send()
     last.wait()
 
 
-def finish(ka, kb, ra, rb, wq, gh, g, tok, groups):
+def finish(ka, kb, kc, ra, rb, rc, wq, gh, g, tok, groups):
     width = tok.shape[1]
     count = tok.shape[0] // SPAN
     one = width // (SPAN * groups)
-    na, nb = ka.shape[2], kb.shape[2]
+    na, nb, nc = ka.shape[2], kb.shape[2], kc.shape[2]
     half = ka.shape[3]
     buf = lambda *n: pltpu.VMEM(n, bf)
     mix = lambda *n: pltpu.VMEM(n + (one, 3 * HW), bf)
     return pl.pallas_call(
         functools.partial(finish_kernel, groups),
         out_shape=(
-            jax.ShapeDtypeStruct((2, na + nb, half), bf),
+            jax.ShapeDtypeStruct((2, na + nb + nc, half), bf),
             jax.ShapeDtypeStruct((count, width), f32),
             jax.ShapeDtypeStruct((SPAN, one, 3 * HW), bf),
         ),
-        in_specs=[ANY] * 6 + [VM] * 2,
+        in_specs=[ANY] * 10,
         out_specs=(VM,) * 3,
         scratch_shapes=[
+            buf(2, SPAN, nc, half), buf(2, SPAN, nc, half), buf(2, 2, nc, half), buf(2, nc, half), buf(nc, half),
+            dma_sems(4), dma_sems(7), dma_sems(7),
             buf(groups, 2, na, half), buf(groups, 2, nb, half), buf(groups, 2, na, half), buf(groups, 2, nb, half),
             buf(groups, na, half), buf(groups, nb, half), buf(groups, na, half), buf(groups, nb, half),
             buf(groups, na, half), buf(groups, nb, half),
             dma_sems(4 * groups), dma_sems(2 * groups), dma_sems(2 * groups),
             dma_sems(2 * groups), dma_sems(2 * groups), dma_sems(2 * groups), dma_sems(2 * groups),
-            buf(3 * width, count), buf(width, 3 * width), pltpu.VMEM((count, width), f32), dma_sems(2),
+            buf(3 * width, count), buf(width, 3 * width), pltpu.VMEM((count, width), f32),
+            buf(*g.shape), buf(*tok.shape), dma_sems(4),
             dma_sems(1), dma_sems(1),
             mix(SPAN * groups), mix(groups, 2), mix(groups, 2), mix(groups, 2), mix(2),
             dma_sems(9), dma_sems(9), dma_sems(groups), dma_sems(groups),
@@ -1138,42 +1230,65 @@
         ],
         compiler_params=comm_params(3),
         name="finish",
-    )(ka, kb, ra, rb, wq, gh, g, tok)
-
-
-def unfold_kernel(pair_ref, part_ref, gate_ref, up_ref, down_ref, out_ref, qkv_ref):
+    )(ka, kb, kc, ra, rb, rc, wq, gh, g, tok)
+
+
+def unfold_kernel(
+    groups, pair_ref, part_ref, grad_ref, score_ref, gain_ref, lost_ref,
+    gate_ref, up_ref, down_ref, out_ref, qkv_ref, token_ref, scores_ref, loss_ref, *gains_refs,
+):
     one = out_ref.shape[0]
     half = pair_ref.shape[2]
+    width = 2 * half
     steps = gate_ref.shape[1] // half
     down = down_ref.shape[0]
+    token_ref[0] = grad_ref[...]
+    top = (steps - UPWARD) * one
     for j in range(steps):
+        at = j * one + (0 if j < steps - UPWARD else down + one)
         for k, ref in enumerate((gate_ref, up_ref)):
-            ref[:, j * half : (j + 1) * half] = pair_ref[k, j * one : (j + 1) * one, :].astype(f32)
-    top = (steps - 1) * one
+            ref[:, j * half : (j + 1) * half] = pair_ref[k, at : at + one, :].astype(f32)
     for k in range(2):
         cols = slice(k * half, (k + 1) * half)
-        down_ref[:, cols] = pair_ref[k, top + one : top + one + down, :].astype(f32)
-        out_ref[:, cols] = pair_ref[k, top + one + down :, :].astype(f32)
+        down_ref[:, cols] = pair_ref[k, top : top + down, :].astype(f32)
+        out_ref[:, cols] = pair_ref[k, top + down : top + down + one, :].astype(f32)
     for k in range(3):
         row = [part_ref[s, :, k * HW : (k + 1) * HW].astype(f32) for s in range(SPAN)]
-        qkv_ref[:, k * SPAN * HW : (k + 1) * SPAN * HW] = jnp.concatenate(row, 1)
-
-
-def unfold(pair, parts, tiles):
+        qkv_ref[:, k * width : (k + 1) * width] = jnp.concatenate(row, 1)
+    docs, size = scores_ref.shape[0], score_ref.shape[0]
+    dot = functools.partial(lax.dot_general, precision=precise, preferred_element_type=f32)
+    row = lax.broadcasted_iota(jnp.int32, (docs, size), 0)
+    col = lax.broadcasted_iota(jnp.int32, (docs, size), 1)
+    pick = jnp.where(row // DOCS_GRP * 8 + lax.rem(row, DOCS_GRP) == col, 1.0, 0.0)
+    some = dot(pick, score_ref[...], (((1,), (0,)), ((), ())))
+    scores_ref[...] = dot(some, pick, (((1,), (1,)), ((), ())))
+    row = lax.broadcasted_iota(jnp.int32, (width, one), 0)
+    col = lax.broadcasted_iota(jnp.int32, (width, one), 1)
+    mine = jnp.where(row == lax.axis_index("dp") * one + col, 1.0, 0.0)
+    gains = dot(gain_ref[...], mine, (((1,), (0,)), ((), ())))
+    for k, ref in enumerate(gains_refs):
+        ref[...] = gains[k : k + 1, :]
+    loss_ref[...] = lost_ref[0:1, 0:1]
+
+
+def unfold(pair, parts, grad, scores, gains, loss, tiles, groups):
     one = parts.shape[1]
     half = pair.shape[2]
     width = 2 * half
+    docs = groups * DOCS_GRP
     sds = jax.ShapeDtypeStruct
     return pl.pallas_call(
-        unfold_kernel,
+        functools.partial(unfold_kernel, groups),
         out_shape=(
             sds((one, tiles * width), f32), sds((one, tiles * width), f32), sds((tiles * one, width), f32),
-            sds((one, width), f32), sds((one, 3 * width), f32),
-        ),
-        in_specs=[VM] * 2,
-        out_specs=(VM,) * 5,
+            sds((one, width), f32), sds((one, 3 * width), f32), sds((1,) + grad.shape, f32),
+            sds((docs, docs), f32), sds((1, 1), f32),
+        )
+        + (sds((1, one), f32),) * 4,
+        in_specs=[VM] * 6,
+        out_specs=(VM,) * 12,
         name="unfold",
-    )(pair, parts)
+    )(pair, parts, grad, scores, gains, loss)
 
 
 def angle_tables(total):
@@ -1200,35 +1315,32 @@
     tower = lax.axis_index("tower")
     place = lax.axis_index("dp")
     me = place % SPAN
-    member_of = doc_ids[0] % DOCS_GRP
-    live = pad_mask[0] == 1
-    code = jnp.where(live, member_of, member_of + 4).astype(f32)[None, :]
     docs = groups * DOCS_GRP
     cos, sin = angle_tables(SPAN * count)
-    tok_all, codes, qa, ka, va, kt = gather(rows, code, cos, sin, w_qkv)
+    tok_all, codes, qa, ka, va, kt = gather(rows, doc_ids, pad_mask, cos, sin, w_qkv)
     heads_out, lse, exact = attn_fwd(codes, qa, ka, va)
-    norms = jnp.stack([ln1_gain, ln1_bias, ln2_gain, ln2_bias] + [jnp.zeros_like(ln1_gain)] * 4, 0)
+    norms = (ln1_gain, ln1_bias, ln2_gain, ln2_bias)
     (
         attended, inner, hidden, grad_mlp, grads, grad_branch, grad_attended, grad_h1, gains, scores_all, loss
-    ) = block(heads_out, rows, code, targets, norms, w_out, w_gate, w_up, w_down, groups)
-    scores = scores_all.reshape(groups, 8, groups, 8)[:, :DOCS_GRP, :, :DOCS_GRP].reshape(docs, docs)
-    by_hand = width % (16 * places) == 0
+    ) = block(heads_out, rows, codes, targets, norms, w_out, w_gate, w_up, w_down, groups)
+    by_hand = groups == 4 and width % (16 * places) == 0
     if by_hand:
-        send_a, keep_a, send_b, keep_b, d_heads, gain_sums = weight_grads(
+        send_a, keep_a, send_b, keep_b, send_c, keep_c, d_heads, gain_sums = weight_grads(
             groups, grad_attended, gains, inner, grads, hidden, grad_mlp, attended, grad_branch
         )
         exchange = lambda v, bit: lax.ppermute(v, "dp", [(i, i ^ bit) for i in range(places)])
-        came_a, came_b = exchange(send_a, 1), exchange(send_b, 2)
+        came_a, came_b, came_c = exchange(send_a, 1), exchange(send_b, 2), exchange(send_c, SPAN)
     else:
         d_heads = tokens_to_heads(grad_attended, 5, "to_heads")
     mixed = attn_bwd(d_heads, exact, lse, qa, ka, va, kt, cos, sin, codes)
     if by_hand:
-        one = width // places
-        gains_out = lax.dynamic_slice_in_dim(gain_sums[:4], place * one, one, 1)
-        pair, token_grad, qkv_parts = finish(
-            keep_a, keep_b, came_a, came_b, w_qkv, grad_h1, mixed, tok_all, groups
+        pair, grad_tokens, qkv_parts = finish(
+            keep_a, keep_b, keep_c, came_a, came_b, came_c, w_qkv, grad_h1, mixed, tok_all, groups
         )
-        gate_out, up_out, down_out, out_out, qkv_out = unfold(pair, qkv_parts, w_gate.shape[1] // width)
+        gate_out, up_out, down_out, out_out, qkv_out, token_grad, scores, loss, *gains_out = unfold(
+            pair, qkv_parts, grad_tokens, scores_all, gain_sums, loss, w_gate.shape[1] // width, groups
+        )
+        gains_out = [v.reshape(-1) for v in gains_out]
     else:
         grad_mixed = heads_to_tokens(mixed, 6, "to_tokens_back")
         qkv_out = spread_sum(tn(rows, grad_mixed.T))
@@ -1241,11 +1353,13 @@
         gate_out, up_out = two[0], two[1]
         down_out = halves(both(flat(hidden), grad_mlp))
         gains_out = spread_sum(gains[:4].T).T
+        scores = scores_all.reshape(groups, 8, groups, 8)[:, :DOCS_GRP, :, :DOCS_GRP].reshape(docs, docs)
         token_grad = grad_h1 + lax.dot_general(
             grad_mixed, w_qkv, (((0,), (1,)), ((), ())), preferred_element_type=f32
         )
+        token_grad = token_grad[None]
     return (
-        scores, loss[0, 0], token_grad[None], qkv_out, out_out, gains_out[0], gains_out[1],
+        scores, loss[0, 0], token_grad, qkv_out, out_out, gains_out[0], gains_out[1],
         gate_out, up_out, down_out, gains_out[2], gains_out[3],
     )
 

time: 265 us -> 231 us (0.87); the launches traced: 265 us -> 226 us
  Pallas kernels: 242 us -> 215 us
  local copies, waits for them, and re-layouts: 9.36 us -> 0.07 us
    pallas_call x1, Pallas kernels: 79.1 us -> 61.8 us  [finish(): pl.pallas_call(functools.partial(finish_kernel, groups), out_shape=(jax.S...]
    pallas_call x1, Pallas kernels: 32.1 us -> 24.5 us  [attn_bwd(): pl.pallas_call(functools.partial(bwd_kernel, KB, QB), out_shape=jax.Shape...]
    pallas_call x1, Pallas kernels: 21.3 us -> 14.6 us  [attn_fwd(): pl.pallas_call(functools.partial(fwd_kernel, KB, QB), out_shape=(sds((HW,...]
    another operation x6 -> x0, local copies, waits for them, and re-layouts: 3.4 us -> none  [local(): jnp.stack([ln1_gain, ln1_bias, ln2_gain, ln2_bias] + [jnp.zeros_like(ln1_...]
    ppermute x2 -> x3, waiting for transfers between devices: 9.78 us -> 8.79 us  [local(): lax.ppermute(v, 'dp', [(i, i ^ bit) for i in range(places)])]
  transfers between devices with their start and end apart: 2 -> 3, of which waited for: 2 -> 2; matrix products, arithmetic and copies ran while one was open for 1% -> 0% of each run, Pallas kernels for 12% -> 11%
where the time goes in v5:
time: 231 us; the launch traced here: 226 us
  Pallas kernels  215 us (93%)
  waiting for transfers between devices  8.79 us (4%)
    pallas_call x1, Pallas kernels, finish(): pl.pallas_call(functools.partial(finish_kernel, groups), out_shape=(jax.S...  61.8 us
    pallas_call x1, Pallas kernels, block(): pl.pallas_call(functools.partial(block_kernel, groups), out_shape=(sds((2...  58.3 us
    pallas_call x1, Pallas kernels, gather(): pl.pallas_call(gather_kernel, out_shape=(jax.ShapeDtypeStruct((total, wid...  32 us
    pallas_call x1, Pallas kernels, attn_bwd(): pl.pallas_call(functools.partial(bwd_kernel, KB, QB), out_shape=jax.Shape...  24.5 us
    pallas_call x1, Pallas kernels, weight_grads(): pl.pallas_call(functools.partial(weights_kernel, groups), out_shape=(part...  19.1 us
    pallas_call x1, Pallas kernels, attn_fwd(): pl.pallas_call(functools.partial(fwd_kernel, KB, QB), out_shape=(sds((HW,...  14.6 us
    ppermute x3, waiting for transfers between devices, local(): lax.ppermute(v, 'dp', [(i, i ^ bit) for i in range(places)])  8.79 us
  transfers between devices with their start and end apart: 3, of which 2 were waited for; matrix products, arithmetic and copies ran while one was open for 0% of the time, Pallas kernels for 11%

profile of v5, /device:TPU:25, one launch (start us, length us, event | category | flops | bytes accessed | tf_op | source)
XLA Modules:
  0.0 226.2 jit_solution(6900745142903476903)
XLA Ops:
  0.6 32.0 %gather.1 = (bf16[2048,768]{1,0:T(8,128)(2,1)}, f32[1,2048]{1,0:T(1,128)}, bf16[3,128,2048]{2,1,0:T(8,128)(2,1)}, bf16[3,2048,128]{2,1,0:T(8,128)(2,1)}, bf16[3,...) custom-call(bf16[512,768]{1,0:T(8,128)(2,1)} %bitcast.6, s32[1,512]{1,0:T(1,128)} %ids_ref.1, s32[1,512]{1,0:T(1,128)} %pads_ref.1, ...), custom_call_target="tpu_custom_call" | custom-call | tf_op jit(solution)/shard_map/gather/pallas_call | solution.py:189
  32.6 14.6 %attn_fwd.1 = (bf16[192,2048]{1,0:T(8,128)(2,1)}, f32[3,2048]{1,0:T(4,128)}, f32[192,2048]{1,0:T(8,128)}) custom-call(f32[1,2048]{1,0:T(1,128)} %get-tuple-element.55.code_ref.codes_ref, bf16[3,128,2048]{2,1,0:T(8,128)(2,1)} %get-tuple-element.56.qa_ref, bf16[3,2048,128]{2,1,0:T(8,128)(2,1)} %get-tuple-element.57.ka_ref, ...), custom_call_target="tpu_custom_call" | custom-call | tf_op jit(solution)/shard_map/attn_fwd/pallas_call | solution.py:368
  47.2 58.3 %block.1 = (bf16[2,768,512]{2,1,0:T(8,128)(2,1)}, bf16[2,512,768]{2,1,0:T(8,128)(2,1)}, bf16[2,4,512,768]{3,2,1,0:T(8,128)(2,1)}, bf16[2,512,384]{2,1,0:T(8,128)...) custom-call(bf16[192,2048]{1,0:T(8,128)(2,1)} %get-tuple-element.59., ...), custom_call_target="tpu_custom_call" | custom-call | tf_op jit(solution)/shard_map/block/pallas_call | solution.py:696
  105.5 19.1 %weight_grads.1 = (bf16[4,2,240,384]{3,2,1,0:T(8,128)(2,1)}, bf16[4,2,240,384]{3,2,1,0:T(8,128)(2,1)}, bf16[4,2,240,384]{3,2,1,0:T(8,128)(2,1)}, bf16[4,2,240,38...) custom-call(bf16[2,512,768]{2,1,0:T(8,128)(2,1)} %get-tuple-element., ...), custom_call_target="tpu_custom_call" | custom-call | flops 5133828096 | bytes 31457280 | tf_op jit(solution)/shard_map/weight_grads/pallas_call | solution.py:855
  124.6 0.4 collective-permute-start.2
  125.0 1.6 collective-permute-start
  126.6 0.0 collective-permute-start.1
  126.6 24.5 %attn_bwd.1.gin_ref = bf16[576,2048]{1,0:T(8,128)(2,1)} custom-call(bf16[192,2048]{1,0:T(8,128)(2,1)} %get-tuple-element.75.do_ref, f32[192,2048]{1,0:T(8,128)} %get-tuple-element.76.o32_ref, f32[3,2048]{1,0:T(4,128)} %get-tuple-element.77.lse_ref, bf16[3,128,2048]{2,1,0:T(8,128)(2,1)} %get-tuple-element.56.qa_ref, ...), custom_call_target="tpu_custom_call" | custom-call | flops 16106127360 | bytes 12582912 | tf_op jit(solution)/shard_map/attn_bwd/pallas_call | solution.py:443
  151.1 0.0 collective-permute-done.2.rc_ref
  151.1 7.8 %collective-permute-done.ra_ref = bf16[4,2,240,384]{3,2,1,0:T(8,128)(2,1)S(1)} collective-permute-done((bf16[4,2,240,384]{3,2,1,0:T(8,128)(2,1)}, bf16[4,2,240,384]{3,2,1,0:T(8,128)(2,1)S(1)}, u32[]{:S(2)}, u32[]{:S(2)}) %collective-permute-start) | collective-permute-done | bytes 1474592 | tf_op jit(solution)/shard_map/ppermute | solution.py:1331
  158.9 0.0 copy-start
  158.9 1.0 collective-permute-done.1.rb_ref
  159.9 0.1 copy-done
  160.0 61.8 %finish.1 = (bf16[2,624,384]{2,1,0:T(8,128)(2,1)}, f32[512,768]{1,0:T(8,128)}, bf16[4,48,576]{2,1,0:T(8,128)(2,1)}) custom-call(bf16[4,2,240,384]{3,2,1,0:T(8,128)(2,1)} %get-tuple-element.68.ka_ref, bf16[4,2,240,384]{3,2,1,0:T(8,128)(2,1)} %get-tuple-element.69.kb_ref, bf16[2,4,144,384]{3,2,1,0:T(8,128)(2,1)} %get-tuple-element.70.kc_ref, ...), custom_call_target="tpu_custom_call" | custom-call | tf_op jit(solution)/shard_map/finish/pallas_call | solution.py:1206
  221.8 4.2 %unfold.1 = (f32[48,3072]{1,0:T(8,128)}, f32[48,3072]{1,0:T(8,128)}, f32[192,768]{1,0:T(8,128)}, f32[48,768]{1,0:T(8,128)}, f32[48,2304]{1,0:T(8,128)}, /*index=...) custom-call(bf16[2,624,384]{2,1,0:T(8,128)(2,1)} %get-tuple-element., ...), custom_call_target="tpu_custom_call" | custom-call | tf_op jit(solution)/shard_map/unfold/pallas_call | solution.py:1280
Async XLA Ops:
  124.6 26.5 %collective-permute-start.2 = (bf16[2,4,144,384]{3,2,1,0:T(8,128)(2,1)}, bf16[2,4,144,384]{3,2,1,0:T(8,128)(2,1)}, u32[]{:S(2)}, u32[]{:S(2)}) collective-permute-start(bf16[2,4,144,384]{3,2,1,0:T(8,128)(2,1)} %get-tuple-element.73), channel_id=1, source_target_pairs={{0,4},{1,5},{2,6},{3,7},{4,0},{5,1},{6,2},{7,3},{8,12},{9,13},{10,... | collective-permute-start | bytes 2654216 | tf_op jit(solution)/shard_map/ppermute | solution.py:1331
  125.0 33.8 %collective-permute-start = (bf16[4,2,240,384]{3,2,1,0:T(8,128)(2,1)}, bf16[4,2,240,384]{3,2,1,0:T(8,128)(2,1)S(1)}, u32[]{:S(2)}, u32[]{:S(2)}) collective-permute-start(bf16[4,2,240,384]{3,2,1,0:T(8,128)(2,1)} %get-tuple-element.71), channel_id=1, source_target_pairs={{0,1},{1,0},{2,3},{3,2},{4,5},{5,4},{6,7},{7,6},{8,9},{9,8},{10,11... | collective-permute-start | bytes 4423688 | tf_op jit(solution)/shard_map/ppermute | solution.py:1331
  126.6 33.3 %collective-permute-start.1 = (bf16[4,2,240,384]{3,2,1,0:T(8,128)(2,1)}, bf16[4,2,240,384]{3,2,1,0:T(8,128)(2,1)}, u32[]{:S(2)}, u32[]{:S(2)}) collective-permute-start(bf16[4,2,240,384]{3,2,1,0:T(8,128)(2,1)} %get-tuple-element.72), channel_id=1, source_target_pairs={{0,2},{1,3},{2,0},{3,1},{4,6},{5,7},{6,4},{7,5},{8,10},{9,11},{10,... | collective-permute-start | bytes 4423688 | tf_op jit(solution)/shard_map/ppermute | solution.py:1331
  158.9 1.1 copy-start

commit v6 on v5

--- a/solution.py
+++ b/solution.py
@@ -83,7 +83,9 @@
 
 def gather_kernel(
     tok_ref, ids_ref, pads_ref, cos_ref, sin_ref, w_ref, out_ref, codes_ref, qa_ref, ka_ref, va_ref, kt_ref,
-    toks, code_ref, codes, wraw, wturn, wt, qa, ka, va, kt, send, recv, csend, crecv, wsem, osem,
+    att_ref, lse_ref, exact_ref,
+    toks, code_ref, codes, wraw, wturn, wt, qa, ka, va, kt, acc, tops, sooner, later, heads,
+    send, recv, csend, crecv, wsem, osem, asend, arecv, asem,
 ):
     t, p, x, y, g = here()
     count, width = tok_ref.shape
@@ -159,6 +161,67 @@
             c.start()
         return puts
 
+    part = count // 2
+    acc[...] = jnp.zeros_like(acc)
+    tops[...] = jnp.full_like(tops, -3e38)
+    chunks = (me, mx, my, md)
+    inside = jnp.where((me == 1) | (me == 2), 1, 0)
+
+    def pick(n, values):
+        got = values[-1]
+        for i in reversed(range(len(values) - 1)):
+            got = jnp.where(n == i, values[i], got)
+        return got
+
+    def segment(q, key_of, trips):
+        qs = whole(q)
+
+        def keys(n, k):
+            return pl.ds(pl.multiple_of(key_of(n) * count + k * part, part), part)
+
+        def scores(n, k, h, ref):
+            ref[h] = nn(ka[h, keys(n, k), :], qa[h, :, qs])
+
+        def absorb(n, k, h, ref, m):
+            s = ref[h]
+            mn = jnp.maximum(m, jnp.max(s, 0, keepdims=True))
+            pr = jnp.exp(s - mn).astype(bf)
+            acc[q, h] = acc[q, h] * jnp.exp(m - mn) + nn(va[h, :80, keys(n, k)], pr)
+            return mn
+
+        for h in range(NH):
+            scores(0, 0, h, sooner)
+
+        def step(n, ms):
+            ms = list(ms)
+            for h in range(NH):
+                scores(n, 1, h, later)
+                ms[h] = absorb(n, 0, h, sooner, ms[h])
+            after = jnp.minimum(n + 1, jnp.maximum(trips - 1, 0))
+            for h in range(NH):
+                scores(after, 0, h, sooner)
+                ms[h] = absorb(n, 1, h, later, ms[h])
+            return tuple(ms)
+
+        ms = lax.fori_loop(0, trips, step, tuple(tops[q * NH + h] for h in range(NH)))
+        for h in range(NH):
+            tops[q * NH + h] = ms[h]
+
+    def finalize(q):
+        qs = whole(q)
+        edge = jnp.where((q == 0) | (q == SPAN - 1), 1.0, 0.0)
+        other = whole(SPAN - 1 - q)
+        for h in range(NH):
+            m = tops[q * NH + h]
+            rest = jnp.sum(va[h, :80, other].astype(f32), 1, keepdims=True)
+            full = acc[q, h] + rest * jnp.where(m < -1e29, edge, 0.0)
+            tot = full[64:65]
+            o = full[:64] / tot
+            at = pl.ds(h * HEAD_DIM, HEAD_DIM)
+            exact_ref[at, qs] = o
+            lse_ref[h : h + 1, qs] = jnp.where(m < -1e29, 0.0, m + jnp.log(tot))
+            heads[at, qs] = o.astype(bf)
+
     done = project(tok_ref, me, 0)
     first[0].wait_recv()
     f0 = remote(toks.at[rows(mx, 0)], toks.at[rows(mx, 0)], send.at[4], recv.at[4], ey)
@@ -166,20 +229,54 @@
     first[1].wait_recv()
     f1 = remote(toks.at[rows(my, 1)], toks.at[rows(my, 1)], send.at[5], recv.at[5], ex)
     f1.start()
+    segment(me, lambda n: me, 1)
     for c in small:
         c.wait()
     first[2].wait_recv()
     done += project(toks.at[whole(mx)], mx, 1)
     first[3].wait_recv()
     done += project(toks.at[whole(my)], my, 2)
+
+    def near(s, _):
+        q = pick(s, chunks[:3])
+        key_of = lambda n: pick(s, (pick(n, (mx, my)), pick(n, (me, mx, my)), pick(n, (me, my, mx))))
+        segment(q, key_of, jnp.where(s == 0, 2, 3 - inside))
+        return 0
+
+    lax.fori_loop(0, 3, near, 0)
     f0.wait_recv()
     f1.wait_recv()
     done += project(toks.at[whole(md)], md, 3)
+
+    def back(s):
+        peer = (ed, ex, ey)[s]
+        m = (md, mx, my)[s]
+        return remote(
+            heads.at[:, whole(m)], att_ref.at[pl.ds(pl.multiple_of(me * HW, HW), HW)], asend.at[s], arecv.at[s], peer
+        )
+
+    def far(s, _):
+        q = pick(s, (md, mx, my, me))
+        key_of = lambda n: jnp.where(s == 0, pick(n, (mx, my, md, me)), md)
+        segment(q, key_of, pick(s, (3 + inside, 1, 1, inside)))
+        finalize(q)
+        for k in range(3):
+            pl.when(s == k)(lambda k=k: back(k).start())
+        return 0
+
+    lax.fori_loop(0, 4, far, 0)
+    own = pltpu.make_async_copy(
+        heads.at[:, whole(me)], att_ref.at[pl.ds(pl.multiple_of(me * HW, HW), HW)], asem.at[0]
+    )
+    own.start()
     codes_ref[...] = codes[...]
     for c in first + [f0, f1]:
         c.wait_send()
     for c in done:
         c.wait()
+    own.wait()
+    for k in range(3):
+        back(k).wait()
 
 
 def gather(tok, ids, pads, cos, sin, w_qkv):
@@ -189,15 +286,25 @@
     return pl.pallas_call(
         gather_kernel,
         out_shape=(jax.ShapeDtypeStruct((total, width), bf), jax.ShapeDtypeStruct((1, total), f32))
-        + tuple(jax.ShapeDtypeStruct(s, bf) for s in shapes),
+        + tuple(jax.ShapeDtypeStruct(s, bf) for s in shapes)
+        + (
+            jax.ShapeDtypeStruct((SPAN * HW, count), bf), jax.ShapeDtypeStruct((NH, total), f32),
+            jax.ShapeDtypeStruct((HW, total), f32),
+        ),
         in_specs=[VM] * 5 + [ANY],
-        out_specs=(ANY, VM) + (ANY,) * 4,
+        out_specs=(ANY, VM) + (ANY,) * 5 + (VM,) * 2,
         scratch_shapes=[
             pltpu.VMEM((total, width), bf), pltpu.VMEM((1, count), f32), pltpu.VMEM((1, total), f32), pltpu.VMEM((3, width, 256), bf),
             pltpu.VMEM((256, width), bf), pltpu.VMEM((3 * HW, width), bf),
         ]
         + [pltpu.VMEM(s, bf) for s in shapes]
-        + [dma_sems(6), dma_sems(6), dma_sems(3), dma_sems(3), dma_sems(3), dma_sems(20)],
+        + [
+            pltpu.VMEM((SPAN, NH, 80, count), f32), pltpu.VMEM((SPAN * NH, 1, count), f32),
+            pltpu.VMEM((NH, count // 2, count), f32), pltpu.VMEM((NH, count // 2, count), f32),
+            pltpu.VMEM((HW, total), bf),
+            dma_sems(6), dma_sems(6), dma_sems(3), dma_sems(3), dma_sems(3), dma_sems(20),
+            dma_sems(3), dma_sems(3), dma_sems(1),
+        ],
         compiler_params=comm_params(0),
         name="gather",
     )(tok, ids, pads, cos, sin, w_qkv)
@@ -307,74 +414,6 @@
     for d in range(3):
         dead = dead | ((first <= d) & (d <= last) & (l[d] == 0))
     return jnp.where(dead, 0, lo), jnp.where(dead, total, hi)
-
-def fwd_kernel(KB, QB, code_ref, qa_ref, ka_ref, va_ref, out_ref, lse_ref, o32_ref, acc_ref, even_ref, odd_ref):
-    T = code_ref.shape[1]
-    blocks = T // KB
-    lims = doc_limits(code_ref[...])
-
-    def keys(j):
-        return pl.ds(pl.multiple_of(j * KB, KB), KB)
-
-    def qblock(i, _):
-        a = i * QB
-        qs = pl.ds(pl.multiple_of(a, QB), QB)
-        lo, hi = block_range(lims, a, QB, T)
-        jlo = lo // KB
-        pairs = ((hi + KB - 1) // KB - jlo + 1) // 2
-        jlo = jnp.minimum(jlo, blocks - 2 * pairs)
-
-        def scores(j, h, ref):
-            ref[h] = nn(ka_ref[h, keys(j), :], qa_ref[h, :, qs])
-
-        def absorb(j, h, ref, m):
-            s = ref[h]
-            mn = jnp.maximum(m, jnp.max(s, 0, keepdims=True))
-            p = jnp.exp(s - mn).astype(bf)
-            acc_ref[h] = acc_ref[h] * jnp.exp(m - mn) + nn(va_ref[h, :80, keys(j)], p)
-            return mn
-
-        for h in range(NH):
-            acc_ref[h] = jnp.zeros_like(acc_ref[h])
-            scores(jlo, h, even_ref)
-
-        def kv(n, ms):
-            j = jlo + 2 * n
-            ms = list(ms)
-            for h in range(NH):
-                scores(j + 1, h, odd_ref)
-                ms[h] = absorb(j, h, even_ref, ms[h])
-            after = jnp.minimum(j + 2, blocks - 1)
-            for h in range(NH):
-                scores(after, h, even_ref)
-                ms[h] = absorb(j + 1, h, odd_ref, ms[h])
-            return tuple(ms)
-
-        ms = lax.fori_loop(0, pairs, kv, tuple(jnp.full((1, QB), -3e38, f32) for _ in range(NH)))
-        for h in range(NH):
-            tot = acc_ref[h, 64:65, :]
-            o = acc_ref[h, :64, :] / tot
-            o32_ref[h * HEAD_DIM : (h + 1) * HEAD_DIM, qs] = o
-            lse_ref[h : h + 1, qs] = jnp.where(ms[h] < -1e29, 0.0, ms[h] + jnp.log(tot))
-            out_ref[h * HEAD_DIM : (h + 1) * HEAD_DIM, qs] = o.astype(bf)
-        return 0
-
-    lax.fori_loop(0, T // QB, qblock, 0)
-
-
-def attn_fwd(code, qa, ka, va, KB=256, QB=512):
-    T = code.shape[1]
-    sds = jax.ShapeDtypeStruct
-    return pl.pallas_call(
-        functools.partial(fwd_kernel, KB, QB),
-        out_shape=(sds((HW, T), bf), sds((NH, T), f32), sds((HW, T), f32)),
-        in_specs=[VM] * 4,
-        out_specs=(VM,) * 3,
-        scratch_shapes=[pltpu.VMEM((NH, 80, QB), f32)] + [pltpu.VMEM((NH, KB, QB), f32)] * 2,
-        compiler_params=pltpu.CompilerParams(vmem_limit_bytes=VLIM),
-        name="attn_fwd",
-    )(code, qa, ka, va)
-
 
 def bwd_kernel(KB, QB, do_ref, o32_ref, lse_ref, qa_ref, ka_ref, va_ref, kt_ref, cos_ref, sin_ref, code_ref, g_ref,
                vn_ref, dn_ref, da_ref, qb_ref, acc_ref, dq_ref):
@@ -510,7 +549,7 @@
     groups, heads_ref, rows_ref, codes_ref, goals_ref, gain1_ref, bias1_ref, gain2_ref, bias2_ref, wo_h, wg_h, wu_h, wd_h,
     att_o, inner_o, hid_o, gm_o, gg_o, gb_o, ga_o, gh1_o, gains_o, scores_o, loss_o,
     att, wo, wg, wu, wd, inner, x1, s1, acc, hid, ab, x2, s2, sec, gm, gm2, gb, gb2, plane, allp, ge,
-    wsem, send, recv, lsem, tsend, trecv, osem, csend, crecv,
+    wsem, lsem, tsend, trecv, osem, csend, crecv,
 ):
     t, p, x, y, g = here()
     peers = plane_peers()
@@ -527,31 +566,19 @@
         return pltpu.make_async_copy(src, dst, wsem.at[1 + 3 * j + k])
 
     first_load = pltpu.make_async_copy(wo_h, wo, wsem.at[0])
+    heads_load = pltpu.make_async_copy(heads_ref, att, lsem.at[0])
+    heads_load.start()
     first_load.start()
     for j in range(tiles):
         for k in range(3):
             weight(j, k).start()
     greet(peers + (sibling,) + line)
-    moves = []
-    for i, peer in enumerate((peers[2], peers[0], peers[1])):
-        m = lax.rem(peer[1], SPAN)
-        moves.append(remote(
-            heads_ref.at[:, pl.ds(pl.multiple_of(m * count, count), count)],
-            att.at[pl.ds(pl.multiple_of(me * HW, HW), HW)], send.at[i], recv.at[i], peer,
-        ))
-    moves.append(pltpu.make_async_copy(
-        heads_ref.at[:, pl.ds(pl.multiple_of(me * count, count), count)],
-        att.at[pl.ds(pl.multiple_of(me * HW, HW), HW)], lsem.at[0],
-    ))
-    for c in moves:
-        c.start()
     code = codes_ref[:, pl.ds(pl.multiple_of(me * count, count), count)]
     zero = jnp.zeros((8 - DOCS_GRP, count), f32)
     mem = jnp.concatenate([jnp.where(code == float(d), 1.0, 0.0) for d in range(DOCS_GRP)] + [zero], 0)
     mem = jnp.concatenate([mem, mem, mem, jnp.zeros((8, count), f32)], 0).astype(bf)
     first_load.wait()
-    for c in moves:
-        c.wait()
+    heads_load.wait()
 
     def pair(i, mine, its, out):
         return (
@@ -701,7 +728,7 @@
             sds((width, count), bf), sds((count, width), f32), sds((8, width), f32),
             sds((size, size), f32), sds((8, 128), f32),
         ),
-        in_specs=[VM, VM, VM, pl.BlockSpec(memory_space=pltpu.SMEM)] + [VM] * 4 + [ANY] * 4,
+        in_specs=[ANY, VM, VM, pl.BlockSpec(memory_space=pltpu.SMEM)] + [VM] * 4 + [ANY] * 4,
         out_specs=(ANY,) * 6 + (VM,) * 5,
         scratch_shapes=[
             vm(width, count), vm(width, width), vm(tiles, width, width), vm(tiles, width, width),
@@ -709,7 +736,7 @@
             vm(tiles, count, width), vm(2, tiles, count, width), vf(count, width), vf(count, 1),
             vm(3, count, width), vm(count, width), vm(2, count, half), vm(count, width), vm(2, count, half),
             vf(4, 8, width), vf(2, groups, 8, width), vf(size, width),
-            dma_sems(1 + 3 * tiles), dma_sems(3), dma_sems(3), dma_sems(1),
+            dma_sems(1 + 3 * tiles), dma_sems(1),
             dma_sems(4 + 2 * tiles), dma_sems(4 + 2 * tiles), dma_sems(4 + 2 * tiles),
             dma_sems(3 + groups), dma_sems(3 + groups),
         ],
@@ -1317,12 +1344,11 @@
     me = place % SPAN
     docs = groups * DOCS_GRP
     cos, sin = angle_tables(SPAN * count)
-    tok_all, codes, qa, ka, va, kt = gather(rows, doc_ids, pad_mask, cos, sin, w_qkv)
-    heads_out, lse, exact = attn_fwd(codes, qa, ka, va)
+    tok_all, codes, qa, ka, va, kt, heads, lse, exact = gather(rows, doc_ids, pad_mask, cos, sin, w_qkv)
     norms = (ln1_gain, ln1_bias, ln2_gain, ln2_bias)
     (
         attended, inner, hidden, grad_mlp, grads, grad_branch, grad_attended, grad_h1, gains, scores_all, loss
-    ) = block(heads_out, rows, codes, targets, norms, w_out, w_gate, w_up, w_down, groups)
+    ) = block(heads, rows, codes, targets, norms, w_out, w_gate, w_up, w_down, groups)
     by_hand = groups == 4 and width % (16 * places) == 0
     if by_hand:
         send_a, keep_a, send_b, keep_b, send_c, keep_c, d_heads, gain_sums = weight_grads(

time: 231 us -> 226 us (0.978)
  the two profiles are of different devices: /device:TPU:25 before, /device:TPU:0 now
where the time goes in v6:
time: 226 us; the launch traced here: 223 us
  Pallas kernels  211 us (93%)
  waiting for transfers between devices  7.24 us (3%)
  starting transfers between devices  3.24 us (1%)
    pallas_call x1, Pallas kernels, finish(): pl.pallas_call(functools.partial(finish_kernel, groups), out_shape=(jax.S...  61.8 us
    pallas_call x1, Pallas kernels, gather(): pl.pallas_call(gather_kernel, out_shape=(jax.ShapeDtypeStruct((total, wid...  50.1 us
    pallas_call x1, Pallas kernels, block(): pl.pallas_call(functools.partial(block_kernel, groups), out_shape=(sds((2...  48.7 us
    pallas_call x1, Pallas kernels, attn_bwd(): pl.pallas_call(functools.partial(bwd_kernel, KB, QB), out_shape=jax.Shape...  25.6 us
    pallas_call x1, Pallas kernels, weight_grads(): pl.pallas_call(functools.partial(weights_kernel, groups), out_shape=(part...  20.6 us
    ppermute x3, waiting for transfers between devices, local(): lax.ppermute(v, 'dp', [(i, i ^ bit) for i in range(places)])  7.24 us
  transfers between devices with their start and end apart: 3, of which 2 were waited for; matrix products, arithmetic and copies ran while one was open for 0% of the time, Pallas kernels for 11%

profile of v6, /device:TPU:0, one launch (start us, length us, event | category | flops | bytes accessed | tf_op | source)
XLA Modules:
  0.0 223.0 jit_solution(10793889127866051806)
XLA Ops:
  0.6 50.1 %gather.1 = (bf16[2048,768]{1,0:T(8,128)(2,1)}, f32[1,2048]{1,0:T(1,128)}, bf16[3,128,2048]{2,1,0:T(8,128)(2,1)}, bf16[3,2048,128]{2,1,0:T(8,128)(2,1)}, bf16[3,...) custom-call(bf16[512,768]{1,0:T(8,128)(2,1)} %bitcast.6, ...), custom_call_target="tpu_custom_call" | custom-call | tf_op jit(solution)/shard_map/gather/pallas_call | solution.py:286
  50.8 48.7 %block.1 = (bf16[2,768,512]{2,1,0:T(8,128)(2,1)}, bf16[2,512,768]{2,1,0:T(8,128)(2,1)}, bf16[2,4,512,768]{3,2,1,0:T(8,128)(2,1)}, bf16[2,512,384]{2,1,0:T(8,128)...) custom-call(bf16[768,512]{1,0:T(8,128)(2,1)} %get-tuple-element.55.h, ...), custom_call_target="tpu_custom_call" | custom-call | tf_op jit(solution)/shard_map/block/pallas_call | solution.py:723
  99.4 20.6 %weight_grads.1 = (bf16[4,2,240,384]{3,2,1,0:T(8,128)(2,1)}, bf16[4,2,240,384]{3,2,1,0:T(8,128)(2,1)}, bf16[4,2,240,384]{3,2,1,0:T(8,128)(2,1)}, bf16[4,2,240,38...) custom-call(bf16[2,512,768]{2,1,0:T(8,128)(2,1)} %get-tuple-element., ...), custom_call_target="tpu_custom_call" | custom-call | flops 5133828096 | bytes 31457280 | tf_op jit(solution)/shard_map/weight_grads/pallas_call | solution.py:882
  120.1 0.9 collective-permute-start.2
  121.0 0.9 collective-permute-start
  121.9 1.4 collective-permute-start.1
  123.3 25.6 %attn_bwd.1.gin_ref = bf16[576,2048]{1,0:T(8,128)(2,1)} custom-call(bf16[192,2048]{1,0:T(8,128)(2,1)} %get-tuple-element.72.do_ref, f32[192,2048]{1,0:T(8,128)} %get-tuple-element.73.o32_ref, f32[3,2048]{1,0:T(4,128)} %get-tuple-element.74.lse_ref, bf16[3,128,2048]{2,1,0:T(8,128)(2,1)} %get-tuple-element.75.qa_ref, ...), custom_call_target="tpu_custom_call" | custom-call | flops 16106127360 | bytes 12582912 | tf_op jit(solution)/shard_map/attn_bwd/pallas_call | solution.py:482
  148.9 0.0 collective-permute-done.2.rc_ref
  148.9 6.5 %collective-permute-done.ra_ref = bf16[4,2,240,384]{3,2,1,0:T(8,128)(2,1)S(1)} collective-permute-done((bf16[4,2,240,384]{3,2,1,0:T(8,128)(2,1)}, bf16[4,2,240,384]{3,2,1,0:T(8,128)(2,1)S(1)}, u32[]{:S(2)}, u32[]{:S(2)}) %collective-permute-start) | collective-permute-done | bytes 1474592 | tf_op jit(solution)/shard_map/ppermute | solution.py:1357
  155.4 0.0 copy-start
  155.4 0.7 collective-permute-done.1.rb_ref
  156.1 0.4 copy-done
  156.5 61.8 %finish.1 = (bf16[2,624,384]{2,1,0:T(8,128)(2,1)}, f32[512,768]{1,0:T(8,128)}, bf16[4,48,576]{2,1,0:T(8,128)(2,1)}) custom-call(bf16[4,2,240,384]{3,2,1,0:T(8,128)(2,1)} %get-tuple-element.65.ka_ref, bf16[4,2,240,384]{3,2,1,0:T(8,128)(2,1)} %get-tuple-element.66.kb_ref, bf16[2,4,144,384]{3,2,1,0:T(8,128)(2,1)} %get-tuple-element.67.kc_ref, ...), custom_call_target="tpu_custom_call" | custom-call | tf_op jit(solution)/shard_map/finish/pallas_call | solution.py:1233
  218.3 4.2 %unfold.1 = (f32[48,3072]{1,0:T(8,128)}, f32[48,3072]{1,0:T(8,128)}, f32[192,768]{1,0:T(8,128)}, f32[48,768]{1,0:T(8,128)}, f32[48,2304]{1,0:T(8,128)}, /*index=...) custom-call(bf16[2,624,384]{2,1,0:T(8,128)(2,1)} %get-tuple-element., ...), custom_call_target="tpu_custom_call" | custom-call | tf_op jit(solution)/shard_map/unfold/pallas_call | solution.py:1307
Async XLA Ops:
  120.1 28.8 %collective-permute-start.2 = (bf16[2,4,144,384]{3,2,1,0:T(8,128)(2,1)}, bf16[2,4,144,384]{3,2,1,0:T(8,128)(2,1)}, u32[]{:S(2)}, u32[]{:S(2)}) collective-permute-start(bf16[2,4,144,384]{3,2,1,0:T(8,128)(2,1)} %get-tuple-element.70), channel_id=1, source_target_pairs={{0,4},{1,5},{2,6},{3,7},{4,0},{5,1},{6,2},{7,3},{8,12},{9,13},{10,... | collective-permute-start | bytes 2654216 | tf_op jit(solution)/shard_map/ppermute | solution.py:1357
  121.0 34.4 %collective-permute-start = (bf16[4,2,240,384]{3,2,1,0:T(8,128)(2,1)}, bf16[4,2,240,384]{3,2,1,0:T(8,128)(2,1)S(1)}, u32[]{:S(2)}, u32[]{:S(2)}) collective-permute-start(bf16[4,2,240,384]{3,2,1,0:T(8,128)(2,1)} %get-tuple-element.68), channel_id=1, source_target_pairs={{0,1},{1,0},{2,3},{3,2},{4,5},{5,4},{6,7},{7,6},{8,9},{9,8},{10,11... | collective-permute-start | bytes 4423688 | tf_op jit(solution)/shard_map/ppermute | solution.py:1357
  121.9 34.2 %collective-permute-start.1 = (bf16[4,2,240,384]{3,2,1,0:T(8,128)(2,1)}, bf16[4,2,240,384]{3,2,1,0:T(8,128)(2,1)}, u32[]{:S(2)}, u32[]{:S(2)}) collective-permute-start(bf16[4,2,240,384]{3,2,1,0:T(8,128)(2,1)} %get-tuple-element.69), channel_id=1, source_target_pairs={{0,2},{1,3},{2,0},{3,1},{4,6},{5,7},{6,4},{7,5},{8,10},{9,11},{10,... | collective-permute-start | bytes 4423688 | tf_op jit(solution)/shard_map/ppermute | solution.py:1357
  155.4 1.1 copy-start

commit v7 on v6

--- a/solution.py
+++ b/solution.py
@@ -60,11 +60,18 @@
     return (t, px), (t, py), (t, pd)
 
 
+def hail(peers):
+    for peer in peers:
+        pl.semaphore_signal(pltpu.get_barrier_semaphore(), inc=1, device_id=peer, device_id_type=MESH)
+
+
+def greeted(peers):
+    pl.semaphore_wait(pltpu.get_barrier_semaphore(), len(peers))
+
+
 def greet(peers):
-    barrier = pltpu.get_barrier_semaphore()
-    for peer in peers:
-        pl.semaphore_signal(barrier, inc=1, device_id=peer, device_id_type=MESH)
-    pl.semaphore_wait(barrier, len(peers))
+    hail(peers)
+    greeted(peers)
 
 
 def remote(src, dst, send, recv, peer):
@@ -81,10 +88,19 @@
     return pltpu.CompilerParams(collective_id=cid, has_side_effects=True, vmem_limit_bytes=VLIM)
 
 
+def fill_angles(base_ref, cos_ref, sin_ref):
+    for i in range(cos_ref.shape[1] // 128):
+        at = slice(i * 128, (i + 1) * 128)
+        ca, sa = base_ref[0, :, i : i + 1], base_ref[1, :, i : i + 1]
+        cb, sb = base_ref[2], base_ref[3]
+        cos_ref[:, at] = ca * cb - sa * sb
+        sin_ref[:, at] = sa * cb + ca * sb
+
+
 def gather_kernel(
-    tok_ref, ids_ref, pads_ref, cos_ref, sin_ref, w_ref, out_ref, codes_ref, qa_ref, ka_ref, va_ref, kt_ref,
+    tok_ref, ids_ref, pads_ref, base_ref, w_ref, out_ref, codes_ref, qa_ref, ka_ref, va_ref, kt_ref,
     att_ref, lse_ref, exact_ref,
-    toks, code_ref, codes, wraw, wturn, wt, qa, ka, va, kt, acc, tops, sooner, later, heads,
+    cos_ref, sin_ref, toks, code_ref, codes, wraw, wturn, wt, qa, ka, va, kt, acc, tops, sooner, later, heads,
     send, recv, csend, crecv, wsem, osem, asend, arecv, asem,
 ):
     t, p, x, y, g = here()
@@ -120,6 +136,7 @@
         c.start()
         small.append(c)
     codes[:, whole(me)] = code_ref[...]
+    fill_angles(base_ref, cos_ref, sin_ref)
     for k in range(3):
         loads[k].wait()
         wturn[...] = wraw[k].T
@@ -279,7 +296,7 @@
         back(k).wait()
 
 
-def gather(tok, ids, pads, cos, sin, w_qkv):
+def gather(tok, ids, pads, base, w_qkv):
     count, width = tok.shape
     total = SPAN * count
     shapes = ((NH, 128, total), (NH, total, 128), (NH, 128, total), (NH, HEAD_DIM, total))
@@ -291,9 +308,10 @@
             jax.ShapeDtypeStruct((SPAN * HW, count), bf), jax.ShapeDtypeStruct((NH, total), f32),
             jax.ShapeDtypeStruct((HW, total), f32),
         ),
-        in_specs=[VM] * 5 + [ANY],
+        in_specs=[VM] * 4 + [ANY],
         out_specs=(ANY, VM) + (ANY,) * 5 + (VM,) * 2,
         scratch_shapes=[
+            pltpu.VMEM((HEAD_DIM // 2, total), f32), pltpu.VMEM((HEAD_DIM // 2, total), f32),
             pltpu.VMEM((total, width), bf), pltpu.VMEM((1, count), f32), pltpu.VMEM((1, total), f32), pltpu.VMEM((3, width, 256), bf),
             pltpu.VMEM((256, width), bf), pltpu.VMEM((3 * HW, width), bf),
         ]
@@ -307,7 +325,7 @@
         ],
         compiler_params=comm_params(0),
         name="gather",
-    )(tok, ids, pads, cos, sin, w_qkv)
+    )(tok, ids, pads, base, w_qkv)
 
 
 def heads_to_tokens_kernel(parts, in_ref, out_ref, send, recv, lsem):
@@ -415,12 +433,13 @@
         dead = dead | ((first <= d) & (d <= last) & (l[d] == 0))
     return jnp.where(dead, 0, lo), jnp.where(dead, total, hi)
 
-def bwd_kernel(KB, QB, do_ref, o32_ref, lse_ref, qa_ref, ka_ref, va_ref, kt_ref, cos_ref, sin_ref, code_ref, g_ref,
-               vn_ref, dn_ref, da_ref, qb_ref, acc_ref, dq_ref):
+def bwd_kernel(KB, QB, do_ref, o32_ref, lse_ref, qa_ref, ka_ref, va_ref, kt_ref, base_ref, code_ref, g_ref,
+               cos_ref, sin_ref, vn_ref, dn_ref, da_ref, qb_ref, acc_ref, dq_ref):
     T = do_ref.shape[1]
     hw = HW
     CH = 512
     lims = doc_limits(code_ref[...])
+    fill_angles(base_ref, cos_ref, sin_ref)
     def prep(c, _):
         sl = pl.ds(pl.multiple_of(c*CH, CH), CH)
         for h in range(NH):
@@ -446,10 +465,13 @@
         a = i*QB
         qs = pl.ds(pl.multiple_of(a, QB), QB)
         lo, hi = block_range(lims, a, QB, T)
-        jlo = lo//KB; jhi = (hi+KB-1)//KB
+        small = KB // 2
+        start = lo // small
+        many = (hi + small - 1) // small - start
         dq_ref[...] = jnp.zeros_like(dq_ref)
-        def kv(j, _):
-            ks = pl.ds(pl.multiple_of(j*KB, KB), KB)
+
+        def visit(at, size):
+            ks = pl.ds(pl.multiple_of(at * small, small), size)
             for h in range(NH):
                 s = nn(ka_ref[h, ks, :], qa_ref[h, :, qs])
                 dp = nn(vn_ref[h, ks, :], da_ref[h, :, qs])
@@ -457,8 +479,12 @@
                 ds = (p*dp).astype(bf)
                 acc_ref[h, ks, :] += nn(p.astype(bf), dn_ref[h, qs, :]) + nn(ds, qb_ref[h, qs, :])
                 dq_ref[h] += nn(kt_ref[h, :, ks], ds)
+
+        def kv(j, _):
+            visit(start + 2 * j, KB)
             return 0
-        lax.fori_loop(jlo, jhi, kv, 0)
+        lax.fori_loop(0, many // 2, kv, 0)
+        pl.when(many % 2 == 1)(lambda: visit(start + many - 1, small))
         cos = cos_ref[:, qs]; sin = sin_ref[:, qs]
         for h in range(NH):
             u = dq_ref[h]*0.125
@@ -477,15 +503,15 @@
         return 0
     lax.fori_loop(0, T//CH, fin, 0)
 
-def attn_bwd(do, o32, lse, qa, ka, va, kt, cos, sin, code, KB=512, QB=256):
+def attn_bwd(do, o32, lse, qa, ka, va, kt, base, code, KB=512, QB=256):
     T = do.shape[1]
     return pl.pallas_call(functools.partial(bwd_kernel, KB, QB),
         out_shape=jax.ShapeDtypeStruct((3*NH*HEAD_DIM, T), bf),
-        in_specs=[pl.BlockSpec(memory_space=pltpu.VMEM)]*10, out_specs=pl.BlockSpec(memory_space=pltpu.VMEM),
-        scratch_shapes=[pltpu.VMEM((NH,T,128), bf), pltpu.VMEM((NH,T,128), bf), pltpu.VMEM((NH,128,T), bf), pltpu.VMEM((NH,T,128), bf),
+        in_specs=[VM] * 9, out_specs=pl.BlockSpec(memory_space=pltpu.VMEM),
+        scratch_shapes=[pltpu.VMEM((HEAD_DIM // 2, T), f32), pltpu.VMEM((HEAD_DIM // 2, T), f32), pltpu.VMEM((NH,T,128), bf), pltpu.VMEM((NH,T,128), bf), pltpu.VMEM((NH,128,T), bf), pltpu.VMEM((NH,T,128), bf),
                         pltpu.VMEM((NH,T,128), f32), pltpu.VMEM((NH,HEAD_DIM,QB), f32)],
         compiler_params=pltpu.CompilerParams(vmem_limit_bytes=VLIM), name="attn_bwd",
-        cost_estimate=pl.CostEstimate(flops=int(10*T*T*128*3), bytes_accessed=12<<20, transcendentals=T*T*3))(do, o32, lse, qa, ka, va, kt, cos, sin, code)
+        cost_estimate=pl.CostEstimate(flops=int(10*T*T*128*3), bytes_accessed=12<<20, transcendentals=T*T*3))(do, o32, lse, qa, ka, va, kt, base, code)
 
 
 def contrast_part(groups, sums, goals_ref, plane, allp, ge, send, recv, scores_ref, loss_ref):
@@ -561,18 +587,19 @@
     me = lax.rem(p, SPAN)
 
     def weight(j, k):
-        cols = pl.ds(j * width, width)
+        cols = pl.ds(j * width if isinstance(j, int) else pl.multiple_of(j * width, width), width)
         src, dst = ((wg_h.at[:, cols], wg.at[j]), (wu_h.at[:, cols], wu.at[j]), (wd_h.at[cols], wd.at[j]))[k]
         return pltpu.make_async_copy(src, dst, wsem.at[1 + 3 * j + k])
 
     first_load = pltpu.make_async_copy(wo_h, wo, wsem.at[0])
+    everyone = peers + (sibling,) + line
+    hail(everyone)
     heads_load = pltpu.make_async_copy(heads_ref, att, lsem.at[0])
     heads_load.start()
     first_load.start()
     for j in range(tiles):
         for k in range(3):
             weight(j, k).start()
-    greet(peers + (sibling,) + line)
     code = codes_ref[:, pl.ds(pl.multiple_of(me * count, count), count)]
     zero = jnp.zeros((8 - DOCS_GRP, count), f32)
     mem = jnp.concatenate([jnp.where(code == float(d), 1.0, 0.0) for d in range(DOCS_GRP)] + [zero], 0)
@@ -590,8 +617,9 @@
         for c in pair(i, mine, its, out):
             c.start()
 
+    acc[...] = tn(att[...], wo[...])
+    greeted(everyone)
     both(0, att, att, att_o)
-    acc[...] = tn(att[...], wo[...])
     step = 64
     gain1, bias1, gain2, bias2 = (r[...].reshape(1, width) for r in (gain1_ref, bias1_ref, gain2_ref, bias2_ref))
 
@@ -623,19 +651,24 @@
             remote(its, out.at[1, j], tsend.at[i + j], trecv.at[i + j], sibling),
         )
 
-    for j in range(tiles):
-        for k in range(3):
-            weight(j, k).wait()
-        gate = nn(inner[...], wg[j])
-        upper = nn(inner[...], wu[j])
-        sig = jax.nn.sigmoid(gate)
-        silu = gate * sig
-        hid[j] = (silu * upper).astype(bf)
-        ab[0, j] = (upper * (sig * (1.0 + gate * (1.0 - sig)))).astype(bf)
-        ab[1, j] = silu.astype(bf)
-        for c in tile_of(j, 2, hid.at[j], hid.at[j], hid_o):
-            c.start()
-        acc[...] += nn(hid[j], wd[j])
+    def forward(n, _):
+        for i in range(2):
+            j = 2 * n + i
+            for k in range(3):
+                weight(j, k).wait()
+            gate = nn(inner[...], wg[j])
+            upper = nn(inner[...], wu[j])
+            sig = jax.nn.sigmoid(gate)
+            silu = gate * sig
+            hid[j] = (silu * upper).astype(bf)
+            ab[0, j] = (upper * (sig * (1.0 + gate * (1.0 - sig)))).astype(bf)
+            ab[1, j] = silu.astype(bf)
+            for c in tile_of(j, 2, hid.at[j], hid.at[j], hid_o):
+                c.start()
+            acc[...] += nn(hid[j], wd[j])
+        return 0
+
+    lax.fori_loop(0, tiles // 2, forward, 0)
 
     def norm_two(i, _):
         sl = chunk(i)
@@ -675,15 +708,20 @@
 
     g2, b2 = lax.fori_loop(0, count // step, back_two, (zeros, zeros))
     both(2 + 2 * tiles, gm2.at[t], gm2.at[1 - t], gm_o)
-    for j in range(tiles):
-        gh = nt(gm[...], wd[j])
-        gg = (gh * ab[0, j].astype(f32)).astype(bf)
-        gu = (gh * ab[1, j].astype(f32)).astype(bf)
-        ab[0, j] = gg
-        ab[1, j] = gu
-        for c in tile_of(j, 2 + tiles, ab.at[t, j], ab.at[1 - t, j], gg_o):
-            c.start()
-        acc[...] += nt(gg, wg[j]) + nt(gu, wu[j])
+    def backward(n, _):
+        for i in range(2):
+            j = 2 * n + i
+            gh = nt(gm[...], wd[j])
+            gg = (gh * ab[0, j].astype(f32)).astype(bf)
+            gu = (gh * ab[1, j].astype(f32)).astype(bf)
+            ab[0, j] = gg
+            ab[1, j] = gu
+            for c in tile_of(j, 2 + tiles, ab.at[t, j], ab.at[1 - t, j], gg_o):
+                c.start()
+            acc[...] += nt(gg, wg[j]) + nt(gu, wu[j])
+        return 0
+
+    lax.fori_loop(0, tiles // 2, backward, 0)
 
     def back_one(i, sums):
         sl = chunk(i)
@@ -746,19 +784,56 @@
 
 
 def weights_kernel(
-    groups, i_ref, g_ref, h_ref, m_ref, a_ref, b_ref, in_ref, gain_ref,
-    sa_ref, ka_ref, sb_ref, kb_ref, sc_ref, kc_ref, heads_ref, sum_ref,
-    iv, it, gv, hv, mv, av, bv, gs, ds, os, plane, line, isem, osem, send, recv, lsem, nsend, nrecv,
+    groups, i_ref, g_ref, h_ref, m_ref, a_ref, b_ref, in_ref,
+    sa_ref, ka_ref, sb_ref, kb_ref, sc_ref, kc_ref, heads_ref,
+    iv, it, gv, hv, mv, av, bv, gs, ds, os, isem, osem, send, recv, lsem,
 ):
     t, p, x, y, g = here()
     level = lax.rem(g, 2)
     peers = plane_peers()
-    sibling = (1 - t, p)
-    others = tuple((t, lax.rem(p + SPAN * k, SPAN * groups)) for k in range(1, groups))
-    greet(peers + (sibling,) + others)
-    around = [remote(gain_ref, plane.at[i], nsend.at[i], nrecv.at[i], q) for i, q in enumerate(peers)]
-    for c in around:
+    count, width = i_ref.shape[1:]
+    half = width // 2
+    tiles = gv.shape[0]
+    shards = SPAN * groups
+    one = width // shards
+    down = ds.shape[1]
+
+    def load(i, src, dst):
+        return pltpu.make_async_copy(src, dst, isem.at[i])
+
+    class Both:
+        def __init__(self, *copies):
+            self.copies = copies
+
+        def start(self):
+            for c in self.copies:
+                c.start()
+
+        def wait(self):
+            for c in self.copies:
+                c.wait()
+
+    def tile(ref, j, buf, base):
+        return Both(*(
+            load(base + 2 * j + i, ref.at[i, j], buf.at[j, pl.ds(i * count, count)]) for i in range(2)
+        ))
+
+    def stack(base, ref, buf):
+        return Both(*(load(base + i, ref.at[i], buf.at[pl.ds(i * count, count)]) for i in range(2)))
+
+    def beside(base, ref, buf):
+        return Both(*(load(base + i, ref.at[i], buf.at[:, pl.ds(i * count, count)]) for i in range(2)))
+
+    hail(peers)
+    few = [stack(0, m_ref, mv), beside(2, a_ref, av), stack(4, b_ref, bv), stack(6, i_ref, iv)]
+    few[0].start()
+    for j in range(tiles):
+        tile(h_ref, j, hv, 8).start()
+    for c in few[1:]:
         c.start()
+    for j in range(tiles):
+        tile(g_ref, j, gv, 8 + 2 * tiles).start()
+    greeted(peers)
     tokens = in_ref.shape[1]
     me = lax.rem(p, SPAN)
     mine = pl.ds(pl.multiple_of(me * tokens, tokens), tokens)
@@ -774,48 +849,20 @@
     ))
     for c in moves:
         c.start()
-    count, width = i_ref.shape[1:]
-    half = width // 2
-    tiles = gv.shape[1]
-    shards = SPAN * groups
-    one = width // shards
-    down = ds.shape[1]
-
-    def load(i, src, dst):
-        return pltpu.make_async_copy(src, dst, isem.at[i])
-
-    def tile(ref, j, buf, base):
-        return load(base + j, ref.at[:, j], buf.at[:, j])
-
-    few = [load(i, a, b) for i, (a, b) in enumerate(((m_ref, mv), (a_ref, av), (b_ref, bv), (i_ref, iv)))]
-    few[0].start()
-    for j in range(tiles):
-        tile(h_ref, j, hv, 4).start()
-    for c in few[1:]:
-        c.start()
-    for j in range(tiles):
-        tile(g_ref, j, gv, 4 + tiles).start()
     few[0].wait()
 
     def downward(j, _):
-        tile(h_ref, j, hv, 4).wait()
-        r = tn(hv[0, j], mv[0]) + tn(hv[1, j], mv[1])
+        tile(h_ref, j, hv, 8).wait()
+        r = tn(hv[j], mv[...])
         ds[pl.ds(j * (width // down), width // down)] = r.astype(bf).reshape(width // down, down, half)
         return 0
 
     lax.fori_loop(0, tiles, downward, 0)
-    for c in few[1:] + around:
+    for c in few[1:]:
         c.wait()
-    line[0] = (gain_ref[...] + plane[0]) + (plane[1] + plane[2])
-    ring = [
-        remote(line.at[0], line.at[1 + k], nsend.at[3 + k], nrecv.at[3 + k], q) for k, q in enumerate(others)
-    ]
-    for c in ring:
-        c.start()
-    r = nn(av[0], bv[0]) + nn(av[1], bv[1])
+    r = nn(av[...], bv[...])
     os[...] = r.astype(bf).reshape(shards, one, half)
-    for i in range(2):
-        it[:, i * count : (i + 1) * count] = iv[i].T
+    it[...] = iv[...].T
     fours = lambda ref, n: ref.reshape(groups, 2, 2, n, half)
 
     def put(i, src, dst):
@@ -845,29 +892,19 @@
         )
 
     for j in range(tiles):
-        tile(g_ref, j, gv, 4 + tiles).wait()
-        r = (nn(it[:, :count], gv[0, j]) + nn(it[:, count:], gv[1, j])).astype(bf)
+        tile(g_ref, j, gv, 8 + 2 * tiles).wait()
+        r = nn(it[...], gv[j]).astype(bf)
         for h in range(2):
             k = 2 * j + h
             gs[k] = r[:, h * half : (h + 1) * half].reshape(shards, one, half)
             outs.extend(top(k))
             for c in outs[-2:]:
                 c.start()
-    for c in ring:
-        c.wait()
-    total = line[0]
-    for k in range(1, groups):
-        total = total + line[k]
-    line[groups] = total
-    last = remote(line.at[groups], line.at[groups + 1], nsend.at[2 + groups], nrecv.at[2 + groups], sibling)
-    last.start()
-    last.wait()
-    sum_ref[...] = line[groups] + line[groups + 1]
     for c in outs + moves:
         c.wait()
 
 
-def weight_grads(groups, grad_heads, gains, inner, grads, hidden, grad_mlp, attended, grad_branch):
+def weight_grads(groups, grad_heads, inner, grads, hidden, grad_mlp, attended, grad_branch):
     count, width = inner.shape[1:]
     half = width // 2
     shards = SPAN * groups
@@ -883,24 +920,22 @@
         functools.partial(weights_kernel, groups),
         out_shape=(
             part(ra), part(ra), part(rb), part(rb), level, level,
-            jax.ShapeDtypeStruct((HW, SPAN * grad_heads.shape[1]), bf), jax.ShapeDtypeStruct(gains.shape, f32),
+            jax.ShapeDtypeStruct((HW, SPAN * grad_heads.shape[1]), bf),
         ),
-        in_specs=[ANY] * 6 + [VM] * 2,
-        out_specs=(ANY,) * 7 + (VM,),
+        in_specs=[ANY] * 6 + [VM],
+        out_specs=(ANY,) * 7,
         scratch_shapes=[
-            vm(2, count, width), vm(width, 2 * count), vm(2, tiles, count, width), vm(2, tiles, count, width),
-            vm(2, count, half), vm(2, width, count), vm(2, count, half),
+            vm(2 * count, width), vm(width, 2 * count), vm(tiles, 2 * count, width), vm(tiles, 2 * count, width),
+            vm(2 * count, half), vm(width, 2 * count), vm(2 * count, half),
             vm(2 * tiles, shards, one, half), vm(shards, down, half), vm(shards, one, half),
-            pltpu.VMEM((3,) + gains.shape, f32), pltpu.VMEM((groups + 2,) + gains.shape, f32),
-            dma_sems(4 + 2 * tiles), dma_sems(8 + 4 * tiles), dma_sems(3), dma_sems(3), dma_sems(1),
-            dma_sems(3 + groups), dma_sems(3 + groups),
+            dma_sems(8 + 4 * tiles), dma_sems(8 + 4 * tiles), dma_sems(3), dma_sems(3), dma_sems(1),
         ],
         compiler_params=comm_params(2),
         name="weight_grads",
         cost_estimate=pl.CostEstimate(
             flops=int(2 * 2 * count * half * width * 8.5), bytes_accessed=30 << 20, transcendentals=0
         ),
-    )(inner, grads, hidden, grad_mlp, attended, grad_branch, grad_heads, gains)
+    )(inner, grads, hidden, grad_mlp, attended, grad_branch, grad_heads)
 
 
 def add_rows(dst, a, b, rows):
@@ -979,8 +1014,9 @@
 
 
 def finish_kernel(
-    groups, ka_ref, kb_ref, kc_ref, ra_ref, rb_ref, rc_ref, wq_ref, gh_ref, gin_ref, tin_ref,
-    pair_ref, tg_ref, out_ref,
+    groups, ka_ref, kb_ref, kc_ref, ra_ref, rb_ref, rc_ref, wq_ref, gh_ref, gin_ref, tin_ref, gain_ref,
+    pair_ref, tg_ref, out_ref, sum_ref,
+    plane, line, nsend, nrecv,
     kvc, rvc, r2c, r3c, r4c, csem, cs, cr, kva, kvb, rva, rvb, r2a, r2b, ua, ub, da, db, isem, s2, q2, us, ur, ds, dr,
     gm_ref, wq, gh, g_ref, tok_ref, wsem, fs, fr,
     w2, sib, ub2, db2, fin, send, recv, ts, tr, us2, ur2, ds2, dr2, ps, pr, lsem,
@@ -1024,6 +1060,9 @@
     for c in more:
         c.start()
     greet(peers + across + (sibling,) + tuple(others))
+    around = [remote(gain_ref, plane.at[i], nsend.at[i], nrecv.at[i], q) for i, q in enumerate(peers)]
+    for c in around:
+        c.start()
 
     def second(c, zt):
         peer, kr, rr, kv, rv, r2, u, d, mine = colours[c]
@@ -1161,6 +1200,14 @@
     fifth.start()
     relay(order[0], 1)
     relay2(2)
+    for c in around:
+        c.wait()
+    line[0] = (gain_ref[...] + plane[0]) + (plane[1] + plane[2])
+    ring = [
+        remote(line.at[0], line.at[1 + k], nsend.at[3 + k], nrecv.at[3 + k], q) for k, q in enumerate(others)
+    ]
+    for c in ring:
+        c.start()
     in_plane(order[2])
     relay(order[1], 1)
     in_plane(order[3])
@@ -1186,6 +1233,18 @@
             away, stay, same = hand(k, tt)
             pl.when(jnp.logical_not(same))(lambda away=away: away().start())
             pl.when(same)(lambda stay=stay: stay().start())
+    for c in ring:
+        c.wait()
+    total = line[0]
+    for k in range(1, groups):
+        total = total + line[k]
+    line[groups] = total
+    gained = remote(line.at[groups], line.at[groups + 1], nsend.at[2 + groups], nrecv.at[2 + groups], sibling)
+    gained.start()
+    for c in copies + list(more):
+        c.wait()
+    turned = nn(wq[...], gm_ref[...]).T
+    tg_ref[...] = gh[...] + turned
     fifth.wait_recv()
     add_rows(pair_ref.at[t, pl.ds(size(0) + size(1), up)], r3c.at[top], r4c, up)
     for zt in order:
@@ -1193,10 +1252,6 @@
             chain(c, zt).finish(pair_ref.at[t, sl], size(c))
     last = remote(pair_ref.at[t], pair_ref.at[t], fs.at[0], fr.at[0], sibling)
     last.start()
-    for c in copies + list(more):
-        c.wait()
-    turned = nn(wq[...], gm_ref[...]).T
-    tg_ref[...] = gh[...] + turned
     for s in range(SPAN):
         from_here = jnp.logical_and(s == me, y == t)
         pl.when(jnp.logical_not(from_here))(
@@ -1219,10 +1274,12 @@
             third(i, k).wait_send()
         fourth(i).wait_send()
     fifth.wait_send()
+    gained.wait()
+    sum_ref[...] = line[groups] + line[groups + 1]
     last.wait()
 
 
-def finish(ka, kb, kc, ra, rb, rc, wq, gh, g, tok, groups):
+def finish(ka, kb, kc, ra, rb, rc, wq, gh, g, tok, gains, groups):
     width = tok.shape[1]
     count = tok.shape[0] // SPAN
     one = width // (SPAN * groups)
@@ -1236,10 +1293,13 @@
             jax.ShapeDtypeStruct((2, na + nb + nc, half), bf),
             jax.ShapeDtypeStruct((count, width), f32),
             jax.ShapeDtypeStruct((SPAN, one, 3 * HW), bf),
+            jax.ShapeDtypeStruct(gains.shape, f32),
         ),
-        in_specs=[ANY] * 10,
-        out_specs=(VM,) * 3,
+        in_specs=[ANY] * 10 + [VM],
+        out_specs=(VM,) * 4,
         scratch_shapes=[
+            pltpu.VMEM((3,) + gains.shape, f32), pltpu.VMEM((groups + 2,) + gains.shape, f32),
+            dma_sems(3 + groups), dma_sems(3 + groups),
             buf(2, SPAN, nc, half), buf(2, SPAN, nc, half), buf(2, 2, nc, half), buf(2, nc, half), buf(nc, half),
             dma_sems(4), dma_sems(7), dma_sems(7),
             buf(groups, 2, na, half), buf(groups, 2, nb, half), buf(groups, 2, na, half), buf(groups, 2, nb, half),
@@ -1257,7 +1317,7 @@
         ],
         compiler_params=comm_params(3),
         name="finish",
-    )(ka, kb, kc, ra, rb, rc, wq, gh, g, tok)
+    )(ka, kb, kc, ra, rb, rc, wq, gh, g, tok, gains)
 
 
 def unfold_kernel(
@@ -1318,11 +1378,13 @@
     )(pair, parts, grad, scores, gains, loss)
 
 
-def angle_tables(total):
+def angle_bases():
     half = HEAD_DIM // 2
     freqs = np.float32(1000.0) ** (-np.arange(half, dtype=np.float32) / np.float32(half))
-    theta = freqs[:, None].astype(np.float32) * np.arange(total, dtype=np.float32)[None, :]
-    return np.cos(theta).astype(np.float32), np.sin(theta).astype(np.float32)
+    steps = np.arange(128, dtype=np.float64)
+    far = freqs[:, None].astype(np.float64) * (128.0 * steps)[None, :]
+    near = freqs[:, None].astype(np.float64) * steps[None, :]
+    return np.stack([np.cos(far), np.sin(far), np.cos(near), np.sin(near)]).astype(np.float32)
 
 
 def spread_sum(value):
@@ -1343,25 +1405,25 @@
     place = lax.axis_index("dp")
     me = place % SPAN
     docs = groups * DOCS_GRP
-    cos, sin = angle_tables(SPAN * count)
-    tok_all, codes, qa, ka, va, kt, heads, lse, exact = gather(rows, doc_ids, pad_mask, cos, sin, w_qkv)
+    base = angle_bases()
+    tok_all, codes, qa, ka, va, kt, heads, lse, exact = gather(rows, doc_ids, pad_mask, base, w_qkv)
     norms = (ln1_gain, ln1_bias, ln2_gain, ln2_bias)
     (
         attended, inner, hidden, grad_mlp, grads, grad_branch, grad_attended, grad_h1, gains, scores_all, loss
     ) = block(heads, rows, codes, targets, norms, w_out, w_gate, w_up, w_down, groups)
     by_hand = groups == 4 and width % (16 * places) == 0
     if by_hand:
-        send_a, keep_a, send_b, keep_b, send_c, keep_c, d_heads, gain_sums = weight_grads(
-            groups, grad_attended, gains, inner, grads, hidden, grad_mlp, attended, grad_branch
+        send_a, keep_a, send_b, keep_b, send_c, keep_c, d_heads = weight_grads(
+            groups, grad_attended, inner, grads, hidden, grad_mlp, attended, grad_branch
         )
         exchange = lambda v, bit: lax.ppermute(v, "dp", [(i, i ^ bit) for i in range(places)])
         came_a, came_b, came_c = exchange(send_a, 1), exchange(send_b, 2), exchange(send_c, SPAN)
     else:
         d_heads = tokens_to_heads(grad_attended, 5, "to_heads")
-    mixed = attn_bwd(d_heads, exact, lse, qa, ka, va, kt, cos, sin, codes)
+    mixed = attn_bwd(d_heads, exact, lse, qa, ka, va, kt, base, codes)
     if by_hand:
-        pair, grad_tokens, qkv_parts = finish(
-            keep_a, keep_b, keep_c, came_a, came_b, came_c, w_qkv, grad_h1, mixed, tok_all, groups
+        pair, grad_tokens, qkv_parts, gain_sums = finish(
+            keep_a, keep_b, keep_c, came_a, came_b, came_c, w_qkv, grad_h1, mixed, tok_all, gains, groups
         )
         gate_out, up_out, down_out, out_out, qkv_out, token_grad, scores, loss, *gains_out = unfold(
             pair, qkv_parts, grad_tokens, scores_all, gain_sums, loss, w_gate.shape[1] // width, groups

time: 226 us -> 223 us (0.987)
  the two profiles are of different devices: /device:TPU:0 before, /device:TPU:25 now
where the time goes in v7:
time: 223 us; the launch traced here: 220 us
  Pallas kernels  208 us (93%)
  waiting for transfers between devices  7.75 us (3%)
  starting transfers between devices  3.1 us (1%)
    pallas_call x1, Pallas kernels, finish(): pl.pallas_call(functools.partial(finish_kernel, groups), out_shape=(jax.S...  66.1 us
    pallas_call x1, Pallas kernels, block(): pl.pallas_call(functools.partial(block_kernel, groups), out_shape=(sds((2...  49.8 us
    pallas_call x1, Pallas kernels, gather(): pl.pallas_call(gather_kernel, out_shape=(jax.ShapeDtypeStruct((total, wid...  47.1 us
    pallas_call x1, Pallas kernels, attn_bwd(): pl.pallas_call(functools.partial(bwd_kernel, KB, QB), out_shape=jax.Shape...  24.3 us
    pallas_call x1, Pallas kernels, weight_grads(): pl.pallas_call(functools.partial(weights_kernel, groups), out_shape=(part...  16.4 us
    ppermute x3, waiting for transfers between devices, local(): lax.ppermute(v, 'dp', [(i, i ^ bit) for i in range(places)])  7.75 us
  transfers between devices with their start and end apart: 3, of which 2 were waited for; matrix products, arithmetic and copies ran while one was open for 0% of the time, Pallas kernels for 11%

profile of v7, /device:TPU:25, one launch (start us, length us, event | category | flops | bytes accessed | tf_op | source)
XLA Modules:
  0.0 220.1 jit_solution(4233681418911496726)
XLA Ops:
  0.6 47.1 %gather.1 = (bf16[2048,768]{1,0:T(8,128)(2,1)}, f32[1,2048]{1,0:T(1,128)}, bf16[3,128,2048]{2,1,0:T(8,128)(2,1)}, bf16[3,2048,128]{2,1,0:T(8,128)(2,1)}, bf16[3,...) custom-call(bf16[512,768]{1,0:T(8,128)(2,1)} %bitcast.6, ...), custom_call_target="tpu_custom_call" | custom-call | tf_op jit(solution)/shard_map/gather/pallas_call | solution.py:303
  47.8 49.8 %block.1 = (bf16[2,768,512]{2,1,0:T(8,128)(2,1)}, bf16[2,512,768]{2,1,0:T(8,128)(2,1)}, bf16[2,4,512,768]{3,2,1,0:T(8,128)(2,1)}, bf16[2,512,384]{2,1,0:T(8,128)...) custom-call(bf16[768,512]{1,0:T(8,128)(2,1)} %get-tuple-element.55.h, ...), custom_call_target="tpu_custom_call" | custom-call | tf_op jit(solution)/shard_map/block/pallas_call | solution.py:761
  97.6 16.4 %weight_grads.1 = (bf16[4,2,240,384]{3,2,1,0:T(8,128)(2,1)}, bf16[4,2,240,384]{3,2,1,0:T(8,128)(2,1)}, bf16[4,2,240,384]{3,2,1,0:T(8,128)(2,1)}, bf16[4,2,240,38...) custom-call(bf16[2,512,768]{2,1,0:T(8,128)(2,1)} %get-tuple-element., ...), custom_call_target="tpu_custom_call" | custom-call | flops 5133828096 | bytes 31457280 | tf_op jit(solution)/shard_map/weight_grads/pallas_call | solution.py:919
  114.0 1.2 collective-permute-start.2
  115.2 0.9 collective-permute-start
  116.2 1.0 collective-permute-start.1
  117.1 24.3 %attn_bwd.1.gin_ref = bf16[576,2048]{1,0:T(8,128)(2,1)} custom-call(bf16[192,2048]{1,0:T(8,128)(2,1)} %get-tuple-element.71.do_ref, f32[192,2048]{1,0:T(8,128)} %get-tuple-element.72.o32_ref, f32[3,2048]{1,0:T(4,128)} %get-tuple-element.73.lse_ref, bf16[3,128,2048]{2,1,0:T(8,128)(2,1)} %get-tuple-element.74.qa_ref, ...), custom_call_target="tpu_custom_call" | custom-call | flops 16106127360 | bytes 12582912 | tf_op jit(solution)/shard_map/attn_bwd/pallas_call | solution.py:508
  141.4 0.0 collective-permute-done.2.rc_ref
  141.4 7.0 %collective-permute-done.ra_ref = bf16[4,2,240,384]{3,2,1,0:T(8,128)(2,1)S(1)} collective-permute-done((bf16[4,2,240,384]{3,2,1,0:T(8,128)(2,1)}, bf16[4,2,240,384]{3,2,1,0:T(8,128)(2,1)S(1)}, u32[]{:S(2)}, u32[]{:S(2)}) %collective-permute-start) | collective-permute-done | bytes 1474592 | tf_op jit(solution)/shard_map/ppermute | solution.py:1419
  148.5 0.0 copy-start
  148.5 0.7 collective-permute-done.1.rb_ref
  149.2 0.4 copy-done
  149.6 66.1 %finish.1 = (bf16[2,624,384]{2,1,0:T(8,128)(2,1)}, f32[512,768]{1,0:T(8,128)}, bf16[4,48,576]{2,1,0:T(8,128)(2,1)}, f32[8,768]{1,0:T(8,128)}) custom-call(bf16[4,2,240,384]{3,2,1,0:T(8,128)(2,1)} %get-tuple-element.64.ka_ref, bf16[4,2,240,384]{3,2,1,0:T(8,128)(2,1)} %get-tuple-element.65.kb_ref, bf16[2,4,144,384]{3,2,1,0:T(8,128)(2,1)} %get-tuple-element.66.kc_ref, ...), custom_call_target="tpu_custom_call" | custom-call | tf_op jit(solution)/shard_map/finish/pallas_call | solution.py:1290
  215.7 4.2 %unfold.1 = (f32[48,3072]{1,0:T(8,128)}, f32[48,3072]{1,0:T(8,128)}, f32[192,768]{1,0:T(8,128)}, f32[48,768]{1,0:T(8,128)}, f32[48,2304]{1,0:T(8,128)}, /*index=...) custom-call(bf16[2,624,384]{2,1,0:T(8,128)(2,1)} %get-tuple-element., ...), custom_call_target="tpu_custom_call" | custom-call | tf_op jit(solution)/shard_map/unfold/pallas_call | solution.py:1367
Async XLA Ops:
  114.0 27.4 %collective-permute-start.2 = (bf16[2,4,144,384]{3,2,1,0:T(8,128)(2,1)}, bf16[2,4,144,384]{3,2,1,0:T(8,128)(2,1)}, u32[]{:S(2)}, u32[]{:S(2)}) collective-permute-start(bf16[2,4,144,384]{3,2,1,0:T(8,128)(2,1)} %get-tuple-element.69), channel_id=1, source_target_pairs={{0,4},{1,5},{2,6},{3,7},{4,0},{5,1},{6,2},{7,3},{8,12},{9,13},{10,... | collective-permute-start | bytes 2654216 | tf_op jit(solution)/shard_map/ppermute | solution.py:1419
  115.2 33.2 %collective-permute-start = (bf16[4,2,240,384]{3,2,1,0:T(8,128)(2,1)}, bf16[4,2,240,384]{3,2,1,0:T(8,128)(2,1)S(1)}, u32[]{:S(2)}, u32[]{:S(2)}) collective-permute-start(bf16[4,2,240,384]{3,2,1,0:T(8,128)(2,1)} %get-tuple-element.67), channel_id=1, source_target_pairs={{0,1},{1,0},{2,3},{3,2},{4,5},{5,4},{6,7},{7,6},{8,9},{9,8},{10,11... | collective-permute-start | bytes 4423688 | tf_op jit(solution)/shard_map/ppermute | solution.py:1419
  116.2 33.0 %collective-permute-start.1 = (bf16[4,2,240,384]{3,2,1,0:T(8,128)(2,1)}, bf16[4,2,240,384]{3,2,1,0:T(8,128)(2,1)}, u32[]{:S(2)}, u32[]{:S(2)}) collective-permute-start(bf16[4,2,240,384]{3,2,1,0:T(8,128)(2,1)} %get-tuple-element.68), channel_id=1, source_target_pairs={{0,2},{1,3},{2,0},{3,1},{4,6},{5,7},{6,4},{7,5},{8,10},{9,11},{10,... | collective-permute-start | bytes 4423688 | tf_op jit(solution)/shard_map/ppermute | solution.py:1419
  148.5 1.1 copy-start

commit v8 on v7

--- a/solution.py
+++ b/solution.py
@@ -14,7 +14,7 @@
 DOCS_GRP = 3
 NH = HEADS // SPAN
 HW = NH * HEAD_DIM
-UPWARD = 3
+UPWARD = 4
 VLIM = 62 * 2**20
 MESH = pl.DeviceIdType.MESH
 f32 = jnp.float32
@@ -709,8 +709,7 @@
     g2, b2 = lax.fori_loop(0, count // step, back_two, (zeros, zeros))
     both(2 + 2 * tiles, gm2.at[t], gm2.at[1 - t], gm_o)
     def backward(n, _):
-        for i in range(2):
-            j = 2 * n + i
+        for j in range(tiles):
             gh = nt(gm[...], wd[j])
             gg = (gh * ab[0, j].astype(f32)).astype(bf)
             gu = (gh * ab[1, j].astype(f32)).astype(bf)
@@ -721,7 +720,7 @@
             acc[...] += nt(gg, wg[j]) + nt(gu, wu[j])
         return 0
 
-    lax.fori_loop(0, tiles // 2, backward, 0)
+    backward(0, 0)
 
     def back_one(i, sums):
         sl = chunk(i)
@@ -863,6 +862,7 @@
     r = nn(av[...], bv[...])
     os[...] = r.astype(bf).reshape(shards, one, half)
     it[...] = iv[...].T
+    third = one // 3
     fours = lambda ref, n: ref.reshape(groups, 2, 2, n, half)
 
     def put(i, src, dst):
@@ -871,7 +871,14 @@
     outs = []
     for i, (ref, k) in enumerate(((sb_ref, 1 - y), (kb_ref, y))):
         outs.append(put(4 * i, fours(ds, down).at[:, k], ref.at[:, :, pl.ds(0, down)]))
-        outs.append(put(4 * i + 1, fours(os, one).at[:, k], ref.at[:, :, pl.ds(down, one)]))
+        outs.append(put(4 * i + 1, fours(os, one).at[:, k, :, pl.ds(third, third)], ref.at[:, :, pl.ds(down, third)]))
+    for i, (ref, k) in enumerate(((sa_ref, 1 - x), (ka_ref, x))):
+        to = ref.at[:, :, pl.ds(ref.shape[2] - third, third)]
+        outs.append(put(2 + i, fours(os, one).at[:, :, k, pl.ds(0, third)], to))
+    levels = os.reshape(groups // 2, 2, SPAN, one, half)
+    for i, (ref, k) in enumerate(((sc_ref, 1 - level), (kc_ref, level))):
+        to = ref.at[:, :, pl.ds(ref.shape[2] - third, third)]
+        outs.append(put(6 + i, levels.at[:, k, :, pl.ds(2 * third, third)], to))
     for c in outs:
         c.start()
 
@@ -911,10 +918,11 @@
     one = width // shards
     tiles = grads.shape[1]
     down = tiles * one
-    ra = (2 * tiles - UPWARD) * one
-    rb = down + one
+    third = one // 3
+    ra = (2 * tiles - UPWARD) * one + third
+    rb = down + third
     part = lambda r: jax.ShapeDtypeStruct((groups, 2, r, half), bf)
-    level = jax.ShapeDtypeStruct((groups // 2, SPAN, UPWARD * one, half), bf)
+    level = jax.ShapeDtypeStruct((groups // 2, SPAN, UPWARD * one + third, half), bf)
     vm = lambda *n: pltpu.VMEM(n, bf)
     return pl.pallas_call(
         functools.partial(weights_kernel, groups),
@@ -1330,15 +1338,17 @@
     steps = gate_ref.shape[1] // half
     down = down_ref.shape[0]
     token_ref[0] = grad_ref[...]
-    top = (steps - UPWARD) * one
+    third = one // 3
+    ends = ((steps - UPWARD) * one, (steps - UPWARD) * one + third + down, pair_ref.shape[1] - third)
     for j in range(steps):
-        at = j * one + (0 if j < steps - UPWARD else down + one)
+        at = j * one + (0 if j < steps - UPWARD else down + 2 * third)
         for k, ref in enumerate((gate_ref, up_ref)):
             ref[:, j * half : (j + 1) * half] = pair_ref[k, at : at + one, :].astype(f32)
     for k in range(2):
         cols = slice(k * half, (k + 1) * half)
-        down_ref[:, cols] = pair_ref[k, top : top + down, :].astype(f32)
-        out_ref[:, cols] = pair_ref[k, top + down : top + down + one, :].astype(f32)
+        down_ref[:, cols] = pair_ref[k, ends[1] - down : ends[1], :].astype(f32)
+        for i, at in enumerate(ends):
+            out_ref[i * third : (i + 1) * third, cols] = pair_ref[k, at : at + third, :].astype(f32)
     for k in range(3):
         row = [part_ref[s, :, k * HW : (k + 1) * HW].astype(f32) for s in range(SPAN)]
         qkv_ref[:, k * width : (k + 1) * width] = jnp.concatenate(row, 1)
@@ -1411,7 +1421,7 @@
     (
         attended, inner, hidden, grad_mlp, grads, grad_branch, grad_attended, grad_h1, gains, scores_all, loss
     ) = block(heads, rows, codes, targets, norms, w_out, w_gate, w_up, w_down, groups)
-    by_hand = groups == 4 and width % (16 * places) == 0
+    by_hand = groups == 4 and width % (48 * places) == 0
     if by_hand:
         send_a, keep_a, send_b, keep_b, send_c, keep_c, d_heads = weight_grads(
             groups, grad_attended, inner, grads, hidden, grad_mlp, attended, grad_branch

time: 223 us -> 219 us (0.982)
  waiting for transfers between devices: 7.75 us -> 2.14 us
    ppermute x3, waiting for transfers between devices: 7.75 us -> 2.14 us  [local(): lax.ppermute(v, 'dp', [(i, i ^ bit) for i in range(places)])]
  transfers between devices with their start and end apart: 3 -> 3, of which waited for: 2 -> 3; matrix products, arithmetic and copies ran while one was open for 0% -> 0% of each run, Pallas kernels for 11% -> 12%
where the time goes in v8:
time: 219 us; the launch traced here: 217 us
  Pallas kernels  210 us (96%)
  starting transfers between devices  3.1 us (1%)
    pallas_call x1, Pallas kernels, finish(): pl.pallas_call(functools.partial(finish_kernel, groups), out_shape=(jax.S...  68.2 us
    pallas_call x1, Pallas kernels, block(): pl.pallas_call(functools.partial(block_kernel, groups), out_shape=(sds((2...  48.5 us
    pallas_call x1, Pallas kernels, gather(): pl.pallas_call(gather_kernel, out_shape=(jax.ShapeDtypeStruct((total, wid...  47.1 us
    pallas_call x1, Pallas kernels, attn_bwd(): pl.pallas_call(functools.partial(bwd_kernel, KB, QB), out_shape=jax.Shape...  25.7 us
    pallas_call x1, Pallas kernels, weight_grads(): pl.pallas_call(functools.partial(weights_kernel, groups), out_shape=(part...  16.7 us
  transfers between devices with their start and end apart: 3, of which 3 were waited for; matrix products, arithmetic and copies ran while one was open for 0% of the time, Pallas kernels for 12%

profile of v8, /device:TPU:25, one launch (start us, length us, event | category | flops | bytes accessed | tf_op | source)
XLA Modules:
  0.0 216.5 jit_solution(414874566902109779)
XLA Ops:
  0.6 47.1 %gather.1 = (bf16[2048,768]{1,0:T(8,128)(2,1)}, f32[1,2048]{1,0:T(1,128)}, bf16[3,128,2048]{2,1,0:T(8,128)(2,1)}, bf16[3,2048,128]{2,1,0:T(8,128)(2,1)}, bf16[3,...) custom-call(bf16[512,768]{1,0:T(8,128)(2,1)} %bitcast.6, ...), custom_call_target="tpu_custom_call" | custom-call | tf_op jit(solution)/shard_map/gather/pallas_call | solution.py:303
  47.8 48.5 %block.1 = (bf16[2,768,512]{2,1,0:T(8,128)(2,1)}, bf16[2,512,768]{2,1,0:T(8,128)(2,1)}, bf16[2,4,512,768]{3,2,1,0:T(8,128)(2,1)}, bf16[2,512,384]{2,1,0:T(8,128)...) custom-call(bf16[768,512]{1,0:T(8,128)(2,1)} %get-tuple-element.55.h, ...), custom_call_target="tpu_custom_call" | custom-call | tf_op jit(solution)/shard_map/block/pallas_call | solution.py:760
  96.3 16.7 %weight_grads.1 = (bf16[4,2,208,384]{3,2,1,0:T(8,128)(2,1)}, bf16[4,2,208,384]{3,2,1,0:T(8,128)(2,1)}, bf16[4,2,208,384]{3,2,1,0:T(8,128)(2,1)}, bf16[4,2,208,38...) custom-call(bf16[2,512,768]{2,1,0:T(8,128)(2,1)} %get-tuple-element., ...), custom_call_target="tpu_custom_call" | custom-call | flops 5133828096 | bytes 31457280 | tf_op jit(solution)/shard_map/weight_grads/pallas_call | solution.py:927
  113.0 1.0 collective-permute-start
  114.0 1.0 collective-permute-start.1
  115.0 1.1 collective-permute-start.2
  116.1 25.7 %attn_bwd.1.gin_ref = bf16[576,2048]{1,0:T(8,128)(2,1)} custom-call(bf16[192,2048]{1,0:T(8,128)(2,1)} %get-tuple-element.71.do_ref, f32[192,2048]{1,0:T(8,128)} %get-tuple-element.72.o32_ref, f32[3,2048]{1,0:T(4,128)} %get-tuple-element.73.lse_ref, bf16[3,128,2048]{2,1,0:T(8,128)(2,1)} %get-tuple-element.74.qa_ref, ...), custom_call_target="tpu_custom_call" | custom-call | flops 16106127360 | bytes 12582912 | tf_op jit(solution)/shard_map/attn_bwd/pallas_call | solution.py:508
  141.8 0.6 collective-permute-done.ra_ref
  142.4 0.0 copy-start
  142.4 0.7 collective-permute-done.1.rb_ref
  143.1 0.8 collective-permute-done.2.rc_ref
  143.9 0.0 copy-done
  143.9 68.2 %finish.1 = (bf16[2,624,384]{2,1,0:T(8,128)(2,1)}, f32[512,768]{1,0:T(8,128)}, bf16[4,48,576]{2,1,0:T(8,128)(2,1)}, f32[8,768]{1,0:T(8,128)}) custom-call(bf16[4,2,208,384]{3,2,1,0:T(8,128)(2,1)} %get-tuple-element.64.ka_ref, bf16[4,2,208,384]{3,2,1,0:T(8,128)(2,1)} %get-tuple-element.65.kb_ref, bf16[2,4,208,384]{3,2,1,0:T(8,128)(2,1)} %get-tuple-element.66.kc_ref, ...), custom_call_target="tpu_custom_call" | custom-call | tf_op jit(solution)/shard_map/finish/pallas_call | solution.py:1298
  212.1 4.2 %unfold.1 = (f32[48,3072]{1,0:T(8,128)}, f32[48,3072]{1,0:T(8,128)}, f32[192,768]{1,0:T(8,128)}, f32[48,768]{1,0:T(8,128)}, f32[48,2304]{1,0:T(8,128)}, /*index=...) custom-call(bf16[2,624,384]{2,1,0:T(8,128)(2,1)} %get-tuple-element., ...), custom_call_target="tpu_custom_call" | custom-call | tf_op jit(solution)/shard_map/unfold/pallas_call | solution.py:1377
Async XLA Ops:
  113.0 29.4 %collective-permute-start = (bf16[4,2,208,384]{3,2,1,0:T(8,128)(2,1)}, bf16[4,2,208,384]{3,2,1,0:T(8,128)(2,1)S(1)}, u32[]{:S(2)}, u32[]{:S(2)}) collective-permute-start(bf16[4,2,208,384]{3,2,1,0:T(8,128)(2,1)} %get-tuple-element.67), channel_id=1, source_target_pairs={{0,1},{1,0},{2,3},{3,2},{4,5},{5,4},{6,7},{7,6},{8,9},{9,8},{10,11... | collective-permute-start | bytes 3833864 | tf_op jit(solution)/shard_map/ppermute | solution.py:1429
  114.0 29.1 %collective-permute-start.1 = (bf16[4,2,208,384]{3,2,1,0:T(8,128)(2,1)}, bf16[4,2,208,384]{3,2,1,0:T(8,128)(2,1)}, u32[]{:S(2)}, u32[]{:S(2)}) collective-permute-start(bf16[4,2,208,384]{3,2,1,0:T(8,128)(2,1)} %get-tuple-element.68), channel_id=1, source_target_pairs={{0,2},{1,3},{2,0},{3,1},{4,6},{5,7},{6,4},{7,5},{8,10},{9,11},{10,... | collective-permute-start | bytes 3833864 | tf_op jit(solution)/shard_map/ppermute | solution.py:1429
  115.0 29.0 %collective-permute-start.2 = (bf16[2,4,208,384]{3,2,1,0:T(8,128)(2,1)}, bf16[2,4,208,384]{3,2,1,0:T(8,128)(2,1)}, u32[]{:S(2)}, u32[]{:S(2)}) collective-permute-start(bf16[2,4,208,384]{3,2,1,0:T(8,128)(2,1)} %get-tuple-element.69), channel_id=1, source_target_pairs={{0,4},{1,5},{2,6},{3,7},{4,0},{5,1},{6,2},{7,3},{8,12},{9,13},{10,... | collective-permute-start | bytes 3833864 | tf_op jit(solution)/shard_map/ppermute | solution.py:1429
  142.4 1.6 copy-start

commit v9 on v8

--- a/solution.py
+++ b/solution.py
@@ -510,7 +510,7 @@
         in_specs=[VM] * 9, out_specs=pl.BlockSpec(memory_space=pltpu.VMEM),
         scratch_shapes=[pltpu.VMEM((HEAD_DIM // 2, T), f32), pltpu.VMEM((HEAD_DIM // 2, T), f32), pltpu.VMEM((NH,T,128), bf), pltpu.VMEM((NH,T,128), bf), pltpu.VMEM((NH,128,T), bf), pltpu.VMEM((NH,T,128), bf),
                         pltpu.VMEM((NH,T,128), f32), pltpu.VMEM((NH,HEAD_DIM,QB), f32)],
-        compiler_params=pltpu.CompilerParams(vmem_limit_bytes=VLIM), name="attn_bwd",
+        compiler_params=pltpu.CompilerParams(vmem_limit_bytes=67043328), name="attn_bwd",
         cost_estimate=pl.CostEstimate(flops=int(10*T*T*128*3), bytes_accessed=12<<20, transcendentals=T*T*3))(do, o32, lse, qa, ka, va, kt, base, code)
 
 
@@ -1252,7 +1252,9 @@
     for c in copies + list(more):
         c.wait()
     turned = nn(wq[...], gm_ref[...]).T
-    tg_ref[...] = gh[...] + turned
+    gh[...] = gh[...] + turned
+    result = pltpu.make_async_copy(gh, tg_ref, wsem.at[4])
+    result.start()
     fifth.wait_recv()
     add_rows(pair_ref.at[t, pl.ds(size(0) + size(1), up)], r3c.at[top], r4c, up)
     for zt in order:
@@ -1284,6 +1286,7 @@
     fifth.wait_send()
     gained.wait()
     sum_ref[...] = line[groups] + line[groups + 1]
+    result.wait()
     last.wait()
 
 
@@ -1304,7 +1307,7 @@
             jax.ShapeDtypeStruct(gains.shape, f32),
         ),
         in_specs=[ANY] * 10 + [VM],
-        out_specs=(VM,) * 4,
+        out_specs=(VM, ANY, VM, VM),
         scratch_shapes=[
             pltpu.VMEM((3,) + gains.shape, f32), pltpu.VMEM((groups + 2,) + gains.shape, f32),
             dma_sems(3 + groups), dma_sems(3 + groups),
@@ -1316,7 +1319,7 @@
             dma_sems(4 * groups), dma_sems(2 * groups), dma_sems(2 * groups),
             dma_sems(2 * groups), dma_sems(2 * groups), dma_sems(2 * groups), dma_sems(2 * groups),
             buf(3 * width, count), buf(width, 3 * width), pltpu.VMEM((count, width), f32),
-            buf(*g.shape), buf(*tok.shape), dma_sems(4),
+            buf(*g.shape), buf(*tok.shape), dma_sems(5),
             dma_sems(1), dma_sems(1),
             mix(SPAN * groups), mix(groups, 2), mix(groups, 2), mix(groups, 2), mix(2),
             dma_sems(9), dma_sems(9), dma_sems(groups), dma_sems(groups),

time: 219 us -> 218 us (level)
  Pallas kernels: 210 us -> 206 us
    pallas_call x1, Pallas kernels: 68.2 us -> 65.8 us  [finish(): pl.pallas_call(functools.partial(finish_kernel, groups), out_shape=(jax.S...]
  transfers between devices with their start and end apart: 3 -> 3, of which waited for: 3 -> 3; matrix products, arithmetic and copies ran while one was open for 0% -> 0% of each run, Pallas kernels for 12% -> 11%
where the time goes in v9:
time: 218 us; the launch traced here: 214 us
  Pallas kernels  206 us (94%)
  waiting for transfers between devices  3.82 us (2%)
  starting transfers between devices  3.09 us (1%)
    pallas_call x1, Pallas kernels, finish(): pl.pallas_call(functools.partial(finish_kernel, groups), out_shape=(jax.S...  65.8 us
    pallas_call x1, Pallas kernels, block(): pl.pallas_call(functools.partial(block_kernel, groups), out_shape=(sds((2...  48.5 us
    pallas_call x1, Pallas kernels, gather(): pl.pallas_call(gather_kernel, out_shape=(jax.ShapeDtypeStruct((total, wid...  47.1 us
    pallas_call x1, Pallas kernels, attn_bwd(): pl.pallas_call(functools.partial(bwd_kernel, KB, QB), out_shape=jax.Shape...  24 us
    pallas_call x1, Pallas kernels, weight_grads(): pl.pallas_call(functools.partial(weights_kernel, groups), out_shape=(part...  16.7 us
  transfers between devices with their start and end apart: 3, of which 3 were waited for; matrix products, arithmetic and copies ran while one was open for 0% of the time, Pallas kernels for 11%

profile of v9, /device:TPU:25, one launch (start us, length us, event | category | flops | bytes accessed | tf_op | source)
XLA Modules:
  0.0 214.2 jit_solution(13611931829560953253)
XLA Ops:
  0.6 47.1 %gather.1 = (bf16[2048,768]{1,0:T(8,128)(2,1)}, f32[1,2048]{1,0:T(1,128)}, bf16[3,128,2048]{2,1,0:T(8,128)(2,1)}, bf16[3,2048,128]{2,1,0:T(8,128)(2,1)}, bf16[3,...) custom-call(bf16[512,768]{1,0:T(8,128)(2,1)} %bitcast.6, ...), custom_call_target="tpu_custom_call" | custom-call | tf_op jit(solution)/shard_map/gather/pallas_call | solution.py:303
  47.8 48.5 %block.1 = (bf16[2,768,512]{2,1,0:T(8,128)(2,1)}, bf16[2,512,768]{2,1,0:T(8,128)(2,1)}, bf16[2,4,512,768]{3,2,1,0:T(8,128)(2,1)}, bf16[2,512,384]{2,1,0:T(8,128)...) custom-call(bf16[768,512]{1,0:T(8,128)(2,1)} %get-tuple-element.55.h, ...), custom_call_target="tpu_custom_call" | custom-call | tf_op jit(solution)/shard_map/block/pallas_call | solution.py:760
  96.3 16.7 %weight_grads.1 = (bf16[4,2,208,384]{3,2,1,0:T(8,128)(2,1)}, bf16[4,2,208,384]{3,2,1,0:T(8,128)(2,1)}, bf16[4,2,208,384]{3,2,1,0:T(8,128)(2,1)}, bf16[4,2,208,38...) custom-call(bf16[2,512,768]{2,1,0:T(8,128)(2,1)} %get-tuple-element., ...), custom_call_target="tpu_custom_call" | custom-call | flops 5133828096 | bytes 31457280 | tf_op jit(solution)/shard_map/weight_grads/pallas_call | solution.py:927
  113.0 1.0 collective-permute-start
  114.0 1.0 collective-permute-start.1
  115.0 1.1 collective-permute-start.2
  116.1 24.0 %attn_bwd.1.gin_ref = bf16[576,2048]{1,0:T(8,128)(2,1)} custom-call(bf16[192,2048]{1,0:T(8,128)(2,1)} %get-tuple-element.71.do_ref, f32[192,2048]{1,0:T(8,128)} %get-tuple-element.72.o32_ref, f32[3,2048]{1,0:T(4,128)} %get-tuple-element.73.lse_ref, bf16[3,128,2048]{2,1,0:T(8,128)(2,1)} %get-tuple-element.74.qa_ref, ...), custom_call_target="tpu_custom_call" | custom-call | flops 16106127360 | bytes 12582912 | tf_op jit(solution)/shard_map/attn_bwd/pallas_call | solution.py:508
  140.1 2.3 %collective-permute-done.ra_ref = bf16[4,2,208,384]{3,2,1,0:T(8,128)(2,1)} collective-permute-done((bf16[4,2,208,384]{3,2,1,0:T(8,128)(2,1)}, bf16[4,2,208,384]{3,2,1,0:T(8,128)(2,1)}, u32[]{:S(2)}, u32[]{:S(2)}) %collective-permute-start) | collective-permute-done | bytes 1277984 | tf_op jit(solution)/shard_map/ppermute | solution.py:1432
  142.4 0.7 collective-permute-done.1.rb_ref
  143.1 0.8 collective-permute-done.2.rc_ref
  143.9 65.8 %finish.1 = (bf16[2,624,384]{2,1,0:T(8,128)(2,1)}, f32[512,768]{1,0:T(8,128)}, bf16[4,48,576]{2,1,0:T(8,128)(2,1)}, f32[8,768]{1,0:T(8,128)}) custom-call(bf16[4,2,208,384]{3,2,1,0:T(8,128)(2,1)} %get-tuple-element.64.ka_ref, bf16[4,2,208,384]{3,2,1,0:T(8,128)(2,1)} %get-tuple-element.65.kb_ref, bf16[2,4,208,384]{3,2,1,0:T(8,128)(2,1)} %get-tuple-element.66.kc_ref, ...), custom_call_target="tpu_custom_call" | custom-call | tf_op jit(solution)/shard_map/finish/pallas_call | solution.py:1301
  209.7 4.2 %unfold.1 = (f32[48,3072]{1,0:T(8,128)}, f32[48,3072]{1,0:T(8,128)}, f32[192,768]{1,0:T(8,128)}, f32[48,768]{1,0:T(8,128)}, f32[48,2304]{1,0:T(8,128)}, /*index=...) custom-call(bf16[2,624,384]{2,1,0:T(8,128)(2,1)} %get-tuple-element., ...), custom_call_target="tpu_custom_call" | custom-call | tf_op jit(solution)/shard_map/unfold/pallas_call | solution.py:1380
Async XLA Ops:
  113.0 29.4 %collective-permute-start = (bf16[4,2,208,384]{3,2,1,0:T(8,128)(2,1)}, bf16[4,2,208,384]{3,2,1,0:T(8,128)(2,1)}, u32[]{:S(2)}, u32[]{:S(2)}) collective-permute-start(bf16[4,2,208,384]{3,2,1,0:T(8,128)(2,1)} %get-tuple-element.67), channel_id=1, source_target_pairs={{0,1},{1,0},{2,3},{3,2},{4,5},{5,4},{6,7},{7,6},{8,9},{9,8},{10,11... | collective-permute-start | bytes 3833864 | tf_op jit(solution)/shard_map/ppermute | solution.py:1432
  114.0 29.1 %collective-permute-start.1 = (bf16[4,2,208,384]{3,2,1,0:T(8,128)(2,1)}, bf16[4,2,208,384]{3,2,1,0:T(8,128)(2,1)}, u32[]{:S(2)}, u32[]{:S(2)}) collective-permute-start(bf16[4,2,208,384]{3,2,1,0:T(8,128)(2,1)} %get-tuple-element.68), channel_id=1, source_target_pairs={{0,2},{1,3},{2,0},{3,1},{4,6},{5,7},{6,4},{7,5},{8,10},{9,11},{10,... | collective-permute-start | bytes 3833864 | tf_op jit(solution)/shard_map/ppermute | solution.py:1432
  115.0 29.0 %collective-permute-start.2 = (bf16[2,4,208,384]{3,2,1,0:T(8,128)(2,1)}, bf16[2,4,208,384]{3,2,1,0:T(8,128)(2,1)}, u32[]{:S(2)}, u32[]{:S(2)}) collective-permute-start(bf16[2,4,208,384]{3,2,1,0:T(8,128)(2,1)} %get-tuple-element.69), channel_id=1, source_target_pairs={{0,4},{1,5},{2,6},{3,7},{4,0},{5,1},{6,2},{7,3},{8,12},{9,13},{10,... | collective-permute-start | bytes 3833864 | tf_op jit(solution)/shard_map/ppermute | solution.py:1432
